TPU v7x, 32 devices: a whole 2x2x4 slice. The times are simulated.
32 devices in a mesh: tm: 4 (over x, core), space: 8 (over z, y).
Axes of the slice: x: 2, y: 2, z: 4, core: 2. Of those that a mesh axis runs over, the one named last changes fastest.
Arguments:
- volume: float32 [4, 128, 8, 2048], P('tm', 'space'), may hold values from -6 to 6
- warp_coef: float32 [4, 4, 4, 128, 2048], P('tm', None, None, 'space'), may hold values from 0.05 to 0.4
- offsets: int32 [4, 8, 4], P('tm', 'space'), may hold values from -6 to 6
- thresholds: float32 [4], replicated, may hold values from 0.1 to 0.5
Outputs:
- regularized: float32 [4, 128, 8, 2048], P('tm', 'space')
All inputs are finite; a program needn't handle non-finite values.
Results may differ from a plain program's by a relative error of at most 0.00002.
Values sent between devices are 32-bit elements; how exact they have to be, the bound alone decides.
No kernel may reach another device: no remote copies, remote signals or barrier semaphores. Data moves between devices by JAX's collectives and lax.ppermute only.
A program may use at most 64 MiB of HBM per device.

v0:
```python
import functools

import jax
import jax.numpy as jnp
from jax import lax
from jax.experimental import pallas as pl
from jax.experimental.pallas import tpu as pltpu
from jax.sharding import PartitionSpec as P

BAND = 4
SECTIONS = 4
SWEEPS = 4
REACH = 6

depth_rate = 0.4
plane_rate = 0.05
root_half = 0.7071067811865476

LANES = 128
SPARE = 64
EDGE = SWEEPS
GROUP = 6
VMEM = pltpu.VMEM
SMEM = pltpu.SMEM


def cells(value):
    return [value[:, i : i + LANES] for i in range(0, value.shape[1], LANES)]


def joined(parts):
    return jnp.concatenate(parts, axis=1)


def lane_ids():
    return lax.broadcasted_iota(jnp.int32, (8, LANES), 1)


def quotient(change):
    return change / (1.0 + change * change)


def moved_right(parts, amount, first):
    turned = [pltpu.roll(part, amount, 1) for part in parts]
    own = lane_ids() >= amount
    ahead = [first] + turned[:-1]
    return [jnp.where(own, a, b) for a, b in zip(turned, ahead)]


def moved_left(parts, amount):
    turned = [pltpu.roll(part, (LANES - amount) % LANES, 1) for part in parts]
    own = lane_ids() < LANES - amount
    return [jnp.where(own, a, b) for a, b in zip(turned, turned[1:])]


def warped_plane(field, coeff_rows, offset):
    zero = jnp.zeros((8, LANES), jnp.float32)
    behind = moved_right(cells(field) + [zero], REACH + BAND // 2, zero)
    total = None
    for band_index in range(BAND):
        shifted = joined(moved_left(behind, offset + REACH + band_index))
        term = jnp.broadcast_to(coeff_rows[band_index], shifted.shape) * shifted
        total = term if total is None else total + term
    return total


def haar(own, warped, sign, level, scale):
    value = (own + sign * warped) * scale
    return value - jnp.clip(value, -level, level)


class Sweep:
    def __init__(self, width, edge_first, edge_last, last_lane):
        rows = lax.broadcasted_iota(jnp.int32, (8, width), 0)
        self.inner_rows = rows < 7
        lanes = lane_ids()
        self.first = jnp.where(lanes == SPARE - 1, edge_first, 1.0)
        self.last = jnp.where(lanes == last_lane % LANES, edge_last, 1.0)
        self.last_part = last_lane // LANES

    def depth(self, low, high):
        return quotient(high - low)

    def plane(self, value, flux_below, flux_above):
        width = value.shape[1]
        change = jnp.where(self.inner_rows, pltpu.roll(value, 7, 0) - value, 0.0)
        flux_y = quotient(change)
        change = cells(pltpu.roll(value, width - 1, 1) - value)
        change[0] = change[0] * self.first
        change[self.last_part] = change[self.last_part] * self.last
        flux_x = quotient(joined(change))
        gain = (flux_y - pltpu.roll(flux_y, 1, 0)) + (flux_x - pltpu.roll(flux_x, 1, 1))
        return value + (plane_rate * gain + depth_rate * (flux_above - flux_below))


class Place:
    def __init__(self):
        self.tm = lax.axis_index("tm")
        self.space = lax.axis_index("space")
        self.pairs = lax.axis_size("space") // 2
        self.far = (self.tm // 2) % 2
        self.slab = self.space % 2
        self.chunk = 2 * self.far + self.slab
        self.pair = self.space // 2
        self.odd = self.pair % 2

    def lower(self, slot, bit):
        value = (self.tm // (1 << bit)) % 2
        if bit == 1 and slot == 1:
            value = 1 - value
        return value == 0

    def signs(self, slot, bit, level):
        is_lower = self.lower(slot, bit)
        sign = jnp.where(is_lower, 1.0, -1.0).astype(jnp.float32)
        return sign, jnp.where(is_lower, 0.0, 0.5 * level).astype(jnp.float32)

    def sweep(self, width):
        first = jnp.where(self.chunk == 0, 0.0, 1.0).astype(jnp.float32)
        last = jnp.where(self.chunk == 3, 0.0, 1.0).astype(jnp.float32)
        return Sweep(width, first, last, width - SPARE - 1)

    def spot(self, side, distance, planes):
        is_top = self.odd == side
        return jnp.where(is_top, planes - 1 - distance, distance)

    def open_face(self, side):
        if side == 0:
            return jnp.float32(1.0)
        closed = (self.pair == 0) | (self.pair == self.pairs - 1)
        return jnp.where(closed, 0.0, 1.0).astype(jnp.float32)


def call(body, outs, *args, spaces=None, scratch=(), flops=0, smem_outs=(), grid=(), blocks=None, out_block=None):
    spaces = spaces or {}
    blocks = blocks or {}
    in_specs = [blocks.get(i, pl.BlockSpec(memory_space=spaces.get(i, VMEM))) for i in range(len(args))]
    out_specs = [out_block or pl.BlockSpec(memory_space=SMEM if i in smem_outs else VMEM) for i in range(len(outs))]
    moved = sum(a.size * 4 for a in args) + sum(o.size * 4 for o in outs)
    return pl.pallas_call(
        body,
        grid=grid,
        out_shape=outs,
        in_specs=in_specs,
        out_specs=out_specs,
        scratch_shapes=list(scratch),
        compiler_params=pltpu.CompilerParams(vmem_limit_bytes=40 << 20),
        cost_estimate=pl.CostEstimate(flops=int(flops), bytes_accessed=int(moved), transcendentals=0),
    )(*args)


def f32(*shape):
    return jax.ShapeDtypeStruct(shape, jnp.float32)


def first_kernel(own_ref, partner_ref, coeff_ref, offset_ref, level_ref, *refs):
    out_refs, whole = refs[:4], refs[4]
    planes, _, width = own_ref.shape
    place = Place()
    sign, level = place.signs(0, 0, level_ref[0])
    offset = offset_ref[0, 0, 0]
    step = width // 4
    zero = jnp.zeros((8, LANES), jnp.float32)

    def body(z, carry):
        rows = [coeff_ref[0, 0, k, pl.ds(z, 1), :] for k in range(BAND)]
        warped = warped_plane(partner_ref[z], rows, offset)
        value = haar(own_ref[z], warped, sign, level, 0.5 * root_half)
        whole[z] = joined(moved_right(cells(value) + [zero], SPARE, zero))
        return carry

    lax.fori_loop(0, planes, body, 0, unroll=2)
    for number, out_ref in enumerate(out_refs):
        start = pl.multiple_of((place.chunk ^ number) * step, LANES)
        out_ref[...] = whole[:, :, pl.ds(start, step + LANES)]


def coeff_kernel(first, coeff_ref, offset_ref, *refs):
    out_refs, whole = refs[:4], refs[4]
    planes, width = coeff_ref.shape[3:]
    place = Place()
    step = width // 4
    zero = jnp.zeros((8, LANES), jnp.float32)
    lanes = lane_ids()
    for k in range(BAND):
        for z in range(0, planes, 8):
            value = coeff_ref[0, 0, k, z : z + 8, :]
            whole[k, z : z + 8] = joined(moved_right(cells(value) + [zero], SPARE, zero))
    offset = offset_ref[0, 0, first + pl.program_id(0)].astype(jnp.float32)
    for number, out_ref in enumerate(out_refs):
        start = pl.multiple_of((place.chunk ^ number) * step, LANES)
        out_ref[0] = whole[:, :, pl.ds(start, step + LANES)]
        out_ref[0, 0, 0:8, 0:LANES] = jnp.where(lanes == 0, offset, out_ref[0, 0, 0:8, 0:LANES])


def gather_coeff_kernel(self_ref, near_ref, far_ref, across_ref, out_ref, offset_ref):
    place = Place()
    sections = self_ref.shape[0]
    for number, ref in enumerate((self_ref, near_ref, far_ref, across_ref)):
        slot = number // 2
        slab = place.slab ^ (number % 2)
        for section in range(sections):
            out_ref[section, slot, slab] = ref[section]
            corner = ref[section, 0, 0:8, 0:LANES]
            offset = jnp.max(jnp.where(lane_ids() == 0, corner, -100.0))
            offset_ref[section, slot, slab] = offset.astype(jnp.int32)


def start_kernel(self_ref, near_ref, far_ref, across_ref, state_ref, side0_ref, side1_ref):
    place = Place()
    half = self_ref.shape[0]
    planes = 2 * half
    for number, ref in enumerate((self_ref, near_ref, far_ref, across_ref)):
        slot = number // 2
        slab = place.slab ^ (number % 2)
        state_ref[slot, pl.ds(slab * half, half)] = ref[...]
    for slot in range(2):
        for side, out_ref in enumerate((side0_ref, side1_ref)):
            for e in range(EDGE):
                out_ref[slot, e] = state_ref[slot, place.spot(side, e, planes)]


def trapezoid(place, load, planes, out_ref, saved_ref, one, two):
    width = one.shape[-1]
    sweep = place.sweep(width)
    for level in range(1, SWEEPS + 1):
        def source(slot, p, level=level):
            if level == 1:
                return load(slot, p)
            return (one, two)[level % 2][slot, p]

        def put(slot, p, value, level=level):
            if level == SWEEPS:
                out_ref[slot, p - EDGE] = value
            else:
                (two, one)[level % 2][slot, p] = value

        carry = []
        for slot in range(2):
            low, here = source(slot, level - 1), source(slot, level)
            carry += [here, sweep.depth(low, here)]

        def body(i, carry):
            return step(i, carry, GROUP)

        def step(i, carry, group):
            new = []
            for slot in range(2):
                here, below = carry[2 * slot : 2 * slot + 2]
                for j in range(group):
                    p = level + GROUP * i + j
                    high = source(slot, p + 1)
                    above = sweep.depth(here, high)
                    put(slot, p, sweep.plane(here, below, above))
                    here, below = high, above
                new += [here, below]
            return new

        count = planes - 2 * level
        carry = lax.fori_loop(0, count // GROUP, body, carry)
        if count % GROUP:
            step(count // GROUP, carry, count % GROUP)
        if level < SWEEPS:
            kept = (two, one)[level % 2]
            for slot in range(2):
                for side in range(2):
                    for j in range(2):
                        spot = place.spot(side, level + j, planes)
                        saved_ref[side, slot, level - 1, j] = kept[slot, spot]


def inner_first_kernel(state_ref, out_ref, saved_ref, one, two):
    place = Place()
    trapezoid(place, lambda slot, p: state_ref[slot, p], state_ref.shape[1], out_ref, saved_ref, one, two)


def inner_kernel(section, bit, own_ref, partner_ref, side0_ref, side1_ref, coeff_ref, offset_ref, level_ref,
                 out_ref, saved_ref, zero_level, one, two):
    place = Place()
    inner = own_ref.shape[1]
    planes = inner + 2 * EDGE
    half = planes // 2
    group = 0 if section == 1 else section - 2
    for slot in range(2):
        for side, ref in enumerate((side0_ref, side1_ref)):
            for e in range(EDGE):
                zero_level[slot, place.spot(side, e, planes)] = ref[slot, e]
    for slot in range(2):
        sign, level = place.signs(slot, bit, level_ref[section])
        other = 1 - slot if bit == 1 else slot
        for slab in range(2):
            offset = offset_ref[group, slot, slab]
            start, stop = (EDGE, half) if slab == 0 else (half, planes - EDGE)

            def body(p, carry):
                rows = [coeff_ref[group, slot, slab, k, pl.ds(p - slab * half, 1), :] for k in range(BAND)]
                warped = warped_plane(partner_ref[other, p - EDGE], rows, offset)
                zero_level[slot, p] = haar(own_ref[slot, p - EDGE], warped, sign, level, root_half)
                return carry

            lax.fori_loop(start, stop, body, 0, unroll=4)
    trapezoid(place, lambda slot, p: zero_level[slot, p], planes, out_ref, saved_ref, one, two)


def wedge(place, sweep, side, slot, edge_ref, halo_ref, saved_ref):
    open_face = place.open_face(side)
    values = [halo_ref[slot, h] for h in (3, 2, 1, 0)] + [edge_ref[slot, 0], edge_ref[slot, 1]]
    for level in range(1, SWEEPS + 1):
        fluxes = [sweep.depth(a, b) for a, b in zip(values[:-1], values[1:])]
        fluxes[EDGE - level] = fluxes[EDGE - level] * open_face
        values = [sweep.plane(values[i], fluxes[i - 1], fluxes[i]) for i in range(1, 5)]
        if level < SWEEPS:
            values += [saved_ref[side, slot, level - 1, j] for j in range(2)]
    return values


def haar_edges(place, section, bit, own_ref, partner_ref, coeff_ref, offset_ref, level_ref, outs):
    half = coeff_ref.shape[4]
    group = 0 if section == 1 else section - 2
    planes = 2 * half
    for slot in range(2):
        sign, level = place.signs(slot, bit, level_ref[section])
        other = 1 - slot if bit == 1 else slot
        for side in range(2):
            slab = jnp.where(place.odd == side, 1, 0)
            offset = offset_ref[group, slot, slab]

            def body(e, carry):
                z = place.spot(side, e, planes) - slab * half
                rows = [coeff_ref[group, slot, slab, k, pl.ds(z, 1), :] for k in range(BAND)]
                warped = warped_plane(partner_ref[side, other, e], rows, offset)
                outs[side][slot, e] = haar(own_ref[side, slot, e], warped, sign, level, root_half)
                return carry

            lax.fori_loop(0, EDGE, body, 0, unroll=True)


def wedge_kernel(side0_ref, side1_ref, halo0_ref, halo1_ref, saved_ref, out_ref):
    place = Place()
    sweep = place.sweep(side0_ref.shape[-1])
    for slot in range(2):
        for side, (edge, halo) in enumerate(((side0_ref, halo0_ref), (side1_ref, halo1_ref))):
            for e, value in enumerate(wedge(place, sweep, side, slot, edge, halo, saved_ref)):
                out_ref[side, slot, e] = value


def wedge_haar_kernel(section, side0_ref, side1_ref, halo0_ref, halo1_ref, saved_ref, coeff_ref, offset_ref, level_ref,
                      out0_ref, out1_ref, kept):
    wedge_kernel(side0_ref, side1_ref, halo0_ref, halo1_ref, saved_ref, kept)
    haar_edges(Place(), section, 1, kept, kept, coeff_ref, offset_ref, level_ref, (out0_ref, out1_ref))


def haar_kernel(section, bit, own_ref, partner_ref, coeff_ref, offset_ref, level_ref, out0_ref, out1_ref):
    haar_edges(Place(), section, bit, own_ref, partner_ref, coeff_ref, offset_ref, level_ref, (out0_ref, out1_ref))


def pieces_kernel(inner_ref, edge_ref, *refs):
    out_refs, whole = refs[:4], refs[4]
    place = Place()
    inner = inner_ref.shape[1]
    planes = inner + 2 * EDGE
    half = planes // 2
    step = whole.shape[-1]
    zero = jnp.zeros((8, LANES), jnp.float32)

    def put(slot, p, value):
        whole[slot, p] = 2.0 * joined(moved_left(cells(value), SPARE)[: step // LANES])

    for slot in range(2):
        def body(p, carry):
            put(slot, p, inner_ref[slot, p - EDGE])
            return carry

        lax.fori_loop(EDGE, planes - EDGE, body, 0, unroll=4)
        for side in range(2):
            for e in range(EDGE):
                put(slot, place.spot(side, e, planes), edge_ref[side, slot, e])
    for number, out_ref in enumerate(out_refs):
        slab = place.slab ^ (number % 2)
        out_ref[...] = whole[number // 2, pl.ds(slab * half, half)]


def output_kernel(self_ref, near_ref, far_ref, across_ref, out_ref):
    place = Place()
    step = self_ref.shape[-1]
    for number, ref in enumerate((self_ref, near_ref, far_ref, across_ref)):
        start = pl.multiple_of((place.chunk ^ number) * step, LANES)
        out_ref[:, :, pl.ds(start, step)] = ref[...]


def on_device(volume, warp_coef, offsets, thresholds):
    frames, slabs = lax.axis_size("tm"), lax.axis_size("space")
    levels = frames.bit_length() - 1
    pairs = slabs // 2
    _, half, rows, length = volume.shape
    planes = 2 * half
    inner = planes - 2 * EDGE
    width = length // 4 + 2 * SPARE
    axes = ("tm", "space")

    def route(frame_bits, slab_bits):
        return [(f * slabs + s, (f ^ frame_bits) * slabs + (s ^ slab_bits)) for f in range(frames) for s in range(slabs)]

    def swap(value, frame_bits, slab_bits=0):
        return lax.ppermute(value, axes, route(frame_bits, slab_bits))

    def spread(pieces):
        return (pieces[0], swap(pieces[1], 0, 1), swap(pieces[2], 2, 0), swap(pieces[3], 2, 1))

    def halo(side0, side1):
        first = [(s, s ^ 2) for s in range(slabs)]
        second = []
        for s in range(slabs):
            pair = s // 2 + 1 if (s // 2) % 2 else s // 2 - 1
            if 0 <= pair < pairs:
                second.append((s, 2 * pair + s % 2))
        return lax.ppermute(side0, "space", first), lax.ppermute(side1, "space", second)

    state_shape = f32(2, planes, rows, width)
    side_shape = f32(2, EDGE, rows, width)
    inner_shape = f32(2, inner, rows, width)
    saved_shape = f32(2, 2, SWEEPS - 1, 2, rows, width)
    level_scratch = pltpu.VMEM((2, planes, rows, width), jnp.float32)
    sweep_flops = 8 * 2 * planes * rows * width * 30

    own_volume = volume[0]
    received = swap(own_volume, 1)

    def coeff_pieces(first, count):
        return call(
            functools.partial(coeff_kernel, first), [f32(count, BAND, half, width)] * 4, warp_coef, offsets, spaces={1: SMEM}, flops=1 << 20,
            grid=(count,),
            blocks={0: pl.BlockSpec((1, 1, BAND, half, length), lambda i: (0, first + i, 0, 0, 0))},
            out_block=pl.BlockSpec((1, BAND, half, width), lambda i: (i, 0, 0, 0)),
            scratch=[pltpu.VMEM((BAND, half, length + LANES), jnp.float32)],
        )

    def coeff_state(pieces, count):
        return call(
            gather_coeff_kernel,
            [f32(count, 2, 2, BAND, half, width), jax.ShapeDtypeStruct((count, 2, 2), jnp.int32)],
            *spread(pieces), smem_outs=(1,), flops=1 << 20,
        )

    early_coeff = coeff_pieces(1, 1)
    late_coeff = coeff_pieces(2, SECTIONS - 2)
    part = pl.BlockSpec((8, rows, length), lambda i: (i, 0, 0))
    pieces = call(
        first_kernel, [f32(half, rows, width)] * 4, own_volume, received, warp_coef, offsets, thresholds,
        spaces={3: SMEM, 4: SMEM}, flops=1 << 23, grid=(half // 8,),
        blocks={0: part, 1: part, 2: pl.BlockSpec((1, 1, BAND, 8, length), lambda i: (0, 0, 0, i, 0))},
        out_block=pl.BlockSpec((8, rows, width), lambda i: (i, 0, 0)),
        scratch=[pltpu.VMEM((8, rows, length + LANES), jnp.float32)],
    )
    state, side0, side1 = call(start_kernel, [state_shape, side_shape, side_shape], *spread(pieces), flops=1 << 20)
    halo0, halo1 = halo(side0, side1)
    early_coeff, state = lax.optimization_barrier((early_coeff, state))
    coeff, shift = coeff_state(early_coeff, 1)
    own, saved = call(
        inner_first_kernel, [inner_shape, saved_shape], state, scratch=[level_scratch] * 2, flops=sweep_flops
    )
    late_coeff, own = lax.optimization_barrier((late_coeff, own))
    later = coeff_state(late_coeff, SECTIONS - 2)
    for section in range(1, SECTIONS):
        bit = section % levels
        if section == 2:
            coeff, shift = later
        if bit == 1:
            partner = own
            side0, side1 = call(
                functools.partial(wedge_haar_kernel, section), [side_shape, side_shape],
                side0, side1, halo0, halo1, saved, coeff, shift, thresholds,
                spaces={6: SMEM, 7: SMEM}, scratch=[pltpu.VMEM((2, 2, EDGE, rows, width), jnp.float32)], flops=1 << 23,
            )
        else:
            partner = swap(own, 1 << bit)
            (edges,) = call(
                wedge_kernel, [f32(2, 2, EDGE, rows, width)], side0, side1, halo0, halo1, saved, flops=1 << 23
            )
            side0, side1 = call(
                functools.partial(haar_kernel, section, bit), [side_shape, side_shape],
                edges, swap(edges, 1 << bit), coeff, shift, thresholds, spaces={3: SMEM, 4: SMEM}, flops=1 << 22,
            )
        halo0, halo1 = halo(side0, side1)
        own, saved = call(
            functools.partial(inner_kernel, section, bit), [inner_shape, saved_shape],
            own, partner, side0, side1, coeff, shift, thresholds,
            spaces={5: SMEM, 6: SMEM}, scratch=[level_scratch] * 3, flops=sweep_flops,
        )
    (edges,) = call(
        wedge_kernel, [f32(2, 2, EDGE, rows, width)], side0, side1, halo0, halo1, saved, flops=1 << 23
    )
    pieces = call(
        pieces_kernel, [f32(half, rows, length // 4)] * 4, own, edges, flops=1 << 20,
        scratch=[pltpu.VMEM((2, planes, rows, length // 4), jnp.float32)],
    )
    (out,) = call(output_kernel, [f32(half, rows, length)], *spread(pieces), flops=1 << 20)
    return out[None]


def solution(mesh):
    return jax.shard_map(
        on_device,
        mesh=mesh,
        in_specs=(
            P("tm", "space", None, None),
            P("tm", None, None, "space", None),
            P("tm", "space", None),
            P(),
        ),
        out_specs=P("tm", "space", None, None),
        check_vma=False,
    )
```

profile of v0, /device:TPU:8, one launch (start us, length us, event | category | flops | bytes accessed | tf_op | source)
XLA Modules:
  0.0 133.5 jit_solution(8755199670948818683)
XLA Ops:
  0.0 0.0 collective-permute-start
  0.0 2.9 %collective-permute-done.partner_ref = f32[16,8,2048]{2,1,0:T(8,128)S(1)} collective-permute-done((f32[16,8,2048]{2,1,0:T(8,128)}, f32[16,8,2048]{2,1,0:T(8,128)S(1)}, u32[]{:S(2)}, u32[]{:S(2)}) %collective-permute-start) | collective-permute-done | bytes 1048608 | tf_op jit(solution)/shard_map/ppermute | solution.py:405
  2.9 1.6 %copy-done = f32[1,4,4,16,2048]{4,3,2,1,0:T(8,128)S(1)} copy-done((f32[1,4,4,16,2048]{4,3,2,1,0:T(8,128)S(1)}, f32[1,4,4,16,2048]{4,3,2,1,0:T(8,128)}, u32[]{:S(2)}) %copy-start) | copy-done | bytes 2097176
  4.5 1.2 copy-done.2
  5.7 0.7 copy-done.3
  6.3 0.7 copy-done.5
  7.0 4.3 %shard_map.48 = (f32[16,8,640]{2,1,0:T(8,128)S(1)}, f32[16,8,640]{2,1,0:T(8,128)S(1)}, f32[16,8,640]{2,1,0:T(8,128)S(1)}, f32[16,8,640]{2,1,0:T(8,128)S(1)}) custom-call(f32[16,8,2048]{2,1,0:T(8,128)S(1)} %bitcast.3, f32[16,8,2048]{2,1,0:T(8,128)S(1)} %collective-permute-done.partner_ref, f32[1,4,4,16,2048]{4,3,2,1,0:T(8,128)S(1)} %copy-done, ...), custom_call_target="tpu_custom_call" | custom-call | flops 8388608 | bytes 5505056 | tf_op jit(solution)/shard_map/pallas_call | solution.py:140
  11.3 1.6 %collective-permute-start.1 = (f32[16,8,640]{2,1,0:T(8,128)S(1)}, f32[16,8,640]{2,1,0:T(8,128)S(1)}, u32[]{:S(2)}, u32[]{:S(2)}) collective-permute-start(f32[16,8,640]{2,1,0:T(8,128)S(1)} %get-tuple-element.61), channel_id=1, source_target_pairs={{0,1},{1,0},{2,3},{3,2},{4,5},{5,4},{6,7},{7,6},{8,9},{9,8},{10,11... | collective-permute-start | bytes 983048 | tf_op jit(solution)/shard_map/ppermute | solution.py:405
  12.9 1.5 %collective-permute-start.2 = (f32[16,8,640]{2,1,0:T(8,128)S(1)}, f32[16,8,640]{2,1,0:T(8,128)S(1)}, u32[]{:S(2)}, u32[]{:S(2)}) collective-permute-start(f32[16,8,640]{2,1,0:T(8,128)S(1)} %get-tuple-element.62), channel_id=1, source_target_pairs={{0,16},{1,17},{2,18},{3,19},{4,20},{5,21},{6,22},{7,23},{8,24},{9,... | collective-permute-start | bytes 983048 | tf_op jit(solution)/shard_map/ppermute | solution.py:405
  14.4 0.5 collective-permute-start.3
  14.9 0.8 shard_map.47
  15.7 5.5 %collective-permute-done.1.near_ref = f32[16,8,640]{2,1,0:T(8,128)S(1)} collective-permute-done((f32[16,8,640]{2,1,0:T(8,128)S(1)}, f32[16,8,640]{2,1,0:T(8,128)S(1)}, u32[]{:S(2)}, u32[]{:S(2)}) %collective-permute-start.1) | collective-permute-done | bytes 327712 | tf_op jit(solution)/shard_map/ppermute | solution.py:405
  21.2 2.4 %collective-permute-done.2.far_ref = f32[16,8,640]{2,1,0:T(8,128)S(1)} collective-permute-done((f32[16,8,640]{2,1,0:T(8,128)S(1)}, f32[16,8,640]{2,1,0:T(8,128)S(1)}, u32[]{:S(2)}, u32[]{:S(2)}) %collective-permute-start.2) | collective-permute-done | bytes 327712 | tf_op jit(solution)/shard_map/ppermute | solution.py:405
  23.5 5.8 %collective-permute-done.3.across_ref = f32[16,8,640]{2,1,0:T(8,128)S(1)} collective-permute-done((f32[16,8,640]{2,1,0:T(8,128)S(1)}, f32[16,8,640]{2,1,0:T(8,128)S(1)}, u32[]{:S(2)}, u32[]{:S(2)}) %collective-permute-start.3) | collective-permute-done | bytes 327712 | tf_op jit(solution)/shard_map/ppermute | solution.py:405
  29.4 0.1 shard_map.49
  29.5 1.6 %collective-permute-start.6 = (f32[1,4,16,640]{3,2,1,0:T(8,128)S(1)}, f32[1,4,16,640]{3,2,1,0:T(8,128)S(1)}, u32[]{:S(2)}, u32[]{:S(2)}) collective-permute-start(f32[1,4,16,640]{3,2,1,0:T(8,128)S(1)} %get-tuple-element.72), channel_id=1, source_target_pairs={{0,1},{1,0},{2,3},{3,2},{4,5},{5,4},{6,7},{7,6},{8,9},{9,8},{10,11... | collective-permute-start | bytes 491528 | tf_op jit(solution)/shard_map/ppermute | solution.py:405
  31.1 1.5 %collective-permute-start.7 = (f32[1,4,16,640]{3,2,1,0:T(8,128)S(1)}, f32[1,4,16,640]{3,2,1,0:T(8,128)S(1)}, u32[]{:S(2)}, u32[]{:S(2)}) collective-permute-start(f32[1,4,16,640]{3,2,1,0:T(8,128)S(1)} %get-tuple-element.73), channel_id=1, source_target_pairs={{0,16},{1,17},{2,18},{3,19},{4,20},{5,21},{6,22},{7,23},{8,24},{9,... | collective-permute-start | bytes 491528 | tf_op jit(solution)/shard_map/ppermute | solution.py:405
  32.6 0.5 collective-permute-start.8
  33.0 0.3 collective-permute-start.4
  33.4 4.7 %collective-permute-start.5 = (f32[2,4,8,640]{3,2,1,0:T(8,128)S(1)}, f32[2,4,8,640]{3,2,1,0:T(8,128)S(1)}, u32[]{:S(2)}, u32[]{:S(2)}) collective-permute-start(f32[2,4,8,640]{3,2,1,0:T(8,128)S(1)} %get-tuple-element.69.side1_ref), channel_id=1, source_target_pairs={{2,4},{3,5},{4,2},{5,3},{10,12},{11,13},{12,10},{13,11},{18,20},{1... | collective-permute-start | bytes 491528 | tf_op jit(solution)/shard_map/ppermute | solution.py:417
  38.1 1.1 shard_map.46
  39.2 0.0 copy-start.4
  39.2 5.8 %shard_map.50 = (f32[2,24,8,640]{3,2,1,0:T(8,128)S(1)}, f32[2,2,3,2,8,640]{5,4,3,2,1,0:T(8,128)S(1)}) custom-call(f32[2,32,8,640]{3,2,1,0:T(8,128)S(1)} %get-tuple-element.65.state_ref), custom_call_target="tpu_custom_call" | custom-call | flops 78643200 | bytes 2785280 | tf_op jit(solution)/shard_map/pallas_call | solution.py:140
  45.0 0.0 collective-permute-done.6.near_ref
  45.0 0.0 collective-permute-done.7.far_ref
  45.0 0.0 collective-permute-done.8.across_ref
  45.0 0.7 shard_map.51
  45.8 0.0 collective-permute-done.4.halo0_ref
  45.8 5.8 %shard_map.52 = (f32[2,4,8,640]{3,2,1,0:T(8,128)S(1)}, f32[2,4,8,640]{3,2,1,0:T(8,128)S(1)}) custom-call(f32[2,4,8,640]{3,2,1,0:T(8,128)S(1)} %get-tuple-element.68.side0_ref, f32[2,4,8,640]{3,2,1,0:T(8,128)S(1)} %get-tuple-element.69.side1_ref, f32[2,4,8,640]{3,2,1,0:T(8,128)S(1)} %collective-permute-done.4.halo0_ref, ...), custom_call_target="tpu_custom_call" | custom-call | flops 8388608 | bytes 2129952 | tf_op jit(solution)/shard_map/pallas_call | solution.py:140
  51.6 9.4 %shard_map.53 = (f32[2,24,8,640]{3,2,1,0:T(8,128)S(1)}, f32[2,2,3,2,8,640]{5,4,3,2,1,0:T(8,128)S(1)}) custom-call(f32[2,24,8,640]{3,2,1,0:T(8,128)S(1)} %get-tuple-element.67.own_ref.partner_ref, f32[2,24,8,640]{3,2,1,0:T(8,128)S(1)} %get-tuple-element.67.own_ref.partner_ref, f32[2,4,8,640]{3,2,1,0:T(8,128)S(1)} %get-tuple-element.77.side0_ref, ...), custom_call_target="tpu_custom_call" | custom-call | flops 78643200 | bytes 4423712 | tf_op jit(solution)/shard_map/pallas_call | solution.py:140
  61.0 0.1 collective-permute-start.9
  61.0 0.1 collective-permute-start.10
  61.1 1.9 %collective-permute-start.11 = (f32[2,4,8,640]{3,2,1,0:T(8,128)S(1)}, f32[2,4,8,640]{3,2,1,0:T(8,128)S(1)}, u32[]{:S(2)}, u32[]{:S(2)}) collective-permute-start(f32[2,4,8,640]{3,2,1,0:T(8,128)S(1)} %get-tuple-element.78.side1_ref), channel_id=1, source_target_pairs={{2,4},{3,5},{4,2},{5,3},{10,12},{11,13},{12,10},{13,11},{18,20},{1... | collective-permute-start | bytes 491528 | tf_op jit(solution)/shard_map/ppermute | solution.py:417
  63.0 1.6 %collective-permute-start.13 = (f32[2,4,16,640]{3,2,1,0:T(8,128)S(1)}, f32[2,4,16,640]{3,2,1,0:T(8,128)S(1)}, u32[]{:S(2)}, u32[]{:S(2)}) collective-permute-start(f32[2,4,16,640]{3,2,1,0:T(8,128)S(1)} %get-tuple-element.82), channel_id=1, source_target_pairs={{0,1},{1,0},{2,3},{3,2},{4,5},{5,4},{6,7},{7,6},{8,9},{9,8},{10,11... | collective-permute-start | bytes 983048 | tf_op jit(solution)/shard_map/ppermute | solution.py:405
  64.6 1.5 %collective-permute-start.14 = (f32[2,4,16,640]{3,2,1,0:T(8,128)S(1)}, f32[2,4,16,640]{3,2,1,0:T(8,128)S(1)}, u32[]{:S(2)}, u32[]{:S(2)}) collective-permute-start(f32[2,4,16,640]{3,2,1,0:T(8,128)S(1)} %get-tuple-element.83), channel_id=1, source_target_pairs={{0,16},{1,17},{2,18},{3,19},{4,20},{5,21},{6,22},{7,23},{8,24},{9,... | collective-permute-start | bytes 983048 | tf_op jit(solution)/shard_map/ppermute | solution.py:405
  66.1 1.5 %collective-permute-done.10.halo0_ref = f32[2,4,8,640]{3,2,1,0:T(8,128)S(1)} collective-permute-done((f32[2,4,8,640]{3,2,1,0:T(8,128)S(1)}, f32[2,4,8,640]{3,2,1,0:T(8,128)S(1)}, u32[]{:S(2)}, u32[]{:S(2)}) %collective-permute-start.10) | collective-permute-done | bytes 163872 | tf_op jit(solution)/shard_map/ppermute | solution.py:417
  67.6 2.4 %collective-permute-start.15 = (f32[2,4,16,640]{3,2,1,0:T(8,128)S(1)}, f32[2,4,16,640]{3,2,1,0:T(8,128)S(1)}, u32[]{:S(2)}, u32[]{:S(2)}) collective-permute-start(f32[2,4,16,640]{3,2,1,0:T(8,128)S(1)} %get-tuple-element.84), channel_id=1, source_target_pairs={{0,17},{1,16},{2,19},{3,18},{4,21},{5,20},{6,23},{7,22},{8,25},{9,... | collective-permute-start | bytes 983048 | tf_op jit(solution)/shard_map/ppermute | solution.py:405
  70.1 2.4 %shard_map.54.own_ref = f32[2,2,4,8,640]{4,3,2,1,0:T(8,128)S(1)} custom-call(f32[2,4,8,640]{3,2,1,0:T(8,128)S(1)} %get-tuple-element.77.side0_ref, f32[2,4,8,640]{3,2,1,0:T(8,128)S(1)} %get-tuple-element.78.side1_ref, f32[2,4,8,640]{3,2,1,0:T(8,128)S(1)} %collective-permute-done.10.halo0_ref, f32[2,4,8,640]{3,2,1,0:T(8,128)S(1)} %collective-permute-done.11.halo1_ref, ...), custom_call_target="tpu_custom_call" | custom-call | flops 8388608 | bytes 1474560 | tf_op jit(solution)/shard_map/pallas_call | solution.py:140
  72.5 0.1 collective-permute-start.12
  72.5 0.6 collective-permute-done.13.near_ref
  73.2 2.0 %collective-permute-done.14.far_ref = f32[2,4,16,640]{3,2,1,0:T(8,128)S(1)} collective-permute-done((f32[2,4,16,640]{3,2,1,0:T(8,128)S(1)}, f32[2,4,16,640]{3,2,1,0:T(8,128)S(1)}, u32[]{:S(2)}, u32[]{:S(2)}) %collective-permute-start.14) | collective-permute-done | bytes 327712 | tf_op jit(solution)/shard_map/ppermute | solution.py:405
  75.2 6.2 %collective-permute-done.15.across_ref = f32[2,4,16,640]{3,2,1,0:T(8,128)S(1)} collective-permute-done((f32[2,4,16,640]{3,2,1,0:T(8,128)S(1)}, f32[2,4,16,640]{3,2,1,0:T(8,128)S(1)}, u32[]{:S(2)}, u32[]{:S(2)}) %collective-permute-start.15) | collective-permute-done | bytes 327712 | tf_op jit(solution)/shard_map/ppermute | solution.py:405
  81.4 0.8 shard_map.55
  82.2 1.9 %shard_map.56 = (f32[2,4,8,640]{3,2,1,0:T(8,128)S(1)}, f32[2,4,8,640]{3,2,1,0:T(8,128)S(1)}) custom-call(f32[2,2,4,8,640]{4,3,2,1,0:T(8,128)S(1)} %shard_map.54.own_ref, f32[2,2,4,8,640]{4,3,2,1,0:T(8,128)S(1)} %collective-permute-done.12.partner_ref, f32[2,2,2,4,16,640]{5,4,3,2,1,0:T(8,128)S(1)} %get-tuple-element.85.coeff_ref, ...), custom_call_target="tpu_custom_call" | custom-call | flops 4194304 | bytes 2293808 | tf_op jit(solution)/shard_map/pallas_call | solution.py:140
  84.1 0.5 collective-permute-start.16
  84.7 3.3 %collective-permute-start.17 = (f32[2,4,8,640]{3,2,1,0:T(8,128)S(1)}, f32[2,4,8,640]{3,2,1,0:T(8,128)S(1)}, u32[]{:S(2)}, u32[]{:S(2)}) collective-permute-start(f32[2,4,8,640]{3,2,1,0:T(8,128)S(1)} %get-tuple-element.88.side1_ref), channel_id=1, source_target_pairs={{2,4},{3,5},{4,2},{5,3},{10,12},{11,13},{12,10},{13,11},{18,20},{1... | collective-permute-start | bytes 491528 | tf_op jit(solution)/shard_map/ppermute | solution.py:417
  88.0 0.0 collective-permute-done.9.partner_ref
  88.0 9.4 %shard_map.57 = (f32[2,24,8,640]{3,2,1,0:T(8,128)S(1)}, f32[2,2,3,2,8,640]{5,4,3,2,1,0:T(8,128)S(1)}) custom-call(f32[2,24,8,640]{3,2,1,0:T(8,128)S(1)} %get-tuple-element.79.own_ref, f32[2,24,8,640]{3,2,1,0:T(8,128)S(1)} %collective-permute-done.9.partner_ref, f32[2,4,8,640]{3,2,1,0:T(8,128)S(1)} %get-tuple-element.87.side0_ref, ...), custom_call_target="tpu_custom_call" | custom-call | flops 78643200 | bytes 5079088 | tf_op jit(solution)/shard_map/pallas_call | solution.py:140
  97.4 0.0 collective-permute-done.16.halo0_ref
  97.4 0.0 collective-permute-done.17.halo1_ref
  97.4 5.8 %shard_map.58 = (f32[2,4,8,640]{3,2,1,0:T(8,128)S(1)}, f32[2,4,8,640]{3,2,1,0:T(8,128)S(1)}) custom-call(f32[2,4,8,640]{3,2,1,0:T(8,128)S(1)} %get-tuple-element.87.side0_ref, f32[2,4,8,640]{3,2,1,0:T(8,128)S(1)} %get-tuple-element.88.side1_ref, f32[2,4,8,640]{3,2,1,0:T(8,128)S(1)} %collective-permute-done.16.halo0_ref, ...), custom_call_target="tpu_custom_call" | custom-call | flops 8388608 | bytes 2785328 | tf_op jit(solution)/shard_map/pallas_call | solution.py:140
  103.2 0.1 collective-permute-start.18
  103.3 2.7 %collective-permute-start.19 = (f32[2,4,8,640]{3,2,1,0:T(8,128)S(1)}, f32[2,4,8,640]{3,2,1,0:T(8,128)S(1)}, u32[]{:S(2)}, u32[]{:S(2)}) collective-permute-start(f32[2,4,8,640]{3,2,1,0:T(8,128)S(1)} %get-tuple-element.92.side1_ref), channel_id=1, source_target_pairs={{2,4},{3,5},{4,2},{5,3},{10,12},{11,13},{12,10},{13,11},{18,20},{1... | collective-permute-start | bytes 491528 | tf_op jit(solution)/shard_map/ppermute | solution.py:417
  106.0 9.4 %shard_map.59 = (f32[2,24,8,640]{3,2,1,0:T(8,128)S(1)}, f32[2,2,3,2,8,640]{5,4,3,2,1,0:T(8,128)S(1)}) custom-call(f32[2,24,8,640]{3,2,1,0:T(8,128)S(1)} %get-tuple-element.89.own_ref.partner_ref, f32[2,24,8,640]{3,2,1,0:T(8,128)S(1)} %get-tuple-element.89.own_ref.partner_ref, f32[2,4,8,640]{3,2,1,0:T(8,128)S(1)} %get-tuple-element.91.side0_ref, ...), custom_call_target="tpu_custom_call" | custom-call | flops 78643200 | bytes 5079088 | tf_op jit(solution)/shard_map/pallas_call | solution.py:140
  115.4 0.0 collective-permute-done.18.halo0_ref
  115.4 2.4 %shard_map.60.edge_ref = f32[2,2,4,8,640]{4,3,2,1,0:T(8,128)S(1)} custom-call(f32[2,4,8,640]{3,2,1,0:T(8,128)S(1)} %get-tuple-element.91.side0_ref, f32[2,4,8,640]{3,2,1,0:T(8,128)S(1)} %get-tuple-element.92.side1_ref, f32[2,4,8,640]{3,2,1,0:T(8,128)S(1)} %collective-permute-done.18.halo0_ref, f32[2,4,8,640]{3,2,1,0:T(8,128)S(1)} %collective-permute-done.19.halo1_ref, ...), custom_call_target="tpu_custom_call" | custom-call | flops 8388608 | bytes 1474560 | tf_op jit(solution)/shard_map/pallas_call | solution.py:140
  117.8 1.3 shard_map.61
  119.1 1.6 %collective-permute-start.20 = (f32[16,8,512]{2,1,0:T(8,128)S(1)}, f32[16,8,512]{2,1,0:T(8,128)S(1)}, u32[]{:S(2)}, u32[]{:S(2)}) collective-permute-start(f32[16,8,512]{2,1,0:T(8,128)S(1)} %get-tuple-element.96), channel_id=1, source_target_pairs={{0,1},{1,0},{2,3},{3,2},{4,5},{5,4},{6,7},{7,6},{8,9},{9,8},{10,11... | collective-permute-start | bytes 786440 | tf_op jit(solution)/shard_map/ppermute | solution.py:405
  120.7 1.5 %collective-permute-start.21 = (f32[16,8,512]{2,1,0:T(8,128)S(1)}, f32[16,8,512]{2,1,0:T(8,128)S(1)}, u32[]{:S(2)}, u32[]{:S(2)}) collective-permute-start(f32[16,8,512]{2,1,0:T(8,128)S(1)} %get-tuple-element.97), channel_id=1, source_target_pairs={{0,16},{1,17},{2,18},{3,19},{4,20},{5,21},{6,22},{7,23},{8,24},{9,... | collective-permute-start | bytes 786440 | tf_op jit(solution)/shard_map/ppermute | solution.py:405
  122.2 0.5 collective-permute-start.22
  122.6 4.8 %collective-permute-done.20.near_ref = f32[16,8,512]{2,1,0:T(8,128)S(1)} collective-permute-done((f32[16,8,512]{2,1,0:T(8,128)S(1)}, f32[16,8,512]{2,1,0:T(8,128)S(1)}, u32[]{:S(2)}, u32[]{:S(2)}) %collective-permute-start.20) | collective-permute-done | bytes 262176 | tf_op jit(solution)/shard_map/ppermute | solution.py:405
  127.5 2.2 %collective-permute-done.21.far_ref = f32[16,8,512]{2,1,0:T(8,128)S(1)} collective-permute-done((f32[16,8,512]{2,1,0:T(8,128)S(1)}, f32[16,8,512]{2,1,0:T(8,128)S(1)}, u32[]{:S(2)}, u32[]{:S(2)}) %collective-permute-start.21) | collective-permute-done | bytes 262176 | tf_op jit(solution)/shard_map/ppermute | solution.py:405
  129.7 2.8 %collective-permute-done.22.across_ref = f32[16,8,512]{2,1,0:T(8,128)S(1)} collective-permute-done((f32[16,8,512]{2,1,0:T(8,128)S(1)}, f32[16,8,512]{2,1,0:T(8,128)S(1)}, u32[]{:S(2)}, u32[]{:S(2)}) %collective-permute-start.22) | collective-permute-done | bytes 262176 | tf_op jit(solution)/shard_map/ppermute | solution.py:405
  132.5 1.1 shard_map.62
  (11 shorter events, 0.0 us)
Async XLA Ops:
  0.0 2.9 %collective-permute-start = (f32[16,8,2048]{2,1,0:T(8,128)}, f32[16,8,2048]{2,1,0:T(8,128)S(1)}, u32[]{:S(2)}, u32[]{:S(2)}) collective-permute-start(f32[16,8,2048]{2,1,0:T(8,128)} %bitcast.2), channel_id=1, source_target_pairs={{0,8},{1,9},{2,10},{3,11},{4,12},{5,13},{6,14},{7,15},{8,0},{9,1},... | collective-permute-start | bytes 3145736 | tf_op jit(solution)/shard_map/ppermute | solution.py:405
  2.9 1.6 %copy-start = (f32[1,4,4,16,2048]{4,3,2,1,0:T(8,128)S(1)}, f32[1,4,4,16,2048]{4,3,2,1,0:T(8,128)}, u32[]{:S(2)}) copy-start(f32[1,4,4,16,2048]{4,3,2,1,0:T(8,128)} %coeff_ref.5) | copy-start | bytes 6291460
  4.5 1.2 copy-start.2
  5.7 0.7 copy-start.3
  6.3 0.7 copy-start.5
  7.0 7.9 %copy-start.1 = (f32[1,4,4,16,2048]{4,3,2,1,0:T(8,128)S(1)}, f32[1,4,4,16,2048]{4,3,2,1,0:T(8,128)}, u32[]{:S(2)}) copy-start(f32[1,4,4,16,2048]{4,3,2,1,0:T(8,128)} %coeff_ref.5) | copy-start | bytes 6291460
  11.3 9.8 %collective-permute-start.1 = (f32[16,8,640]{2,1,0:T(8,128)S(1)}, f32[16,8,640]{2,1,0:T(8,128)S(1)}, u32[]{:S(2)}, u32[]{:S(2)}) collective-permute-start(f32[16,8,640]{2,1,0:T(8,128)S(1)} %get-tuple-element.61), channel_id=1, source_target_pairs={{0,1},{1,0},{2,3},{3,2},{4,5},{5,4},{6,7},{7,6},{8,9},{9,8},{10,11... | collective-permute-start | bytes 983048 | tf_op jit(solution)/shard_map/ppermute | solution.py:405
  12.9 10.6 %collective-permute-start.2 = (f32[16,8,640]{2,1,0:T(8,128)S(1)}, f32[16,8,640]{2,1,0:T(8,128)S(1)}, u32[]{:S(2)}, u32[]{:S(2)}) collective-permute-start(f32[16,8,640]{2,1,0:T(8,128)S(1)} %get-tuple-element.62), channel_id=1, source_target_pairs={{0,16},{1,17},{2,18},{3,19},{4,20},{5,21},{6,22},{7,23},{8,24},{9,... | collective-permute-start | bytes 983048 | tf_op jit(solution)/shard_map/ppermute | solution.py:405
  14.4 14.9 %collective-permute-start.3 = (f32[16,8,640]{2,1,0:T(8,128)S(1)}, f32[16,8,640]{2,1,0:T(8,128)S(1)}, u32[]{:S(2)}, u32[]{:S(2)}) collective-permute-start(f32[16,8,640]{2,1,0:T(8,128)S(1)} %get-tuple-element.63), channel_id=1, source_target_pairs={{0,17},{1,16},{2,19},{3,18},{4,21},{5,20},{6,23},{7,22},{8,25},{9,... | collective-permute-start | bytes 983048 | tf_op jit(solution)/shard_map/ppermute | solution.py:405
  29.5 15.5 %collective-permute-start.6 = (f32[1,4,16,640]{3,2,1,0:T(8,128)S(1)}, f32[1,4,16,640]{3,2,1,0:T(8,128)S(1)}, u32[]{:S(2)}, u32[]{:S(2)}) collective-permute-start(f32[1,4,16,640]{3,2,1,0:T(8,128)S(1)} %get-tuple-element.72), channel_id=1, source_target_pairs={{0,1},{1,0},{2,3},{3,2},{4,5},{5,4},{6,7},{7,6},{8,9},{9,8},{10,11... | collective-permute-start | bytes 491528 | tf_op jit(solution)/shard_map/ppermute | solution.py:405
  31.1 13.9 %collective-permute-start.7 = (f32[1,4,16,640]{3,2,1,0:T(8,128)S(1)}, f32[1,4,16,640]{3,2,1,0:T(8,128)S(1)}, u32[]{:S(2)}, u32[]{:S(2)}) collective-permute-start(f32[1,4,16,640]{3,2,1,0:T(8,128)S(1)} %get-tuple-element.73), channel_id=1, source_target_pairs={{0,16},{1,17},{2,18},{3,19},{4,20},{5,21},{6,22},{7,23},{8,24},{9,... | collective-permute-start | bytes 491528 | tf_op jit(solution)/shard_map/ppermute | solution.py:405
  32.6 12.5 %collective-permute-start.8 = (f32[1,4,16,640]{3,2,1,0:T(8,128)S(1)}, f32[1,4,16,640]{3,2,1,0:T(8,128)S(1)}, u32[]{:S(2)}, u32[]{:S(2)}) collective-permute-start(f32[1,4,16,640]{3,2,1,0:T(8,128)S(1)} %get-tuple-element.74), channel_id=1, source_target_pairs={{0,17},{1,16},{2,19},{3,18},{4,21},{5,20},{6,23},{7,22},{8,25},{9,... | collective-permute-start | bytes 491528 | tf_op jit(solution)/shard_map/ppermute | solution.py:405
  33.0 12.7 %collective-permute-start.4 = (f32[2,4,8,640]{3,2,1,0:T(8,128)S(1)}, f32[2,4,8,640]{3,2,1,0:T(8,128)S(1)}, u32[]{:S(2)}, u32[]{:S(2)}) collective-permute-start(f32[2,4,8,640]{3,2,1,0:T(8,128)S(1)} %get-tuple-element.68.side0_ref), channel_id=1, source_target_pairs={{0,2},{1,3},{2,0},{3,1},{4,6},{5,7},{6,4},{7,5},{8,10},{9,11},{10,... | collective-permute-start | bytes 491528 | tf_op jit(solution)/shard_map/ppermute | solution.py:417
  33.4 12.4 %collective-permute-start.5 = (f32[2,4,8,640]{3,2,1,0:T(8,128)S(1)}, f32[2,4,8,640]{3,2,1,0:T(8,128)S(1)}, u32[]{:S(2)}, u32[]{:S(2)}) collective-permute-start(f32[2,4,8,640]{3,2,1,0:T(8,128)S(1)} %get-tuple-element.69.side1_ref), channel_id=1, source_target_pairs={{2,4},{3,5},{4,2},{5,3},{10,12},{11,13},{12,10},{13,11},{18,20},{1... | collective-permute-start | bytes 491528 | tf_op jit(solution)/shard_map/ppermute | solution.py:417
  39.2 6.6 %copy-start.4 = (f32[4]{0:T(128)S(1)}, f32[4]{0:T(128)}, u32[]{:S(2)}) copy-start(f32[4]{0:T(128)} %level_ref.13) | copy-start | bytes 52
  61.0 27.1 %collective-permute-start.9 = (f32[2,24,8,640]{3,2,1,0:T(8,128)S(1)}, f32[2,24,8,640]{3,2,1,0:T(8,128)S(1)}, u32[]{:S(2)}, u32[]{:S(2)}) collective-permute-start(f32[2,24,8,640]{3,2,1,0:T(8,128)S(1)} %get-tuple-element.79.own_ref), channel_id=1, source_target_pairs={{0,8},{1,9},{2,10},{3,11},{4,12},{5,13},{6,14},{7,15},{8,0},{9,1},... | collective-permute-start | bytes 2949128 | tf_op jit(solution)/shard_map/ppermute | solution.py:405
  61.0 6.6 %collective-permute-start.10 = (f32[2,4,8,640]{3,2,1,0:T(8,128)S(1)}, f32[2,4,8,640]{3,2,1,0:T(8,128)S(1)}, u32[]{:S(2)}, u32[]{:S(2)}) collective-permute-start(f32[2,4,8,640]{3,2,1,0:T(8,128)S(1)} %get-tuple-element.77.side0_ref), channel_id=1, source_target_pairs={{0,2},{1,3},{2,0},{3,1},{4,6},{5,7},{6,4},{7,5},{8,10},{9,11},{10,... | collective-permute-start | bytes 491528 | tf_op jit(solution)/shard_map/ppermute | solution.py:417
  61.1 9.0 %collective-permute-start.11 = (f32[2,4,8,640]{3,2,1,0:T(8,128)S(1)}, f32[2,4,8,640]{3,2,1,0:T(8,128)S(1)}, u32[]{:S(2)}, u32[]{:S(2)}) collective-permute-start(f32[2,4,8,640]{3,2,1,0:T(8,128)S(1)} %get-tuple-element.78.side1_ref), channel_id=1, source_target_pairs={{2,4},{3,5},{4,2},{5,3},{10,12},{11,13},{12,10},{13,11},{18,20},{1... | collective-permute-start | bytes 491528 | tf_op jit(solution)/shard_map/ppermute | solution.py:417
  63.0 10.1 %collective-permute-start.13 = (f32[2,4,16,640]{3,2,1,0:T(8,128)S(1)}, f32[2,4,16,640]{3,2,1,0:T(8,128)S(1)}, u32[]{:S(2)}, u32[]{:S(2)}) collective-permute-start(f32[2,4,16,640]{3,2,1,0:T(8,128)S(1)} %get-tuple-element.82), channel_id=1, source_target_pairs={{0,1},{1,0},{2,3},{3,2},{4,5},{5,4},{6,7},{7,6},{8,9},{9,8},{10,11... | collective-permute-start | bytes 983048 | tf_op jit(solution)/shard_map/ppermute | solution.py:405
  64.6 10.6 %collective-permute-start.14 = (f32[2,4,16,640]{3,2,1,0:T(8,128)S(1)}, f32[2,4,16,640]{3,2,1,0:T(8,128)S(1)}, u32[]{:S(2)}, u32[]{:S(2)}) collective-permute-start(f32[2,4,16,640]{3,2,1,0:T(8,128)S(1)} %get-tuple-element.83), channel_id=1, source_target_pairs={{0,16},{1,17},{2,18},{3,19},{4,20},{5,21},{6,22},{7,23},{8,24},{9,... | collective-permute-start | bytes 983048 | tf_op jit(solution)/shard_map/ppermute | solution.py:405
  67.6 13.7 %collective-permute-start.15 = (f32[2,4,16,640]{3,2,1,0:T(8,128)S(1)}, f32[2,4,16,640]{3,2,1,0:T(8,128)S(1)}, u32[]{:S(2)}, u32[]{:S(2)}) collective-permute-start(f32[2,4,16,640]{3,2,1,0:T(8,128)S(1)} %get-tuple-element.84), channel_id=1, source_target_pairs={{0,17},{1,16},{2,19},{3,18},{4,21},{5,20},{6,23},{7,22},{8,25},{9,... | collective-permute-start | bytes 983048 | tf_op jit(solution)/shard_map/ppermute | solution.py:405
  72.5 9.7 %collective-permute-start.12 = (f32[2,2,4,8,640]{4,3,2,1,0:T(8,128)S(1)}, f32[2,2,4,8,640]{4,3,2,1,0:T(8,128)S(1)}, u32[]{:S(2)}, u32[]{:S(2)}) collective-permute-start(f32[2,2,4,8,640]{4,3,2,1,0:T(8,128)S(1)} %shard_map.54.own_ref), channel_id=1, source_target_pairs={{0,8},{1,9},{2,10},{3,11},{4,12},{5,13},{6,14},{7,15},{8,0},{9,1},... | collective-permute-start | bytes 983048 | tf_op jit(solution)/shard_map/ppermute | solution.py:405
  84.1 13.3 %collective-permute-start.16 = (f32[2,4,8,640]{3,2,1,0:T(8,128)S(1)}, f32[2,4,8,640]{3,2,1,0:T(8,128)S(1)}, u32[]{:S(2)}, u32[]{:S(2)}) collective-permute-start(f32[2,4,8,640]{3,2,1,0:T(8,128)S(1)} %get-tuple-element.87.side0_ref), channel_id=1, source_target_pairs={{0,2},{1,3},{2,0},{3,1},{4,6},{5,7},{6,4},{7,5},{8,10},{9,11},{10,... | collective-permute-start | bytes 491528 | tf_op jit(solution)/shard_map/ppermute | solution.py:417
  84.7 12.8 %collective-permute-start.17 = (f32[2,4,8,640]{3,2,1,0:T(8,128)S(1)}, f32[2,4,8,640]{3,2,1,0:T(8,128)S(1)}, u32[]{:S(2)}, u32[]{:S(2)}) collective-permute-start(f32[2,4,8,640]{3,2,1,0:T(8,128)S(1)} %get-tuple-element.88.side1_ref), channel_id=1, source_target_pairs={{2,4},{3,5},{4,2},{5,3},{10,12},{11,13},{12,10},{13,11},{18,20},{1... | collective-permute-start | bytes 491528 | tf_op jit(solution)/shard_map/ppermute | solution.py:417
  103.2 12.1 %collective-permute-start.18 = (f32[2,4,8,640]{3,2,1,0:T(8,128)S(1)}, f32[2,4,8,640]{3,2,1,0:T(8,128)S(1)}, u32[]{:S(2)}, u32[]{:S(2)}) collective-permute-start(f32[2,4,8,640]{3,2,1,0:T(8,128)S(1)} %get-tuple-element.91.side0_ref), channel_id=1, source_target_pairs={{0,2},{1,3},{2,0},{3,1},{4,6},{5,7},{6,4},{7,5},{8,10},{9,11},{10,... | collective-permute-start | bytes 491528 | tf_op jit(solution)/shard_map/ppermute | solution.py:417
  103.3 12.1 %collective-permute-start.19 = (f32[2,4,8,640]{3,2,1,0:T(8,128)S(1)}, f32[2,4,8,640]{3,2,1,0:T(8,128)S(1)}, u32[]{:S(2)}, u32[]{:S(2)}) collective-permute-start(f32[2,4,8,640]{3,2,1,0:T(8,128)S(1)} %get-tuple-element.92.side1_ref), channel_id=1, source_target_pairs={{2,4},{3,5},{4,2},{5,3},{10,12},{11,13},{12,10},{13,11},{18,20},{1... | collective-permute-start | bytes 491528 | tf_op jit(solution)/shard_map/ppermute | solution.py:417
  119.1 8.4 %collective-permute-start.20 = (f32[16,8,512]{2,1,0:T(8,128)S(1)}, f32[16,8,512]{2,1,0:T(8,128)S(1)}, u32[]{:S(2)}, u32[]{:S(2)}) collective-permute-start(f32[16,8,512]{2,1,0:T(8,128)S(1)} %get-tuple-element.96), channel_id=1, source_target_pairs={{0,1},{1,0},{2,3},{3,2},{4,5},{5,4},{6,7},{7,6},{8,9},{9,8},{10,11... | collective-permute-start | bytes 786440 | tf_op jit(solution)/shard_map/ppermute | solution.py:405
  120.7 9.0 %collective-permute-start.21 = (f32[16,8,512]{2,1,0:T(8,128)S(1)}, f32[16,8,512]{2,1,0:T(8,128)S(1)}, u32[]{:S(2)}, u32[]{:S(2)}) collective-permute-start(f32[16,8,512]{2,1,0:T(8,128)S(1)} %get-tuple-element.97), channel_id=1, source_target_pairs={{0,16},{1,17},{2,18},{3,19},{4,20},{5,21},{6,22},{7,23},{8,24},{9,... | collective-permute-start | bytes 786440 | tf_op jit(solution)/shard_map/ppermute | solution.py:405
  122.2 10.3 %collective-permute-start.22 = (f32[16,8,512]{2,1,0:T(8,128)S(1)}, f32[16,8,512]{2,1,0:T(8,128)S(1)}, u32[]{:S(2)}, u32[]{:S(2)}) collective-permute-start(f32[16,8,512]{2,1,0:T(8,128)S(1)} %get-tuple-element.98), channel_id=1, source_target_pairs={{0,17},{1,16},{2,19},{3,18},{4,21},{5,20},{6,23},{7,22},{8,25},{9,... | collective-permute-start | bytes 786440 | tf_op jit(solution)/shard_map/ppermute | solution.py:405
where the time goes:
time: 135 us; the launch traced here: 134 us
  Pallas kernels  62.3 us (46%)
  waiting for transfers between devices  36.7 us (27%)
  starting transfers between devices  30 us (22%)
  local copies, waits for them, and re-layouts  4.13 us (3%)
    pallas_call x17, Pallas kernels, call(): pl.pallas_call(body, grid=grid, out_shape=outs, in_specs=in_specs, out_sp...  62.3 us
    ppermute x15, waiting for transfers between devices, swap(): return lax.ppermute(value, axes, route(frame_bits, slab_bits))  35.2 us
    ppermute x15, starting transfers between devices, swap(): return lax.ppermute(value, axes, route(frame_bits, slab_bits))  16.3 us
    ppermute x4, starting transfers between devices, halo(): lax.ppermute(side1, 'space', second)  12.7 us
    unnamed x12, local copies, waits for them, and re-layouts  4.13 us
  transfers between devices with their start and end apart: 23, of which 11 were waited for; matrix products, arithmetic and copies ran while one was open for 0% of the time, Pallas kernels for 24%

commit v1 on v0

v1 whole, which is shorter than its diff:
```python
import functools

import jax
import jax.numpy as jnp
from jax import lax
from jax.experimental import pallas as pl
from jax.experimental.pallas import tpu as pltpu
from jax.sharding import PartitionSpec as P

BAND = 4
SECTIONS = 4
SWEEPS = 4
REACH = 6

depth_rate = 0.4
plane_rate = 0.05
root_half = 0.7071067811865476

LANES = 128
SPARE = 64
EDGE = SWEEPS
GROUP = 12
VMEM = pltpu.VMEM
SMEM = pltpu.SMEM


def cells(value):
    return [value[:, i : i + LANES] for i in range(0, value.shape[1], LANES)]


def joined(parts):
    return jnp.concatenate(parts, axis=1)


def lane_ids():
    return lax.broadcasted_iota(jnp.int32, (8, LANES), 1)


def quotient(change):
    return change / (1.0 + change * change)


def moved_right(parts, amount, first):
    turned = [pltpu.roll(part, amount, 1) for part in parts]
    own = lane_ids() >= amount
    ahead = [first] + turned[:-1]
    return [jnp.where(own, a, b) for a, b in zip(turned, ahead)]


def moved_left(parts, amount):
    turned = [pltpu.roll(part, (LANES - amount) % LANES, 1) for part in parts]
    own = lane_ids() < LANES - amount
    return [jnp.where(own, a, b) for a, b in zip(turned, turned[1:])]


def warped_plane(field, coeff_rows, offset):
    width = field.shape[1]
    total = None
    for band_index in range(BAND):
        shifted = pltpu.roll(field, (width + BAND // 2 - band_index - offset) % width, 1)
        term = jnp.broadcast_to(coeff_rows[band_index], shifted.shape) * shifted
        total = term if total is None else total + term
    return total


def haar(own, warped, sign, level, scale):
    value = (own + sign * warped) * scale
    return value - jnp.clip(value, -level, level)


class Sweep:
    def __init__(self, width, edge_first, edge_last, last_lane):
        rows = lax.broadcasted_iota(jnp.int32, (8, width), 0)
        self.inner_rows = rows < 7
        lanes = lane_ids()
        self.first = jnp.where(lanes == SPARE - 1, edge_first, 1.0)
        self.last = jnp.where(lanes == last_lane % LANES, edge_last, 1.0)
        self.last_part = last_lane // LANES

    def depth(self, low, high):
        return quotient(high - low)

    def plane(self, value, flux_below, flux_above):
        width = value.shape[1]
        change = jnp.where(self.inner_rows, pltpu.roll(value, 7, 0) - value, 0.0)
        flux_y = quotient(change)
        change = cells(pltpu.roll(value, width - 1, 1) - value)
        change[0] = change[0] * self.first
        change[self.last_part] = change[self.last_part] * self.last
        flux_x = quotient(joined(change))
        gain = (flux_y - pltpu.roll(flux_y, 1, 0)) + (flux_x - pltpu.roll(flux_x, 1, 1))
        return value + (plane_rate * gain + depth_rate * (flux_above - flux_below))


class Place:
    def __init__(self):
        self.tm = lax.axis_index("tm")
        self.space = lax.axis_index("space")
        self.pairs = lax.axis_size("space") // 2
        self.far = (self.tm // 2) % 2
        self.slab = self.space % 2
        self.chunk = 2 * self.far + self.slab
        self.pair = self.space // 2
        self.odd = self.pair % 2

    def lower(self, slot, bit):
        value = (self.tm // (1 << bit)) % 2
        if bit == 1 and slot == 1:
            value = 1 - value
        return value == 0

    def signs(self, slot, bit, level):
        is_lower = self.lower(slot, bit)
        sign = jnp.where(is_lower, 1.0, -1.0).astype(jnp.float32)
        return sign, jnp.where(is_lower, 0.0, 0.5 * level).astype(jnp.float32)

    def sweep(self, width):
        first = jnp.where(self.chunk == 0, 0.0, 1.0).astype(jnp.float32)
        last = jnp.where(self.chunk == 3, 0.0, 1.0).astype(jnp.float32)
        return Sweep(width, first, last, width - SPARE - 1)

    def spot(self, side, distance, planes):
        is_top = self.odd == side
        return jnp.where(is_top, planes - 1 - distance, distance)

    def open_face(self, side):
        if side == 0:
            return jnp.float32(1.0)
        closed = (self.pair == 0) | (self.pair == self.pairs - 1)
        return jnp.where(closed, 0.0, 1.0).astype(jnp.float32)


def call(body, outs, *args, spaces=None, scratch=(), micros=1.0, smem_outs=(), aliases=None, room=40):
    spaces = spaces or {}
    in_specs = [pl.BlockSpec(memory_space=spaces.get(i, VMEM)) for i in range(len(args))]
    out_specs = [pl.BlockSpec(memory_space=SMEM if i in smem_outs else VMEM) for i in range(len(outs))]
    moved = sum(a.size * 4 for a in args) + sum(o.size * 4 for o in outs)
    return pl.pallas_call(
        body,
        out_shape=outs,
        in_specs=in_specs,
        out_specs=out_specs,
        scratch_shapes=list(scratch),
        input_output_aliases=aliases or {},
        compiler_params=pltpu.CompilerParams(vmem_limit_bytes=room << 20),
        cost_estimate=pl.CostEstimate(flops=int(micros * 1.1e9), bytes_accessed=int(moved), transcendentals=0),
    )(*args)


def f32(*shape):
    return jax.ShapeDtypeStruct(shape, jnp.float32)


def fetch(copies, sems):
    started = [pltpu.make_async_copy(a, b, sems.at[i]) for i, (a, b) in enumerate(copies)]
    for copy in started:
        copy.start()
    return started


def pack_section(place, coeff_ref, offset, whole, outs):
    planes, width = coeff_ref.shape[1:]
    step = width // 4
    zero = jnp.zeros((8, LANES), jnp.float32)
    lanes = lane_ids()
    for k in range(BAND):
        for z in range(0, planes, 8):
            value = coeff_ref[k, z : z + 8, :]
            whole[k, z : z + 8] = joined(moved_right(cells(value) + [zero], SPARE, zero))
    for number, out_ref in enumerate(outs):
        start = pl.multiple_of((place.chunk ^ number) * step, LANES)
        out_ref[...] = whole[:, :, pl.ds(start, step + LANES)]
        out_ref[0, 0:8, 0:LANES] = jnp.where(lanes == 0, offset.astype(jnp.float32), out_ref[0, 0:8, 0:LANES])


def intake_kernel(coeff_hbm, offset_ref, coeff_ref, *refs):
    out_refs, (later, whole, sems) = refs[:4], refs[4:]
    now_copy, later_copy = fetch([(coeff_hbm.at[0, 0], coeff_ref), (coeff_hbm.at[0, 1], later)], sems)
    later_copy.wait()
    pack_section(Place(), later, offset_ref[0, 0, 1], whole, [ref.at[0] for ref in out_refs])
    now_copy.wait()


def coeff_kernel(first, count, coeff_hbm, offset_ref, *refs):
    out_refs, (sections, whole, sems) = refs[:4], refs[4:]
    copies = fetch([(coeff_hbm.at[0, first + i], sections.at[i]) for i in range(count)], sems)
    for i in range(count):
        copies[i].wait()
        pack_section(Place(), sections.at[i], offset_ref[0, 0, first + i], whole, [ref.at[i] for ref in out_refs])


def first_kernel(own_ref, partner_ref, coeff_ref, offset_ref, level_ref, *refs):
    out_refs, whole = refs[:4], refs[4]
    planes, _, width = own_ref.shape
    place = Place()
    sign, level = place.signs(0, 0, level_ref[0])
    offset = offset_ref[0, 0, 0]
    step = width // 4
    zero = jnp.zeros((8, LANES), jnp.float32)
    no_rows = jnp.zeros((1, LANES), jnp.float32)

    def body(z, carry):
        field = joined([partner_ref[z], zero])
        width = field.shape[1]
        shifted = pltpu.roll(field, (width + BAND // 2 - offset) % width, 1)
        warped = None
        for k in range(BAND):
            row = joined([coeff_ref[k, pl.ds(z, 1), :], no_rows])
            term = jnp.broadcast_to(row, shifted.shape) * (pltpu.roll(shifted, width - k, 1) if k else shifted)
            warped = term if warped is None else warped + term
        value = haar(joined([own_ref[z], zero]), warped, sign, level, 0.5 * root_half)
        whole[z] = pltpu.roll(value, SPARE, 1)
        return carry

    lax.fori_loop(0, planes, body, 0, unroll=2)
    for number, out_ref in enumerate(out_refs):
        start = pl.multiple_of((place.chunk ^ number) * step, LANES)
        out_ref[...] = whole[:, :, pl.ds(start, step + LANES)]


def gather_coeff_kernel(self_ref, near_ref, far_ref, across_ref, out_ref, offset_ref):
    place = Place()
    sections = self_ref.shape[0]
    for number, ref in enumerate((self_ref, near_ref, far_ref, across_ref)):
        slot = number // 2
        slab = place.slab ^ (number % 2)
        for section in range(sections):
            out_ref[section, slot, slab] = ref[section]
            corner = ref[section, 0, 0:8, 0:LANES]
            offset = jnp.max(jnp.where(lane_ids() == 0, corner, -100.0))
            offset_ref[section, slot, slab] = offset.astype(jnp.int32)


def start_kernel(self_ref, near_ref, far_ref, across_ref, side0_ref, side1_ref):
    place = Place()
    half = self_ref.shape[0]
    for side, out_ref in enumerate((side0_ref, side1_ref)):
        is_top = place.odd == side
        slab = jnp.where(is_top, 1, 0)
        for own_slab in (True, False):
            pieces = (self_ref, far_ref) if own_slab else (near_ref, across_ref)

            @pl.when((slab == place.slab) == own_slab)
            def _():
                for slot, piece in enumerate(pieces):
                    for e in range(EDGE):
                        out_ref[slot, e] = piece[jnp.where(is_top, half - 1 - e, e)]


def trapezoid(place, load, planes, emit, saved_ref, one, two, slots=(0, 1)):
    width = one.shape[-1]
    sweep = place.sweep(width)
    size = GROUP // len(slots)
    for level in range(1, SWEEPS + 1):
        def source(slot, p, level=level):
            if level == 1:
                return load(slot, p)
            return (one, two)[level % 2][slot, p]

        def put(slot, p, value, level=level):
            if level == SWEEPS:
                emit(slot, p - EDGE, value)
            else:
                (two, one)[level % 2][slot, p] = value

        carry = []
        for slot in slots:
            low, here = source(slot, level - 1), source(slot, level)
            carry += [here, sweep.depth(low, here)]

        def body(i, carry):
            return step(i, carry, size)

        def step(i, carry, group):
            new = []
            for slot in slots:
                at = 2 * slots.index(slot)
                here, below = carry[at : at + 2]
                for j in range(group):
                    p = level + size * i + j
                    high = source(slot, p + 1)
                    above = sweep.depth(here, high)
                    put(slot, p, sweep.plane(here, below, above))
                    here, below = high, above
                new += [here, below]
            return new

        count = planes - 2 * level
        carry = lax.fori_loop(0, count // size, body, carry)
        if count % size:
            step(count // size, carry, count % size)
        if level < SWEEPS:
            kept = (two, one)[level % 2]
            for slot in slots:
                for side in range(2):
                    for j in range(2):
                        spot = place.spot(side, level + j, planes)
                        saved_ref[side, slot % saved_ref.shape[1], level - 1, j] = kept[slot, spot]


def inner_first_kernel(slot, own_ref, other_ref, *refs):
    out_ref, saved_ref, state, one, two = refs[-5:]
    place = Place()
    half = own_ref.shape[0]
    state[slot, pl.ds(place.slab * half, half)] = own_ref[...]
    state[slot, pl.ds((1 - place.slab) * half, half)] = other_ref[...]

    def emit(slot, i, value):
        out_ref[slot, i] = value

    trapezoid(place, lambda slot, p: state[slot, p], 2 * half, emit, saved_ref, one, two, (slot,))


def finished(value):
    return 2.0 * joined(moved_left(cells(value), SPARE)[: (value.shape[1] - 2 * SPARE) // LANES])


def inner_haar(place, section, bit, slots, own_ref, partner_ref, sides, coeff_ref, offset_ref, level_ref, zero_level):
    inner = own_ref.shape[1]
    planes = inner + 2 * EDGE
    half = planes // 2
    group = 0 if section == 1 else section - 2
    for slot in slots:
        for side, ref in enumerate(sides):
            for e in range(EDGE):
                zero_level[slot, place.spot(side, e, planes)] = ref[slot, e]
    for slot in slots:
        sign, level = place.signs(slot, bit, level_ref[section])
        other = 1 - slot if bit == 1 else slot
        for slab in range(2):
            offset = offset_ref[group, slot, slab]
            start, stop = (EDGE, half) if slab == 0 else (half, planes - EDGE)
            for p in range(start, stop):
                rows = [coeff_ref[group, slot, slab, k, pl.ds(p - slab * half, 1), :] for k in range(BAND)]
                warped = warped_plane(partner_ref[other, p - EDGE], rows, offset)
                zero_level[slot, p] = haar(own_ref[slot, p - EDGE], warped, sign, level, root_half)


def inner_kernel(section, bit, own_ref, partner_ref, side0_ref, side1_ref, coeff_ref, offset_ref, level_ref,
                 out_ref, saved_ref, zero_level, one, two):
    place = Place()
    planes = own_ref.shape[1] + 2 * EDGE
    sides = (side0_ref, side1_ref)
    inner_haar(place, section, bit, (0, 1), own_ref, partner_ref, sides, coeff_ref, offset_ref, level_ref, zero_level)

    def emit(slot, i, value):
        out_ref[slot, i] = value

    trapezoid(place, lambda slot, p: zero_level[slot, p], planes, emit, saved_ref, one, two)


def inner_last_kernel(section, bit, slot, own_ref, partner_ref, side0_ref, side1_ref, coeff_ref, offset_ref, level_ref,
                      mine_ref, other_ref, saved_ref, zero_level, one, two, done):
    place = Place()
    planes = own_ref.shape[1] + 2 * EDGE
    sides = (side0_ref, side1_ref)
    inner_haar(place, section, bit, (slot,), own_ref, partner_ref, sides, coeff_ref, offset_ref, level_ref, zero_level)

    def emit(slot, i, value):
        done[i] = finished(value)

    trapezoid(place, lambda slot, p: zero_level[slot, p], planes, emit, saved_ref, one, two, (slot,))
    count = mine_ref.shape[0]
    mine_ref[...] = done[pl.ds(place.slab * count, count)]
    other_ref[...] = done[pl.ds((1 - place.slab) * count, count)]


def wedge(place, sweep, side, edge_ref, halo_ref, saved):
    open_face = place.open_face(side)
    values = [
        [halo_ref[slot, h] for h in (3, 2, 1, 0)] + [edge_ref[slot, 0], edge_ref[slot, 1]] for slot in range(2)
    ]
    for level in range(1, SWEEPS + 1):
        for slot in range(2):
            here = values[slot]
            fluxes = [sweep.depth(a, b) for a, b in zip(here[:-1], here[1:])]
            fluxes[EDGE - level] = fluxes[EDGE - level] * open_face
            here = [sweep.plane(here[i], fluxes[i - 1], fluxes[i]) for i in range(1, 5)]
            if level < SWEEPS:
                here += [saved(side, slot, level - 1, j) for j in range(2)]
            values[slot] = here
    return values


def wedge_kernel(side0_ref, side1_ref, halo0_ref, halo1_ref, saved_ref, out_ref):
    place = Place()
    sweep = place.sweep(side0_ref.shape[-1])
    for side, (edge, halo) in enumerate(((side0_ref, halo0_ref), (side1_ref, halo1_ref))):
        values = wedge(place, sweep, side, edge, halo, lambda *at: saved_ref[at])
        for slot in range(2):
            for e in range(EDGE):
                out_ref[side, slot, e] = values[slot][e]


def haar_kernel(section, bit, own_ref, partner_ref, coeff_ref, offset_ref, level_ref, out0_ref, out1_ref):
    place = Place()
    outs = (out0_ref, out1_ref)
    half = coeff_ref.shape[4]
    group = 0 if section == 1 else section - 2
    planes = 2 * half
    for slot in range(2):
        sign, level = place.signs(slot, bit, level_ref[section])
        other = 1 - slot if bit == 1 else slot
        for side in range(2):
            slab = jnp.where(place.odd == side, 1, 0)
            offset = offset_ref[group, slot, slab]
            for e in range(EDGE):
                z = place.spot(side, e, planes) - slab * half
                rows = [coeff_ref[group, slot, slab, k, pl.ds(z, 1), :] for k in range(BAND)]
                warped = warped_plane(partner_ref[side, other, e], rows, offset)
                outs[side][slot, e] = haar(own_ref[side, slot, e], warped, sign, level, root_half)


def wedge_last_kernel(side0_ref, side1_ref, halo0_ref, halo1_ref, saved0_ref, saved1_ref, *refs):
    out_refs, done = refs[:4], refs[4]
    place = Place()
    sweep = place.sweep(side0_ref.shape[-1])
    saved_refs = (saved0_ref, saved1_ref)

    def saved(side, slot, level, j):
        return saved_refs[slot][side, 0, level, j]

    for side, (edge, halo) in enumerate(((side0_ref, halo0_ref), (side1_ref, halo1_ref))):
        values = wedge(place, sweep, side, edge, halo, saved)
        for slot in range(2):
            for e in range(EDGE):
                done[side, slot, e] = finished(values[slot][e])
    for number, out_ref in enumerate(out_refs):
        slab = place.slab ^ (number % 2)
        side = jnp.where(slab == 1, place.odd, 1 - place.odd)
        out_ref[...] = done[side, number // 2]


def output_kernel(*refs):
    inner_refs, edge_refs, out_ref = refs[:4], refs[4:8], refs[8]
    place = Place()
    half = out_ref.shape[0]
    inner, _, step = inner_refs[0].shape
    for number in range(4):
        lanes = pl.ds(pl.multiple_of((place.chunk ^ number) * step, LANES), step)
        out_ref[pl.ds((1 - place.slab) * EDGE, inner), :, lanes] = inner_refs[number][...]
        for e in range(EDGE):
            out_ref[jnp.where(place.slab == 1, half - 1 - e, e), :, lanes] = edge_refs[number][e]


def on_device(volume, warp_coef, offsets, thresholds):
    frames, slabs = lax.axis_size("tm"), lax.axis_size("space")
    levels = frames.bit_length() - 1
    pairs = slabs // 2
    _, half, rows, length = volume.shape
    planes = 2 * half
    inner = planes - 2 * EDGE
    width = length // 4 + 2 * SPARE
    axes = ("tm", "space")

    def route(frame_bits, slab_bits):
        return [(f * slabs + s, (f ^ frame_bits) * slabs + (s ^ slab_bits)) for f in range(frames) for s in range(slabs)]

    def swap(value, frame_bits, slab_bits=0):
        return lax.ppermute(value, axes, route(frame_bits, slab_bits))

    def spread(pieces):
        return (pieces[0], swap(pieces[1], 0, 1), swap(pieces[2], 2, 0), swap(pieces[3], 2, 1))

    def halo(side0, side1):
        first = [(s, s ^ 2) for s in range(slabs)]
        second = []
        for s in range(slabs):
            pair = s // 2 + 1 if (s // 2) % 2 else s // 2 - 1
            if 0 <= pair < pairs:
                second.append((s, 2 * pair + s % 2))
        return lax.ppermute(side0, "space", first), lax.ppermute(side1, "space", second)

    side_shape = f32(2, EDGE, rows, width)
    inner_shape = f32(2, inner, rows, width)
    saved_shape = f32(2, 2, SWEEPS - 1, 2, rows, width)
    edges_shape = f32(2, 2, EDGE, rows, width)
    level_scratch = pltpu.VMEM((2, planes, rows, width), jnp.float32)
    packed = pltpu.VMEM((BAND, half, length + LANES), jnp.float32)

    def coeff_state(pieces, count):
        return call(
            gather_coeff_kernel,
            [f32(count, 2, 2, BAND, half, width), jax.ShapeDtypeStruct((count, 2, 2), jnp.int32)],
            *pieces, smem_outs=(1,), micros=0.8,
        )

    received = swap(volume[0], 1)
    first_coeff, *early = call(
        intake_kernel, [f32(BAND, half, length)] + [f32(1, BAND, half, width)] * 4, warp_coef, offsets,
        spaces={0: pltpu.HBM, 1: SMEM}, micros=1.2,
        scratch=[pltpu.VMEM((BAND, half, length), jnp.float32), packed, pltpu.SemaphoreType.DMA((2,))],
    )
    early = spread(early)
    late_count = SECTIONS - 2
    pieces = call(
        first_kernel, [f32(half, rows, width)] * 4, volume[0], received, first_coeff, offsets, thresholds,
        spaces={3: SMEM, 4: SMEM}, micros=4.0, scratch=[pltpu.VMEM((half, rows, length + LANES), jnp.float32)],
    )
    pieces, early = lax.optimization_barrier((pieces, early))
    late = call(
        functools.partial(coeff_kernel, 2, late_count), [f32(late_count, BAND, half, width)] * 4, warp_coef, offsets,
        spaces={0: pltpu.HBM, 1: SMEM}, micros=1.5,
        scratch=[
            pltpu.VMEM((late_count, BAND, half, length), jnp.float32), packed, pltpu.SemaphoreType.DMA((late_count,)),
        ],
    )
    mine, near, far = pieces[0], swap(pieces[1], 0, 1), swap(pieces[2], 2, 0)
    last, near, far = lax.optimization_barrier((pieces[3], near, far))
    across = swap(last, 2, 1)
    own, saved = call(
        functools.partial(inner_first_kernel, 0), [inner_shape, saved_shape], mine, near,
        scratch=[level_scratch] * 3, micros=3.5,
    )
    across, own = lax.optimization_barrier((across, own))
    side0, side1 = call(start_kernel, [side_shape, side_shape], mine, near, far, across, micros=0.2)
    late, side0 = lax.optimization_barrier((late, side0))
    halo0, halo1 = halo(side0, side1)
    own, saved = call(
        functools.partial(inner_first_kernel, 1), [inner_shape, saved_shape], far, across, own, saved,
        scratch=[level_scratch] * 3, micros=3.5, aliases={2: 0, 3: 1},
    )
    late = spread(late)
    coeff, shift = coeff_state(early, 1)
    for section in range(1, SECTIONS):
        bit = section % levels
        (edges,) = call(wedge_kernel, [edges_shape], side0, side1, halo0, halo1, saved, micros=2.4)
        partner, partner_edges = own, edges
        if bit != 1:
            partner, edges = lax.optimization_barrier((own, edges))
            partner, partner_edges = swap(partner, 1 << bit), swap(edges, 1 << bit)
        side0, side1 = call(
            functools.partial(haar_kernel, section, bit), [side_shape, side_shape],
            edges, partner_edges, coeff, shift, thresholds, spaces={3: SMEM, 4: SMEM}, micros=1.1,
        )
        used = coeff, shift
        if section == 1:
            late, side0, side1 = lax.optimization_barrier((late, side0, side1))
            coeff, shift = coeff_state(late, late_count)
        halo0, halo1 = halo(side0, side1)
        if section == SECTIONS - 1:
            break
        own, saved = call(
            functools.partial(inner_kernel, section, bit), [inner_shape, saved_shape],
            own, partner, side0, side1, *used, thresholds,
            spaces={5: SMEM, 6: SMEM}, scratch=[level_scratch] * 3, micros=8.0,
        )
    piece_shape = f32(half - EDGE, rows, length // 4)
    edge_shape = f32(EDGE, rows, length // 4)
    slot_saved = f32(2, 1, SWEEPS - 1, 2, rows, width)

    def last_inner(slot):
        return call(
            functools.partial(inner_last_kernel, section, bit, slot), [piece_shape, piece_shape, slot_saved],
            own, partner, side0, side1, *used, thresholds, spaces={5: SMEM, 6: SMEM}, micros=4.2,
            scratch=[level_scratch] * 3 + [pltpu.VMEM((inner, rows, length // 4), jnp.float32)],
        )

    far, across, saved1 = last_inner(1)
    across = swap(across, 2, 1)
    mine, near, saved0 = last_inner(0)
    across, halo0 = lax.optimization_barrier((across, halo0))
    inners = (mine, swap(near, 0, 1), swap(far, 2, 0), across)
    edges = call(
        wedge_last_kernel, [edge_shape] * 4, side0, side1, halo0, halo1, saved0, saved1, micros=2.5,
        scratch=[pltpu.VMEM((2, 2, EDGE, rows, length // 4), jnp.float32)],
    )
    (out,) = call(output_kernel, [f32(half, rows, length)], *inners, *spread(edges), micros=1.0)
    return out[None]


def solution(mesh):
    return jax.shard_map(
        on_device,
        mesh=mesh,
        in_specs=(
            P("tm", "space", None, None),
            P("tm", None, None, "space", None),
            P("tm", "space", None),
            P(),
        ),
        out_specs=P("tm", "space", None, None),
        check_vma=False,
    )
```

time: 135 us -> 108 us (0.80); the launches traced: 134 us -> 108 us
  waiting for transfers between devices: 36.7 us -> 19.5 us
  Pallas kernels: 62.3 us -> 50.3 us
  starting transfers between devices: 30 us -> 35.8 us
  local copies, waits for them, and re-layouts: 4.13 us -> 2.26 us
    ppermute x15 -> x18, waiting for transfers between devices: 35.2 us -> 19.3 us  [swap(): return lax.ppermute(value, axes, route(frame_bits, slab_bits))]
    pallas_call x17 -> x20, Pallas kernels: 62.3 us -> 50.3 us  [call(): pl.pallas_call(body, out_shape=outs, in_specs=in_specs, out_specs=out_spe...]
    ppermute x15 -> x18, starting transfers between devices: 16.3 us -> 19.3 us  [swap(): return lax.ppermute(value, axes, route(frame_bits, slab_bits))]
    ppermute x4, starting transfers between devices: 12.7 us -> 14.7 us  [halo(): lax.ppermute(side1, 'space', second)]
    unnamed x12 -> x10, local copies, waits for them, and re-layouts: 4.13 us -> 2.26 us
    ppermute x4, waiting for transfers between devices: 1.53 us -> 0.01 us  [halo(): lax.ppermute(side0, 'space', first)]
  transfers between devices with their start and end apart: 23 -> 26, of which waited for: 11 -> 12; matrix products, arithmetic and copies ran while one was open for 0% -> 0% of each run, Pallas kernels for 24% -> 41%
where the time goes in v1:
time: 108 us
  Pallas kernels  50.3 us (47%)
  starting transfers between devices  35.8 us (33%)
  waiting for transfers between devices  19.5 us (18%)
  local copies, waits for them, and re-layouts  2.26 us (2%)
    pallas_call x20, Pallas kernels, call(): pl.pallas_call(body, out_shape=outs, in_specs=in_specs, out_specs=out_spe...  50.3 us
    ppermute x18, waiting for transfers between devices, swap(): return lax.ppermute(value, axes, route(frame_bits, slab_bits))  19.3 us
    ppermute x18, starting transfers between devices, swap(): return lax.ppermute(value, axes, route(frame_bits, slab_bits))  19.3 us
    ppermute x4, starting transfers between devices, halo(): lax.ppermute(side1, 'space', second)  14.7 us
    unnamed x10, local copies, waits for them, and re-layouts  2.26 us
  transfers between devices with their start and end apart: 26, of which 12 were waited for; matrix products, arithmetic and copies ran while one was open for 0% of the time, Pallas kernels for 41%

profile of v1, /device:TPU:8, one launch (start us, length us, event | category | flops | bytes accessed | tf_op | source)
XLA Modules:
  0.0 108.2 jit_solution(13343866282601697776)
XLA Ops:
  0.0 1.6 %copy-done = f32[1,4,4,16,2048]{4,3,2,1,0:T(8,128)S(1)} copy-done((f32[1,4,4,16,2048]{4,3,2,1,0:T(8,128)S(1)}, f32[1,4,4,16,2048]{4,3,2,1,0:T(8,128)}, u32[]{:S(2)}) %copy-start) | copy-done | bytes 2097176
  1.6 0.7 copy-done.3
  2.3 0.9 shard_map.46
  3.1 1.6 %collective-permute-start.1 = (f32[1,4,16,640]{3,2,1,0:T(8,128)S(1)}, f32[1,4,16,640]{3,2,1,0:T(8,128)S(1)}, u32[]{:S(2)}, u32[]{:S(2)}) collective-permute-start(f32[1,4,16,640]{3,2,1,0:T(8,128)S(1)} %get-tuple-element.82), channel_id=1, source_target_pairs={{0,1},{1,0},{2,3},{3,2},{4,5},{5,4},{6,7},{7,6},{8,9},{9,8},{10,11... | collective-permute-start | bytes 491528 | tf_op jit(solution)/shard_map/ppermute | solution.py:460
  4.7 1.5 %collective-permute-start.2 = (f32[1,4,16,640]{3,2,1,0:T(8,128)S(1)}, f32[1,4,16,640]{3,2,1,0:T(8,128)S(1)}, u32[]{:S(2)}, u32[]{:S(2)}) collective-permute-start(f32[1,4,16,640]{3,2,1,0:T(8,128)S(1)} %get-tuple-element.83), channel_id=1, source_target_pairs={{0,16},{1,17},{2,18},{3,19},{4,20},{5,21},{6,22},{7,23},{8,24},{9,... | collective-permute-start | bytes 491528 | tf_op jit(solution)/shard_map/ppermute | solution.py:460
  6.2 0.5 collective-permute-start.3
  6.7 0.0 copy-start.1
  6.7 3.6 %shard_map.47 = (f32[16,8,640]{2,1,0:T(8,128)S(1)}, f32[16,8,640]{2,1,0:T(8,128)S(1)}, f32[16,8,640]{2,1,0:T(8,128)S(1)}, f32[16,8,640]{2,1,0:T(8,128)S(1)}) custom-call(f32[16,8,2048]{2,1,0:T(8,128)S(1)} %bitcast.3, f32[16,8,2048]{2,1,0:T(8,128)S(1)} %collective-permute-done.partner_ref, f32[4,16,2048]{2,1,0:T(8,128)S(1)} %get-tuple-element.76.coeff_ref, ...), custom_call_target="tpu_custom_call" | custom-call | flops 4400000000 | bytes 3932192 | tf_op jit(solution)/shard_map/pallas_call | solution.py:138
  10.3 1.5 %collective-permute-done.2.far_ref = f32[1,4,16,640]{3,2,1,0:T(8,128)S(1)} collective-permute-done((f32[1,4,16,640]{3,2,1,0:T(8,128)S(1)}, f32[1,4,16,640]{3,2,1,0:T(8,128)S(1)}, u32[]{:S(2)}, u32[]{:S(2)}) %collective-permute-start.2) | collective-permute-done | bytes 163872 | tf_op jit(solution)/shard_map/ppermute | solution.py:460
  11.8 2.8 %collective-permute-done.3.across_ref = f32[1,4,16,640]{3,2,1,0:T(8,128)S(1)} collective-permute-done((f32[1,4,16,640]{3,2,1,0:T(8,128)S(1)}, f32[1,4,16,640]{3,2,1,0:T(8,128)S(1)}, u32[]{:S(2)}, u32[]{:S(2)}) %collective-permute-start.3) | collective-permute-done | bytes 163872 | tf_op jit(solution)/shard_map/ppermute | solution.py:460
  14.5 1.5 %collective-permute-start.4 = (f32[16,8,640]{2,1,0:T(8,128)S(1)}, f32[16,8,640]{2,1,0:T(8,128)S(1)}, u32[]{:S(2)}, u32[]{:S(2)}) collective-permute-start(f32[16,8,640]{2,1,0:T(8,128)S(1)} %get-tuple-element.86), channel_id=1, source_target_pairs={{0,1},{1,0},{2,3},{3,2},{4,5},{5,4},{6,7},{7,6},{8,9},{9,8},{10,11... | collective-permute-start | bytes 983048 | tf_op jit(solution)/shard_map/ppermute | solution.py:460
  16.0 1.5 %collective-permute-start.5 = (f32[16,8,640]{2,1,0:T(8,128)S(1)}, f32[16,8,640]{2,1,0:T(8,128)S(1)}, u32[]{:S(2)}, u32[]{:S(2)}) collective-permute-start(f32[16,8,640]{2,1,0:T(8,128)S(1)} %get-tuple-element.87), channel_id=1, source_target_pairs={{0,16},{1,17},{2,18},{3,19},{4,20},{5,21},{6,22},{7,23},{8,24},{9,... | collective-permute-start | bytes 983048 | tf_op jit(solution)/shard_map/ppermute | solution.py:460
  17.5 1.1 %shard_map.50 = (f32[2,4,16,640]{3,2,1,0:T(8,128)S(1)}, f32[2,4,16,640]{3,2,1,0:T(8,128)S(1)}, f32[2,4,16,640]{3,2,1,0:T(8,128)S(1)}, f32[2,4,16,640]{3,2,1,0:T(8,128)S(1)}) custom-call(f32[1,4,4,16,2048]{4,3,2,1,0:T(8,128)S(1)} %copy-done.1, s32[1,1,4]{2,1,0:T(1,128)S(1)} %copy-done.3), custom_call_target="tpu_custom_call" | custom-call | flops 1650000000 | bytes 3407888 | tf_op jit(solution)/shard_map/pallas_call | solution.py:138
  18.7 0.7 shard_map.53
  19.4 4.1 %collective-permute-done.4.other_ref.near_ref = f32[16,8,640]{2,1,0:T(8,128)S(1)} collective-permute-done((f32[16,8,640]{2,1,0:T(8,128)S(1)}, f32[16,8,640]{2,1,0:T(8,128)S(1)}, u32[]{:S(2)}, u32[]{:S(2)}) %collective-permute-start.4) | collective-permute-done | bytes 327712 | tf_op jit(solution)/shard_map/ppermute | solution.py:460
  23.5 1.2 %collective-permute-done.5.own_ref.far_ref = f32[16,8,640]{2,1,0:T(8,128)S(1)} collective-permute-done((f32[16,8,640]{2,1,0:T(8,128)S(1)}, f32[16,8,640]{2,1,0:T(8,128)S(1)}, u32[]{:S(2)}, u32[]{:S(2)}) %collective-permute-start.5) | collective-permute-done | bytes 327712 | tf_op jit(solution)/shard_map/ppermute | solution.py:460
  24.8 1.4 %collective-permute-start.6 = (f32[16,8,640]{2,1,0:T(8,128)S(1)}, f32[16,8,640]{2,1,0:T(8,128)S(1)}, u32[]{:S(2)}, u32[]{:S(2)}) collective-permute-start(f32[16,8,640]{2,1,0:T(8,128)S(1)} %get-tuple-element.89), channel_id=1, source_target_pairs={{0,17},{1,16},{2,19},{3,18},{4,21},{5,20},{6,23},{7,22},{8,25},{9,... | collective-permute-start | bytes 983048 | tf_op jit(solution)/shard_map/ppermute | solution.py:460
  26.2 3.1 %shard_map.48 = (f32[2,24,8,640]{3,2,1,0:T(8,128)S(1)}, f32[2,2,3,2,8,640]{5,4,3,2,1,0:T(8,128)S(1)}) custom-call(f32[16,8,640]{2,1,0:T(8,128)S(1)} %get-tuple-element.90.own_ref.self_ref, f32[16,8,640]{2,1,0:T(8,128)S(1)} %collective-permute-done.4.other_ref.near_ref), custom_call_target="tpu_custom_call" | custom-call | flops 3849999872 | bytes 2129920 | tf_op jit(solution)/shard_map/pallas_call | solution.py:138
  29.3 4.2 %collective-permute-done.6.other_ref.across_ref = f32[16,8,640]{2,1,0:T(8,128)S(1)} collective-permute-done((f32[16,8,640]{2,1,0:T(8,128)S(1)}, f32[16,8,640]{2,1,0:T(8,128)S(1)}, u32[]{:S(2)}, u32[]{:S(2)}) %collective-permute-start.6) | collective-permute-done | bytes 327712 | tf_op jit(solution)/shard_map/ppermute | solution.py:460
  33.5 0.6 collective-permute-start.7
  34.2 1.5 %collective-permute-start.8 = (f32[2,4,16,640]{3,2,1,0:T(8,128)S(1)}, f32[2,4,16,640]{3,2,1,0:T(8,128)S(1)}, u32[]{:S(2)}, u32[]{:S(2)}) collective-permute-start(f32[2,4,16,640]{3,2,1,0:T(8,128)S(1)} %get-tuple-element.104), channel_id=1, source_target_pairs={{0,16},{1,17},{2,18},{3,19},{4,20},{5,21},{6,22},{7,23},{8,24},{9,... | collective-permute-start | bytes 983048 | tf_op jit(solution)/shard_map/ppermute | solution.py:460
  35.7 1.4 %collective-permute-start.9 = (f32[2,4,16,640]{3,2,1,0:T(8,128)S(1)}, f32[2,4,16,640]{3,2,1,0:T(8,128)S(1)}, u32[]{:S(2)}, u32[]{:S(2)}) collective-permute-start(f32[2,4,16,640]{3,2,1,0:T(8,128)S(1)} %get-tuple-element.105), channel_id=1, source_target_pairs={{0,17},{1,16},{2,19},{3,18},{4,21},{5,20},{6,23},{7,22},{8,25},{9,... | collective-permute-start | bytes 983048 | tf_op jit(solution)/shard_map/ppermute | solution.py:460
  37.1 0.4 collective-permute-start.10
  37.5 4.6 %collective-permute-start.11 = (f32[2,4,8,640]{3,2,1,0:T(8,128)S(1)}, f32[2,4,8,640]{3,2,1,0:T(8,128)S(1)}, u32[]{:S(2)}, u32[]{:S(2)}) collective-permute-start(f32[2,4,8,640]{3,2,1,0:T(8,128)S(1)} %get-tuple-element.107.side1_ref), channel_id=1, source_target_pairs={{2,4},{3,5},{4,2},{5,3},{10,12},{11,13},{12,10},{13,11},{18,20},{1... | collective-permute-start | bytes 491528 | tf_op jit(solution)/shard_map/ppermute | solution.py:472
  42.2 3.1 %shard_map.49 = (f32[2,24,8,640]{3,2,1,0:T(8,128)S(1)}, f32[2,2,3,2,8,640]{5,4,3,2,1,0:T(8,128)S(1)}) custom-call(f32[16,8,640]{2,1,0:T(8,128)S(1)} %collective-permute-done.5.own_ref.far_ref, f32[16,8,640]{2,1,0:T(8,128)S(1)} %collective-permute-done.6.other_ref.across_ref, ...), custom_call_target="tpu_custom_call", output_to_operand_aliasing={{0}: (2, {}), {1}: (3, {})} | custom-call | flops 3849999872 | bytes 3604480 | tf_op jit(solution)/shard_map/pallas_call | solution.py:138
  45.3 0.0 collective-permute-done.10.halo0_ref
  45.3 0.1 collective-permute-done.11.halo1_ref
  45.4 2.1 %shard_map.52.own_ref.partner_ref = f32[2,2,4,8,640]{4,3,2,1,0:T(8,128)S(1)} custom-call(f32[2,4,8,640]{3,2,1,0:T(8,128)S(1)} %get-tuple-element.106.side0_ref, f32[2,4,8,640]{3,2,1,0:T(8,128)S(1)} %get-tuple-element.107.side1_ref, f32[2,4,8,640]{3,2,1,0:T(8,128)S(1)} %collective-permute-done.10.halo0_ref, ...), custom_call_target="tpu_custom_call" | custom-call | flops 2640000000 | bytes 1474560 | tf_op jit(solution)/shard_map/pallas_call | solution.py:138
  47.5 1.1 shard_map.54
  48.6 0.0 collective-permute-done.8.far_ref
  48.6 0.1 collective-permute-done.9.across_ref
  48.7 0.4 collective-permute-start.12
  49.2 4.8 %collective-permute-start.13 = (f32[2,4,8,640]{3,2,1,0:T(8,128)S(1)}, f32[2,4,8,640]{3,2,1,0:T(8,128)S(1)}, u32[]{:S(2)}, u32[]{:S(2)}) collective-permute-start(f32[2,4,8,640]{3,2,1,0:T(8,128)S(1)} %get-tuple-element.118.side1_ref), channel_id=1, source_target_pairs={{2,4},{3,5},{4,2},{5,3},{10,12},{11,13},{12,10},{13,11},{18,20},{1... | collective-permute-start | bytes 491528 | tf_op jit(solution)/shard_map/ppermute | solution.py:472
  54.0 7.6 %shard_map.55 = (f32[2,24,8,640]{3,2,1,0:T(8,128)S(1)}, f32[2,2,3,2,8,640]{5,4,3,2,1,0:T(8,128)S(1)}) custom-call(f32[2,24,8,640]{3,2,1,0:T(8,128)S(1)} %get-tuple-element.96.own_ref.partner_ref, f32[2,24,8,640]{3,2,1,0:T(8,128)S(1)} %get-tuple-element.96.own_ref.partner_ref, f32[2,4,8,640]{3,2,1,0:T(8,128)S(1)} %get-tuple-element.117.side0_ref, ...), custom_call_target="tpu_custom_call" | custom-call | flops 8800000000 | bytes 4423712 | tf_op jit(solution)/shard_map/pallas_call | solution.py:138
  61.6 0.0 collective-permute-done.13.halo1_ref
  61.6 2.1 %shard_map.56.own_ref = f32[2,2,4,8,640]{4,3,2,1,0:T(8,128)S(1)} custom-call(f32[2,4,8,640]{3,2,1,0:T(8,128)S(1)} %get-tuple-element.117.side0_ref, f32[2,4,8,640]{3,2,1,0:T(8,128)S(1)} %get-tuple-element.118.side1_ref, f32[2,4,8,640]{3,2,1,0:T(8,128)S(1)} %collective-permute-done.12.halo0_ref, f32[2,4,8,640]{3,2,1,0:T(8,128)S(1)} %collective-permute-done.13.halo1_ref, ...), custom_call_target="tpu_custom_call" | custom-call | flops 2640000000 | bytes 1474560 | tf_op jit(solution)/shard_map/pallas_call | solution.py:138
  63.7 0.1 collective-permute-start.14
  63.8 0.5 collective-permute-start.15
  64.3 0.8 shard_map.57
  65.1 1.7 %collective-permute-done.15.partner_ref = f32[2,2,4,8,640]{4,3,2,1,0:T(8,128)S(1)} collective-permute-done((f32[2,2,4,8,640]{4,3,2,1,0:T(8,128)S(1)}, f32[2,2,4,8,640]{4,3,2,1,0:T(8,128)S(1)}, u32[]{:S(2)}, u32[]{:S(2)}) %collective-permute-start.15) | collective-permute-done | bytes 327712 | tf_op jit(solution)/shard_map/ppermute | solution.py:460
  66.8 1.1 shard_map.58
  67.8 0.1 collective-permute-start.16
  67.9 1.9 %collective-permute-start.17 = (f32[2,4,8,640]{3,2,1,0:T(8,128)S(1)}, f32[2,4,8,640]{3,2,1,0:T(8,128)S(1)}, u32[]{:S(2)}, u32[]{:S(2)}) collective-permute-start(f32[2,4,8,640]{3,2,1,0:T(8,128)S(1)} %get-tuple-element.130.side1_ref), channel_id=1, source_target_pairs={{2,4},{3,5},{4,2},{5,3},{10,12},{11,13},{12,10},{13,11},{18,20},{1... | collective-permute-start | bytes 491528 | tf_op jit(solution)/shard_map/ppermute | solution.py:472
  69.9 7.6 %shard_map.59 = (f32[2,24,8,640]{3,2,1,0:T(8,128)S(1)}, f32[2,2,3,2,8,640]{5,4,3,2,1,0:T(8,128)S(1)}) custom-call(f32[2,24,8,640]{3,2,1,0:T(8,128)S(1)} %get-tuple-element.121.own_ref, f32[2,24,8,640]{3,2,1,0:T(8,128)S(1)} %collective-permute-done.14.partner_ref, f32[2,4,8,640]{3,2,1,0:T(8,128)S(1)} %get-tuple-element.129.side0_ref, ...), custom_call_target="tpu_custom_call" | custom-call | flops 8800000000 | bytes 5079088 | tf_op jit(solution)/shard_map/pallas_call | solution.py:138
  77.5 0.0 collective-permute-done.16.halo0_ref
  77.5 0.0 collective-permute-done.17.halo1_ref
  77.5 2.1 %shard_map.60.own_ref.partner_ref = f32[2,2,4,8,640]{4,3,2,1,0:T(8,128)S(1)} custom-call(f32[2,4,8,640]{3,2,1,0:T(8,128)S(1)} %get-tuple-element.129.side0_ref, f32[2,4,8,640]{3,2,1,0:T(8,128)S(1)} %get-tuple-element.130.side1_ref, f32[2,4,8,640]{3,2,1,0:T(8,128)S(1)} %collective-permute-done.16.halo0_ref, ...), custom_call_target="tpu_custom_call" | custom-call | flops 2640000000 | bytes 1474560 | tf_op jit(solution)/shard_map/pallas_call | solution.py:138
  79.6 1.1 shard_map.61
  80.7 0.8 collective-permute-start.21
  81.5 3.4 %collective-permute-start.22 = (f32[2,4,8,640]{3,2,1,0:T(8,128)S(1)}, f32[2,4,8,640]{3,2,1,0:T(8,128)S(1)}, u32[]{:S(2)}, u32[]{:S(2)}) collective-permute-start(f32[2,4,8,640]{3,2,1,0:T(8,128)S(1)} %get-tuple-element.134.side1_ref), channel_id=1, source_target_pairs={{2,4},{3,5},{4,2},{5,3},{10,12},{11,13},{12,10},{13,11},{18,20},{1... | collective-permute-start | bytes 491528 | tf_op jit(solution)/shard_map/ppermute | solution.py:472
  84.9 4.5 %shard_map.63 = (f32[12,8,512]{2,1,0:T(8,128)S(1)}, f32[12,8,512]{2,1,0:T(8,128)S(1)}, f32[2,1,3,2,8,640]{5,4,3,2,1,0:T(8,128)S(1)}) custom-call(f32[2,24,8,640]{3,2,1,0:T(8,128)S(1)} %get-tuple-element.131.own_ref.partner_ref, f32[2,24,8,640]{3,2,1,0:T(8,128)S(1)} %get-tuple-element.131.own_ref.partner_ref, ...), custom_call_target="tpu_custom_call" | custom-call | flops 4620000256 | bytes 4243504 | tf_op jit(solution)/shard_map/pallas_call | solution.py:138
  89.4 1.6 %collective-permute-start.20 = (f32[12,8,512]{2,1,0:T(8,128)S(1)}, f32[12,8,512]{2,1,0:T(8,128)S(1)}, u32[]{:S(2)}, u32[]{:S(2)}) collective-permute-start(f32[12,8,512]{2,1,0:T(8,128)S(1)} %get-tuple-element.138), channel_id=1, source_target_pairs={{0,17},{1,16},{2,19},{3,18},{4,21},{5,20},{6,23},{7,22},{8,25},{9,... | collective-permute-start | bytes 589832 | tf_op jit(solution)/shard_map/ppermute | solution.py:460
  91.0 4.5 %shard_map.62 = (f32[12,8,512]{2,1,0:T(8,128)S(1)}, f32[12,8,512]{2,1,0:T(8,128)S(1)}, f32[2,1,3,2,8,640]{5,4,3,2,1,0:T(8,128)S(1)}) custom-call(f32[2,24,8,640]{3,2,1,0:T(8,128)S(1)} %get-tuple-element.131.own_ref.partner_ref, f32[2,24,8,640]{3,2,1,0:T(8,128)S(1)} %get-tuple-element.131.own_ref.partner_ref, ...), custom_call_target="tpu_custom_call" | custom-call | flops 4620000256 | bytes 4243504 | tf_op jit(solution)/shard_map/pallas_call | solution.py:138
  95.4 1.5 %collective-permute-start.18 = (f32[12,8,512]{2,1,0:T(8,128)S(1)}, f32[12,8,512]{2,1,0:T(8,128)S(1)}, u32[]{:S(2)}, u32[]{:S(2)}) collective-permute-start(f32[12,8,512]{2,1,0:T(8,128)S(1)} %get-tuple-element.136), channel_id=1, source_target_pairs={{0,1},{1,0},{2,3},{3,2},{4,5},{5,4},{6,7},{7,6},{8,9},{9,8},{10,11... | collective-permute-start | bytes 589832 | tf_op jit(solution)/shard_map/ppermute | solution.py:460
  96.9 0.5 collective-permute-start.19
  97.5 2.3 %shard_map.64 = (f32[4,8,512]{2,1,0:T(8,128)S(1)}, f32[4,8,512]{2,1,0:T(8,128)S(1)}, f32[4,8,512]{2,1,0:T(8,128)S(1)}, f32[4,8,512]{2,1,0:T(8,128)S(1)}) custom-call(f32[2,4,8,640]{3,2,1,0:T(8,128)S(1)} %get-tuple-element.133.side0_ref, f32[2,4,8,640]{3,2,1,0:T(8,128)S(1)} %get-tuple-element.134.side1_ref, ...), custom_call_target="tpu_custom_call" | custom-call | flops 2750000128 | bytes 1409024 | tf_op jit(solution)/shard_map/pallas_call | solution.py:138
  99.8 0.7 collective-permute-start.23
  100.4 1.5 %collective-permute-start.24 = (f32[4,8,512]{2,1,0:T(8,128)S(1)}, f32[4,8,512]{2,1,0:T(8,128)S(1)}, u32[]{:S(2)}, u32[]{:S(2)}) collective-permute-start(f32[4,8,512]{2,1,0:T(8,128)S(1)} %get-tuple-element.145), channel_id=1, source_target_pairs={{0,16},{1,17},{2,18},{3,19},{4,20},{5,21},{6,22},{7,23},{8,24},{9,... | collective-permute-start | bytes 196616 | tf_op jit(solution)/shard_map/ppermute | solution.py:460
  101.9 1.4 %collective-permute-start.25 = (f32[4,8,512]{2,1,0:T(8,128)S(1)}, f32[4,8,512]{2,1,0:T(8,128)S(1)}, u32[]{:S(2)}, u32[]{:S(2)}) collective-permute-start(f32[4,8,512]{2,1,0:T(8,128)S(1)} %get-tuple-element.146), channel_id=1, source_target_pairs={{0,17},{1,16},{2,19},{3,18},{4,21},{5,20},{6,23},{7,22},{8,25},{9,... | collective-permute-start | bytes 196616 | tf_op jit(solution)/shard_map/ppermute | solution.py:460
  103.3 0.1 collective-permute-done.19.refs_2_
  103.4 1.4 %collective-permute-done.23.refs_5_ = f32[4,8,512]{2,1,0:T(8,128)S(1)} collective-permute-done((f32[4,8,512]{2,1,0:T(8,128)S(1)}, f32[4,8,512]{2,1,0:T(8,128)S(1)}, u32[]{:S(2)}, u32[]{:S(2)}) %collective-permute-start.23) | collective-permute-done | bytes 65568 | tf_op jit(solution)/shard_map/ppermute | solution.py:460
  104.8 0.2 collective-permute-done.24.refs_6_
  105.0 2.1 %collective-permute-done.25.refs_7_ = f32[4,8,512]{2,1,0:T(8,128)S(1)} collective-permute-done((f32[4,8,512]{2,1,0:T(8,128)S(1)}, f32[4,8,512]{2,1,0:T(8,128)S(1)}, u32[]{:S(2)}, u32[]{:S(2)}) %collective-permute-start.25) | collective-permute-done | bytes 65568 | tf_op jit(solution)/shard_map/ppermute | solution.py:460
  107.1 1.1 shard_map.65
  (18 shorter events, 0.1 us)
Async XLA Ops:
  0.0 6.7 %collective-permute-start = (f32[16,8,2048]{2,1,0:T(8,128)}, f32[16,8,2048]{2,1,0:T(8,128)S(1)}, u32[]{:S(2)}, u32[]{:S(2)}) collective-permute-start(f32[16,8,2048]{2,1,0:T(8,128)} %bitcast.2), channel_id=1, source_target_pairs={{0,8},{1,9},{2,10},{3,11},{4,12},{5,13},{6,14},{7,15},{8,0},{9,1},... | collective-permute-start | bytes 3145736 | tf_op jit(solution)/shard_map/ppermute | solution.py:460
  0.0 1.6 %copy-start = (f32[1,4,4,16,2048]{4,3,2,1,0:T(8,128)S(1)}, f32[1,4,4,16,2048]{4,3,2,1,0:T(8,128)}, u32[]{:S(2)}) copy-start(f32[1,4,4,16,2048]{4,3,2,1,0:T(8,128)} %coeff_hbm.3) | copy-start | bytes 6291460
  1.6 0.7 copy-start.3
  2.3 4.5 %copy-start.2 = (f32[1,16,8,2048]{3,2,1,0:T(8,128)S(1)}, f32[1,16,8,2048]{3,2,1,0:T(8,128)}, u32[]{:S(2)}) copy-start(f32[1,16,8,2048]{3,2,1,0:T(8,128)} %param.4) | copy-start | bytes 3145732
  2.3 4.5 %copy-start.4 = (f32[4]{0:T(128)S(1)}, f32[4]{0:T(128)}, u32[]{:S(2)}) copy-start(f32[4]{0:T(128)} %level_ref.15) | copy-start | bytes 52
  3.1 7.2 %collective-permute-start.1 = (f32[1,4,16,640]{3,2,1,0:T(8,128)S(1)}, f32[1,4,16,640]{3,2,1,0:T(8,128)S(1)}, u32[]{:S(2)}, u32[]{:S(2)}) collective-permute-start(f32[1,4,16,640]{3,2,1,0:T(8,128)S(1)} %get-tuple-element.82), channel_id=1, source_target_pairs={{0,1},{1,0},{2,3},{3,2},{4,5},{5,4},{6,7},{7,6},{8,9},{9,8},{10,11... | collective-permute-start | bytes 491528 | tf_op jit(solution)/shard_map/ppermute | solution.py:460
  4.7 7.0 %collective-permute-start.2 = (f32[1,4,16,640]{3,2,1,0:T(8,128)S(1)}, f32[1,4,16,640]{3,2,1,0:T(8,128)S(1)}, u32[]{:S(2)}, u32[]{:S(2)}) collective-permute-start(f32[1,4,16,640]{3,2,1,0:T(8,128)S(1)} %get-tuple-element.83), channel_id=1, source_target_pairs={{0,16},{1,17},{2,18},{3,19},{4,20},{5,21},{6,22},{7,23},{8,24},{9,... | collective-permute-start | bytes 491528 | tf_op jit(solution)/shard_map/ppermute | solution.py:460
  6.2 8.3 %collective-permute-start.3 = (f32[1,4,16,640]{3,2,1,0:T(8,128)S(1)}, f32[1,4,16,640]{3,2,1,0:T(8,128)S(1)}, u32[]{:S(2)}, u32[]{:S(2)}) collective-permute-start(f32[1,4,16,640]{3,2,1,0:T(8,128)S(1)} %get-tuple-element.84), channel_id=1, source_target_pairs={{0,17},{1,16},{2,19},{3,18},{4,21},{5,20},{6,23},{7,22},{8,25},{9,... | collective-permute-start | bytes 491528 | tf_op jit(solution)/shard_map/ppermute | solution.py:460
  6.7 10.8 %copy-start.1 = (f32[1,4,4,16,2048]{4,3,2,1,0:T(8,128)S(1)}, f32[1,4,4,16,2048]{4,3,2,1,0:T(8,128)}, u32[]{:S(2)}) copy-start(f32[1,4,4,16,2048]{4,3,2,1,0:T(8,128)} %coeff_hbm.3) | copy-start | bytes 6291460
  14.5 9.0 %collective-permute-start.4 = (f32[16,8,640]{2,1,0:T(8,128)S(1)}, f32[16,8,640]{2,1,0:T(8,128)S(1)}, u32[]{:S(2)}, u32[]{:S(2)}) collective-permute-start(f32[16,8,640]{2,1,0:T(8,128)S(1)} %get-tuple-element.86), channel_id=1, source_target_pairs={{0,1},{1,0},{2,3},{3,2},{4,5},{5,4},{6,7},{7,6},{8,9},{9,8},{10,11... | collective-permute-start | bytes 983048 | tf_op jit(solution)/shard_map/ppermute | solution.py:460
  16.0 8.7 %collective-permute-start.5 = (f32[16,8,640]{2,1,0:T(8,128)S(1)}, f32[16,8,640]{2,1,0:T(8,128)S(1)}, u32[]{:S(2)}, u32[]{:S(2)}) collective-permute-start(f32[16,8,640]{2,1,0:T(8,128)S(1)} %get-tuple-element.87), channel_id=1, source_target_pairs={{0,16},{1,17},{2,18},{3,19},{4,20},{5,21},{6,22},{7,23},{8,24},{9,... | collective-permute-start | bytes 983048 | tf_op jit(solution)/shard_map/ppermute | solution.py:460
  24.8 8.7 %collective-permute-start.6 = (f32[16,8,640]{2,1,0:T(8,128)S(1)}, f32[16,8,640]{2,1,0:T(8,128)S(1)}, u32[]{:S(2)}, u32[]{:S(2)}) collective-permute-start(f32[16,8,640]{2,1,0:T(8,128)S(1)} %get-tuple-element.89), channel_id=1, source_target_pairs={{0,17},{1,16},{2,19},{3,18},{4,21},{5,20},{6,23},{7,22},{8,25},{9,... | collective-permute-start | bytes 983048 | tf_op jit(solution)/shard_map/ppermute | solution.py:460
  33.5 15.1 %collective-permute-start.7 = (f32[2,4,16,640]{3,2,1,0:T(8,128)S(1)}, f32[2,4,16,640]{3,2,1,0:T(8,128)S(1)}, u32[]{:S(2)}, u32[]{:S(2)}) collective-permute-start(f32[2,4,16,640]{3,2,1,0:T(8,128)S(1)} %get-tuple-element.103), channel_id=1, source_target_pairs={{0,1},{1,0},{2,3},{3,2},{4,5},{5,4},{6,7},{7,6},{8,9},{9,8},{10,11... | collective-permute-start | bytes 983048 | tf_op jit(solution)/shard_map/ppermute | solution.py:460
  34.2 14.4 %collective-permute-start.8 = (f32[2,4,16,640]{3,2,1,0:T(8,128)S(1)}, f32[2,4,16,640]{3,2,1,0:T(8,128)S(1)}, u32[]{:S(2)}, u32[]{:S(2)}) collective-permute-start(f32[2,4,16,640]{3,2,1,0:T(8,128)S(1)} %get-tuple-element.104), channel_id=1, source_target_pairs={{0,16},{1,17},{2,18},{3,19},{4,20},{5,21},{6,22},{7,23},{8,24},{9,... | collective-permute-start | bytes 983048 | tf_op jit(solution)/shard_map/ppermute | solution.py:460
  35.7 13.1 %collective-permute-start.9 = (f32[2,4,16,640]{3,2,1,0:T(8,128)S(1)}, f32[2,4,16,640]{3,2,1,0:T(8,128)S(1)}, u32[]{:S(2)}, u32[]{:S(2)}) collective-permute-start(f32[2,4,16,640]{3,2,1,0:T(8,128)S(1)} %get-tuple-element.105), channel_id=1, source_target_pairs={{0,17},{1,16},{2,19},{3,18},{4,21},{5,20},{6,23},{7,22},{8,25},{9,... | collective-permute-start | bytes 983048 | tf_op jit(solution)/shard_map/ppermute | solution.py:460
  37.1 8.2 %collective-permute-start.10 = (f32[2,4,8,640]{3,2,1,0:T(8,128)S(1)}, f32[2,4,8,640]{3,2,1,0:T(8,128)S(1)}, u32[]{:S(2)}, u32[]{:S(2)}) collective-permute-start(f32[2,4,8,640]{3,2,1,0:T(8,128)S(1)} %get-tuple-element.106.side0_ref), channel_id=1, source_target_pairs={{0,2},{1,3},{2,0},{3,1},{4,6},{5,7},{6,4},{7,5},{8,10},{9,11},{10,... | collective-permute-start | bytes 491528 | tf_op jit(solution)/shard_map/ppermute | solution.py:472
  37.5 7.9 %collective-permute-start.11 = (f32[2,4,8,640]{3,2,1,0:T(8,128)S(1)}, f32[2,4,8,640]{3,2,1,0:T(8,128)S(1)}, u32[]{:S(2)}, u32[]{:S(2)}) collective-permute-start(f32[2,4,8,640]{3,2,1,0:T(8,128)S(1)} %get-tuple-element.107.side1_ref), channel_id=1, source_target_pairs={{2,4},{3,5},{4,2},{5,3},{10,12},{11,13},{12,10},{13,11},{18,20},{1... | collective-permute-start | bytes 491528 | tf_op jit(solution)/shard_map/ppermute | solution.py:472
  48.7 12.8 %collective-permute-start.12 = (f32[2,4,8,640]{3,2,1,0:T(8,128)S(1)}, f32[2,4,8,640]{3,2,1,0:T(8,128)S(1)}, u32[]{:S(2)}, u32[]{:S(2)}) collective-permute-start(f32[2,4,8,640]{3,2,1,0:T(8,128)S(1)} %get-tuple-element.117.side0_ref), channel_id=1, source_target_pairs={{0,2},{1,3},{2,0},{3,1},{4,6},{5,7},{6,4},{7,5},{8,10},{9,11},{10,... | collective-permute-start | bytes 491528 | tf_op jit(solution)/shard_map/ppermute | solution.py:472
  49.2 12.4 %collective-permute-start.13 = (f32[2,4,8,640]{3,2,1,0:T(8,128)S(1)}, f32[2,4,8,640]{3,2,1,0:T(8,128)S(1)}, u32[]{:S(2)}, u32[]{:S(2)}) collective-permute-start(f32[2,4,8,640]{3,2,1,0:T(8,128)S(1)} %get-tuple-element.118.side1_ref), channel_id=1, source_target_pairs={{2,4},{3,5},{4,2},{5,3},{10,12},{11,13},{12,10},{13,11},{18,20},{1... | collective-permute-start | bytes 491528 | tf_op jit(solution)/shard_map/ppermute | solution.py:472
  63.7 6.2 %collective-permute-start.14 = (f32[2,24,8,640]{3,2,1,0:T(8,128)S(1)}, f32[2,24,8,640]{3,2,1,0:T(8,128)S(1)}, u32[]{:S(2)}, u32[]{:S(2)}) collective-permute-start(f32[2,24,8,640]{3,2,1,0:T(8,128)S(1)} %get-tuple-element.121.own_ref), channel_id=1, source_target_pairs={{0,8},{1,9},{2,10},{3,11},{4,12},{5,13},{6,14},{7,15},{8,0},{9,1},... | collective-permute-start | bytes 2949128 | tf_op jit(solution)/shard_map/ppermute | solution.py:460
  63.8 3.0 %collective-permute-start.15 = (f32[2,2,4,8,640]{4,3,2,1,0:T(8,128)S(1)}, f32[2,2,4,8,640]{4,3,2,1,0:T(8,128)S(1)}, u32[]{:S(2)}, u32[]{:S(2)}) collective-permute-start(f32[2,2,4,8,640]{4,3,2,1,0:T(8,128)S(1)} %shard_map.56.own_ref), channel_id=1, source_target_pairs={{0,8},{1,9},{2,10},{3,11},{4,12},{5,13},{6,14},{7,15},{8,0},{9,1},... | collective-permute-start | bytes 983048 | tf_op jit(solution)/shard_map/ppermute | solution.py:460
  67.8 9.6 %collective-permute-start.16 = (f32[2,4,8,640]{3,2,1,0:T(8,128)S(1)}, f32[2,4,8,640]{3,2,1,0:T(8,128)S(1)}, u32[]{:S(2)}, u32[]{:S(2)}) collective-permute-start(f32[2,4,8,640]{3,2,1,0:T(8,128)S(1)} %get-tuple-element.129.side0_ref), channel_id=1, source_target_pairs={{0,2},{1,3},{2,0},{3,1},{4,6},{5,7},{6,4},{7,5},{8,10},{9,11},{10,... | collective-permute-start | bytes 491528 | tf_op jit(solution)/shard_map/ppermute | solution.py:472
  67.9 9.6 %collective-permute-start.17 = (f32[2,4,8,640]{3,2,1,0:T(8,128)S(1)}, f32[2,4,8,640]{3,2,1,0:T(8,128)S(1)}, u32[]{:S(2)}, u32[]{:S(2)}) collective-permute-start(f32[2,4,8,640]{3,2,1,0:T(8,128)S(1)} %get-tuple-element.130.side1_ref), channel_id=1, source_target_pairs={{2,4},{3,5},{4,2},{5,3},{10,12},{11,13},{12,10},{13,11},{18,20},{1... | collective-permute-start | bytes 491528 | tf_op jit(solution)/shard_map/ppermute | solution.py:472
  80.7 16.8 %collective-permute-start.21 = (f32[2,4,8,640]{3,2,1,0:T(8,128)S(1)}, f32[2,4,8,640]{3,2,1,0:T(8,128)S(1)}, u32[]{:S(2)}, u32[]{:S(2)}) collective-permute-start(f32[2,4,8,640]{3,2,1,0:T(8,128)S(1)} %get-tuple-element.133.side0_ref), channel_id=1, source_target_pairs={{0,2},{1,3},{2,0},{3,1},{4,6},{5,7},{6,4},{7,5},{8,10},{9,11},{10,... | collective-permute-start | bytes 491528 | tf_op jit(solution)/shard_map/ppermute | solution.py:472
  81.5 16.0 %collective-permute-start.22 = (f32[2,4,8,640]{3,2,1,0:T(8,128)S(1)}, f32[2,4,8,640]{3,2,1,0:T(8,128)S(1)}, u32[]{:S(2)}, u32[]{:S(2)}) collective-permute-start(f32[2,4,8,640]{3,2,1,0:T(8,128)S(1)} %get-tuple-element.134.side1_ref), channel_id=1, source_target_pairs={{2,4},{3,5},{4,2},{5,3},{10,12},{11,13},{12,10},{13,11},{18,20},{1... | collective-permute-start | bytes 491528 | tf_op jit(solution)/shard_map/ppermute | solution.py:472
  89.4 8.1 %collective-permute-start.20 = (f32[12,8,512]{2,1,0:T(8,128)S(1)}, f32[12,8,512]{2,1,0:T(8,128)S(1)}, u32[]{:S(2)}, u32[]{:S(2)}) collective-permute-start(f32[12,8,512]{2,1,0:T(8,128)S(1)} %get-tuple-element.138), channel_id=1, source_target_pairs={{0,17},{1,16},{2,19},{3,18},{4,21},{5,20},{6,23},{7,22},{8,25},{9,... | collective-permute-start | bytes 589832 | tf_op jit(solution)/shard_map/ppermute | solution.py:460
  95.4 7.9 %collective-permute-start.18 = (f32[12,8,512]{2,1,0:T(8,128)S(1)}, f32[12,8,512]{2,1,0:T(8,128)S(1)}, u32[]{:S(2)}, u32[]{:S(2)}) collective-permute-start(f32[12,8,512]{2,1,0:T(8,128)S(1)} %get-tuple-element.136), channel_id=1, source_target_pairs={{0,1},{1,0},{2,3},{3,2},{4,5},{5,4},{6,7},{7,6},{8,9},{9,8},{10,11... | collective-permute-start | bytes 589832 | tf_op jit(solution)/shard_map/ppermute | solution.py:460
  96.9 6.5 %collective-permute-start.19 = (f32[12,8,512]{2,1,0:T(8,128)S(1)}, f32[12,8,512]{2,1,0:T(8,128)S(1)}, u32[]{:S(2)}, u32[]{:S(2)}) collective-permute-start(f32[12,8,512]{2,1,0:T(8,128)S(1)} %get-tuple-element.137), channel_id=1, source_target_pairs={{0,16},{1,17},{2,18},{3,19},{4,20},{5,21},{6,22},{7,23},{8,24},{9,... | collective-permute-start | bytes 589832 | tf_op jit(solution)/shard_map/ppermute | solution.py:460
  99.8 5.0 %collective-permute-start.23 = (f32[4,8,512]{2,1,0:T(8,128)S(1)}, f32[4,8,512]{2,1,0:T(8,128)S(1)}, u32[]{:S(2)}, u32[]{:S(2)}) collective-permute-start(f32[4,8,512]{2,1,0:T(8,128)S(1)} %get-tuple-element.144), channel_id=1, source_target_pairs={{0,1},{1,0},{2,3},{3,2},{4,5},{5,4},{6,7},{7,6},{8,9},{9,8},{10,11... | collective-permute-start | bytes 196616 | tf_op jit(solution)/shard_map/ppermute | solution.py:460
  100.4 4.5 %collective-permute-start.24 = (f32[4,8,512]{2,1,0:T(8,128)S(1)}, f32[4,8,512]{2,1,0:T(8,128)S(1)}, u32[]{:S(2)}, u32[]{:S(2)}) collective-permute-start(f32[4,8,512]{2,1,0:T(8,128)S(1)} %get-tuple-element.145), channel_id=1, source_target_pairs={{0,16},{1,17},{2,18},{3,19},{4,20},{5,21},{6,22},{7,23},{8,24},{9,... | collective-permute-start | bytes 196616 | tf_op jit(solution)/shard_map/ppermute | solution.py:460
  101.9 5.2 %collective-permute-start.25 = (f32[4,8,512]{2,1,0:T(8,128)S(1)}, f32[4,8,512]{2,1,0:T(8,128)S(1)}, u32[]{:S(2)}, u32[]{:S(2)}) collective-permute-start(f32[4,8,512]{2,1,0:T(8,128)S(1)} %get-tuple-element.146), channel_id=1, source_target_pairs={{0,17},{1,16},{2,19},{3,18},{4,21},{5,20},{6,23},{7,22},{8,25},{9,... | collective-permute-start | bytes 196616 | tf_op jit(solution)/shard_map/ppermute | solution.py:460

commit v2 on v1

--- a/solution.py
+++ b/solution.py
@@ -17,9 +17,10 @@
 root_half = 0.7071067811865476
 
 LANES = 128
+HELD = (0.25 / plane_rate) ** 0.5
 SPARE = 64
 EDGE = SWEEPS
-GROUP = 12
+GROUP = {1: 12, 2: 8}
 VMEM = pltpu.VMEM
 SMEM = pltpu.SMEM
 
@@ -37,7 +38,7 @@
 
 
 def quotient(change):
-    return change / (1.0 + change * change)
+    return change / (1.0 / plane_rate + change * change)
 
 
 def moved_right(parts, amount, first):
@@ -89,7 +90,7 @@
         change[self.last_part] = change[self.last_part] * self.last
         flux_x = quotient(joined(change))
         gain = (flux_y - pltpu.roll(flux_y, 1, 0)) + (flux_x - pltpu.roll(flux_x, 1, 1))
-        return value + (plane_rate * gain + depth_rate * (flux_above - flux_below))
+        return value + (gain + (depth_rate / plane_rate) * (flux_above - flux_below))
 
 
 class Place:
@@ -112,7 +113,7 @@
     def signs(self, slot, bit, level):
         is_lower = self.lower(slot, bit)
         sign = jnp.where(is_lower, 1.0, -1.0).astype(jnp.float32)
-        return sign, jnp.where(is_lower, 0.0, 0.5 * level).astype(jnp.float32)
+        return sign, jnp.where(is_lower, 0.0, HELD * level).astype(jnp.float32)
 
     def sweep(self, width):
         first = jnp.where(self.chunk == 0, 0.0, 1.0).astype(jnp.float32)
@@ -151,18 +152,14 @@
     return jax.ShapeDtypeStruct(shape, jnp.float32)
 
 
-def fetch(copies, sems):
-    started = [pltpu.make_async_copy(a, b, sems.at[i]) for i, (a, b) in enumerate(copies)]
-    for copy in started:
-        copy.start()
-    return started
-
-
-def pack_section(place, coeff_ref, offset, whole, outs):
+def marked(value, offset):
+    return jnp.where(lane_ids() == 0, offset.astype(jnp.float32), value)
+
+
+def pack_section(place, coeff_ref, whole, outs):
     planes, width = coeff_ref.shape[1:]
     step = width // 4
     zero = jnp.zeros((8, LANES), jnp.float32)
-    lanes = lane_ids()
     for k in range(BAND):
         for z in range(0, planes, 8):
             value = coeff_ref[k, z : z + 8, :]
@@ -170,23 +167,18 @@
     for number, out_ref in enumerate(outs):
         start = pl.multiple_of((place.chunk ^ number) * step, LANES)
         out_ref[...] = whole[:, :, pl.ds(start, step + LANES)]
-        out_ref[0, 0:8, 0:LANES] = jnp.where(lanes == 0, offset.astype(jnp.float32), out_ref[0, 0:8, 0:LANES])
-
-
-def intake_kernel(coeff_hbm, offset_ref, coeff_ref, *refs):
-    out_refs, (later, whole, sems) = refs[:4], refs[4:]
-    now_copy, later_copy = fetch([(coeff_hbm.at[0, 0], coeff_ref), (coeff_hbm.at[0, 1], later)], sems)
-    later_copy.wait()
-    pack_section(Place(), later, offset_ref[0, 0, 1], whole, [ref.at[0] for ref in out_refs])
-    now_copy.wait()
-
-
-def coeff_kernel(first, count, coeff_hbm, offset_ref, *refs):
-    out_refs, (sections, whole, sems) = refs[:4], refs[4:]
-    copies = fetch([(coeff_hbm.at[0, first + i], sections.at[i]) for i in range(count)], sems)
-    for i in range(count):
-        copies[i].wait()
-        pack_section(Place(), sections.at[i], offset_ref[0, 0, first + i], whole, [ref.at[i] for ref in out_refs])
+
+
+def early_kernel(coeff_ref, *refs):
+    pack_section(Place(), coeff_ref, refs[4], refs[:4])
+
+
+def late_kernel(coeff_ref, offset_ref, *refs):
+    for section in range(2, SECTIONS):
+        outs = [ref.at[section - 2] for ref in refs[:4]]
+        pack_section(Place(), coeff_ref.at[0, section], refs[4], outs)
+        for out in outs:
+            out[0, 0:8, 0:LANES] = marked(out[0, 0:8, 0:LANES], offset_ref[0, 0, section])
 
 
 def first_kernel(own_ref, partner_ref, coeff_ref, offset_ref, level_ref, *refs):
@@ -205,10 +197,10 @@
         shifted = pltpu.roll(field, (width + BAND // 2 - offset) % width, 1)
         warped = None
         for k in range(BAND):
-            row = joined([coeff_ref[k, pl.ds(z, 1), :], no_rows])
+            row = joined([coeff_ref[0, 0, k, pl.ds(z, 1), :], no_rows])
             term = jnp.broadcast_to(row, shifted.shape) * (pltpu.roll(shifted, width - k, 1) if k else shifted)
             warped = term if warped is None else warped + term
-        value = haar(joined([own_ref[z], zero]), warped, sign, level, 0.5 * root_half)
+        value = haar(joined([own_ref[z], zero]), warped, sign, level, HELD * root_half)
         whole[z] = pltpu.roll(value, SPARE, 1)
         return carry
 
@@ -216,19 +208,13 @@
     for number, out_ref in enumerate(out_refs):
         start = pl.multiple_of((place.chunk ^ number) * step, LANES)
         out_ref[...] = whole[:, :, pl.ds(start, step + LANES)]
-
-
-def gather_coeff_kernel(self_ref, near_ref, far_ref, across_ref, out_ref, offset_ref):
-    place = Place()
-    sections = self_ref.shape[0]
-    for number, ref in enumerate((self_ref, near_ref, far_ref, across_ref)):
-        slot = number // 2
-        slab = place.slab ^ (number % 2)
-        for section in range(sections):
-            out_ref[section, slot, slab] = ref[section]
-            corner = ref[section, 0, 0:8, 0:LANES]
-            offset = jnp.max(jnp.where(lane_ids() == 0, corner, -100.0))
-            offset_ref[section, slot, slab] = offset.astype(jnp.int32)
+        out_ref[0, :, 0:LANES] = marked(out_ref[0, :, 0:LANES], offset_ref[0, 0, 1])
+
+
+def coeff_rows(section, refs):
+    if section == 1:
+        return [lambda k, z, ref=ref: ref[k, pl.ds(z, 1), :] for ref in refs]
+    return [lambda k, z, ref=ref: ref[section - 2, k, pl.ds(z, 1), :] for ref in refs]
 
 
 def start_kernel(self_ref, near_ref, far_ref, across_ref, side0_ref, side1_ref):
@@ -250,7 +236,7 @@
 def trapezoid(place, load, planes, emit, saved_ref, one, two, slots=(0, 1)):
     width = one.shape[-1]
     sweep = place.sweep(width)
-    size = GROUP // len(slots)
+    size = GROUP[len(slots)]
     for level in range(1, SWEEPS + 1):
         def source(slot, p, level=level):
             if level == 1:
@@ -312,14 +298,14 @@
 
 
 def finished(value):
-    return 2.0 * joined(moved_left(cells(value), SPARE)[: (value.shape[1] - 2 * SPARE) // LANES])
-
-
-def inner_haar(place, section, bit, slots, own_ref, partner_ref, sides, coeff_ref, offset_ref, level_ref, zero_level):
+    return (1.0 / HELD) * joined(moved_left(cells(value), SPARE)[: (value.shape[1] - 2 * SPARE) // LANES])
+
+
+def inner_haar(place, section, bit, slots, own_ref, partner_ref, sides, coeff_refs, offset_ref, level_ref, zero_level):
     inner = own_ref.shape[1]
     planes = inner + 2 * EDGE
     half = planes // 2
-    group = 0 if section == 1 else section - 2
+    rows_of = coeff_rows(section, coeff_refs)
     for slot in slots:
         for side, ref in enumerate(sides):
             for e in range(EDGE):
@@ -327,21 +313,24 @@
     for slot in slots:
         sign, level = place.signs(slot, bit, level_ref[section])
         other = 1 - slot if bit == 1 else slot
-        for slab in range(2):
-            offset = offset_ref[group, slot, slab]
-            start, stop = (EDGE, half) if slab == 0 else (half, planes - EDGE)
-            for p in range(start, stop):
-                rows = [coeff_ref[group, slot, slab, k, pl.ds(p - slab * half, 1), :] for k in range(BAND)]
+        for away in range(2):
+            slab = place.slab ^ away
+            offset = offset_ref[0 if section == 1 else section - 2, slot, away]
+            start = jnp.where(slab == 0, EDGE, 0)
+            for i in range(half - EDGE):
+                z = start + i
+                p = slab * half + z
+                rows = [rows_of[2 * slot + away](k, z) for k in range(BAND)]
                 warped = warped_plane(partner_ref[other, p - EDGE], rows, offset)
                 zero_level[slot, p] = haar(own_ref[slot, p - EDGE], warped, sign, level, root_half)
 
 
-def inner_kernel(section, bit, own_ref, partner_ref, side0_ref, side1_ref, coeff_ref, offset_ref, level_ref,
-                 out_ref, saved_ref, zero_level, one, two):
+def inner_kernel(section, bit, own_ref, partner_ref, side0_ref, side1_ref, offset_ref, level_ref, *refs):
+    coeff_refs, (out_ref, saved_ref, zero_level, one, two) = refs[:4], refs[4:]
     place = Place()
     planes = own_ref.shape[1] + 2 * EDGE
     sides = (side0_ref, side1_ref)
-    inner_haar(place, section, bit, (0, 1), own_ref, partner_ref, sides, coeff_ref, offset_ref, level_ref, zero_level)
+    inner_haar(place, section, bit, (0, 1), own_ref, partner_ref, sides, coeff_refs, offset_ref, level_ref, zero_level)
 
     def emit(slot, i, value):
         out_ref[slot, i] = value
@@ -349,12 +338,12 @@
     trapezoid(place, lambda slot, p: zero_level[slot, p], planes, emit, saved_ref, one, two)
 
 
-def inner_last_kernel(section, bit, slot, own_ref, partner_ref, side0_ref, side1_ref, coeff_ref, offset_ref, level_ref,
-                      mine_ref, other_ref, saved_ref, zero_level, one, two, done):
+def inner_last_kernel(section, bit, slot, own_ref, partner_ref, side0_ref, side1_ref, offset_ref, level_ref, *refs):
+    coeff_refs, (mine_ref, other_ref, saved_ref, zero_level, one, two, done) = refs[:4], refs[4:]
     place = Place()
     planes = own_ref.shape[1] + 2 * EDGE
     sides = (side0_ref, side1_ref)
-    inner_haar(place, section, bit, (slot,), own_ref, partner_ref, sides, coeff_ref, offset_ref, level_ref, zero_level)
+    inner_haar(place, section, bit, (slot,), own_ref, partner_ref, sides, coeff_refs, offset_ref, level_ref, zero_level)
 
     def emit(slot, i, value):
         done[i] = finished(value)
@@ -382,9 +371,14 @@
     return values
 
 
-def wedge_kernel(side0_ref, side1_ref, halo0_ref, halo1_ref, saved_ref, out_ref):
+def wedge_kernel(corners, side0_ref, side1_ref, halo0_ref, halo1_ref, saved_ref, *refs):
+    marked_refs, out_ref = refs[: 4 * bool(corners)], refs[4 * bool(corners)]
     place = Place()
     sweep = place.sweep(side0_ref.shape[-1])
+    for number, ref in enumerate(marked_refs):
+        for i, at in enumerate(corners):
+            value = jnp.max(jnp.where(lane_ids() == 0, ref[*at, 0:8, 0:LANES], -100.0))
+            refs[5][i, number // 2, number % 2] = value.astype(jnp.int32)
     for side, (edge, halo) in enumerate(((side0_ref, halo0_ref), (side1_ref, halo1_ref))):
         values = wedge(place, sweep, side, edge, halo, lambda *at: saved_ref[at])
         for slot in range(2):
@@ -392,23 +386,25 @@
                 out_ref[side, slot, e] = values[slot][e]
 
 
-def haar_kernel(section, bit, own_ref, partner_ref, coeff_ref, offset_ref, level_ref, out0_ref, out1_ref):
-    place = Place()
-    outs = (out0_ref, out1_ref)
-    half = coeff_ref.shape[4]
-    group = 0 if section == 1 else section - 2
-    planes = 2 * half
+def haar_kernel(section, bit, own_ref, partner_ref, offset_ref, level_ref, *refs):
+    coeff_refs, (out0_ref, out1_ref, done) = refs[:4], refs[4:]
+    place = Place()
+    half = coeff_refs[0].shape[-2]
+    rows_of = coeff_rows(section, coeff_refs)
     for slot in range(2):
         sign, level = place.signs(slot, bit, level_ref[section])
         other = 1 - slot if bit == 1 else slot
-        for side in range(2):
-            slab = jnp.where(place.odd == side, 1, 0)
-            offset = offset_ref[group, slot, slab]
+        for away in range(2):
+            is_top = place.slab ^ away == 1
+            side = jnp.where(is_top, place.odd, 1 - place.odd)
+            offset = offset_ref[0 if section == 1 else section - 2, slot, away]
             for e in range(EDGE):
-                z = place.spot(side, e, planes) - slab * half
-                rows = [coeff_ref[group, slot, slab, k, pl.ds(z, 1), :] for k in range(BAND)]
+                z = jnp.where(is_top, half - 1 - e, e)
+                rows = [rows_of[2 * slot + away](k, z) for k in range(BAND)]
                 warped = warped_plane(partner_ref[side, other, e], rows, offset)
-                outs[side][slot, e] = haar(own_ref[side, slot, e], warped, sign, level, root_half)
+                done[side, slot, e] = haar(own_ref[side, slot, e], warped, sign, level, root_half)
+    out0_ref[...] = done[0]
+    out1_ref[...] = done[1]
 
 
 def wedge_last_kernel(side0_ref, side1_ref, halo0_ref, halo1_ref, saved0_ref, saved1_ref, *refs):
@@ -478,32 +474,19 @@
     level_scratch = pltpu.VMEM((2, planes, rows, width), jnp.float32)
     packed = pltpu.VMEM((BAND, half, length + LANES), jnp.float32)
 
-    def coeff_state(pieces, count):
-        return call(
-            gather_coeff_kernel,
-            [f32(count, 2, 2, BAND, half, width), jax.ShapeDtypeStruct((count, 2, 2), jnp.int32)],
-            *pieces, smem_outs=(1,), micros=0.8,
-        )
-
     received = swap(volume[0], 1)
-    first_coeff, *early = call(
-        intake_kernel, [f32(BAND, half, length)] + [f32(1, BAND, half, width)] * 4, warp_coef, offsets,
-        spaces={0: pltpu.HBM, 1: SMEM}, micros=1.2,
-        scratch=[pltpu.VMEM((BAND, half, length), jnp.float32), packed, pltpu.SemaphoreType.DMA((2,))],
+    early = call(
+        early_kernel, [f32(BAND, half, width)] * 4, warp_coef[0, 1], micros=0.8, scratch=[packed],
     )
     early = spread(early)
-    late_count = SECTIONS - 2
     pieces = call(
-        first_kernel, [f32(half, rows, width)] * 4, volume[0], received, first_coeff, offsets, thresholds,
+        first_kernel, [f32(half, rows, width)] * 4, volume[0], received, warp_coef, offsets, thresholds,
         spaces={3: SMEM, 4: SMEM}, micros=4.0, scratch=[pltpu.VMEM((half, rows, length + LANES), jnp.float32)],
     )
-    pieces, early = lax.optimization_barrier((pieces, early))
+    pieces, coeff = lax.optimization_barrier((pieces, early))
     late = call(
-        functools.partial(coeff_kernel, 2, late_count), [f32(late_count, BAND, half, width)] * 4, warp_coef, offsets,
-        spaces={0: pltpu.HBM, 1: SMEM}, micros=1.5,
-        scratch=[
-            pltpu.VMEM((late_count, BAND, half, length), jnp.float32), packed, pltpu.SemaphoreType.DMA((late_count,)),
-        ],
+        late_kernel, [f32(SECTIONS - 2, BAND, half, width)] * 4, warp_coef, offsets, spaces={1: SMEM}, micros=1.5,
+        scratch=[packed],
     )
     mine, near, far = pieces[0], swap(pieces[1], 0, 1), swap(pieces[2], 2, 0)
     last, near, far = lax.optimization_barrier((pieces[3], near, far))
@@ -521,29 +504,37 @@
         scratch=[level_scratch] * 3, micros=3.5, aliases={2: 0, 3: 1},
     )
     late = spread(late)
-    coeff, shift = coeff_state(early, 1)
+    table = None
     for section in range(1, SECTIONS):
         bit = section % levels
-        (edges,) = call(wedge_kernel, [edges_shape], side0, side1, halo0, halo1, saved, micros=2.4)
+        corners = {1: [(0,)], 2: [(i, 0) for i in range(SECTIONS - 2)]}.get(section, [])
+        edges, *shift = call(
+            functools.partial(wedge_kernel, corners),
+            [edges_shape] + [jax.ShapeDtypeStruct((len(corners), 2, 2), jnp.int32)] * bool(corners),
+            side0, side1, halo0, halo1, saved, *({1: (mine, near, far, across), 2: coeff}.get(section, ())),
+            smem_outs=(1,), micros=2.4,
+        )
+        table = shift[0] if shift else table
         partner, partner_edges = own, edges
         if bit != 1:
-            partner, edges = lax.optimization_barrier((own, edges))
-            partner, partner_edges = swap(partner, 1 << bit), swap(edges, 1 << bit)
+            partner, partner_edges = lax.optimization_barrier((own, swap(edges, 1 << bit)))
+            partner = swap(partner, 1 << bit)
         side0, side1 = call(
             functools.partial(haar_kernel, section, bit), [side_shape, side_shape],
-            edges, partner_edges, coeff, shift, thresholds, spaces={3: SMEM, 4: SMEM}, micros=1.1,
+            edges, partner_edges, table, thresholds, *coeff, spaces={2: SMEM, 3: SMEM}, micros=1.1,
+            scratch=[pltpu.VMEM((2, 2, EDGE, rows, width), jnp.float32)],
         )
-        used = coeff, shift
+        used = table, thresholds, *coeff
         if section == 1:
             late, side0, side1 = lax.optimization_barrier((late, side0, side1))
-            coeff, shift = coeff_state(late, late_count)
+            coeff = late
         halo0, halo1 = halo(side0, side1)
         if section == SECTIONS - 1:
             break
         own, saved = call(
             functools.partial(inner_kernel, section, bit), [inner_shape, saved_shape],
-            own, partner, side0, side1, *used, thresholds,
-            spaces={5: SMEM, 6: SMEM}, scratch=[level_scratch] * 3, micros=8.0,
+            own, partner, side0, side1, *used,
+            spaces={4: SMEM, 5: SMEM}, scratch=[level_scratch] * 3, micros=8.0,
         )
     piece_shape = f32(half - EDGE, rows, length // 4)
     edge_shape = f32(EDGE, rows, length // 4)
@@ -552,7 +543,7 @@
     def last_inner(slot):
         return call(
             functools.partial(inner_last_kernel, section, bit, slot), [piece_shape, piece_shape, slot_saved],
-            own, partner, side0, side1, *used, thresholds, spaces={5: SMEM, 6: SMEM}, micros=4.2,
+            own, partner, side0, side1, *used, spaces={4: SMEM, 5: SMEM}, micros=4.2,
             scratch=[level_scratch] * 3 + [pltpu.VMEM((inner, rows, length // 4), jnp.float32)],
         )
 

time: 108 us -> 106 us (0.981)
  Pallas kernels: 50.3 us -> 47.7 us
  waiting for transfers between devices: 19.5 us -> 20.6 us
    pallas_call x20 -> x18, Pallas kernels: 50.3 us -> 47.7 us  [call(): pl.pallas_call(body, out_shape=outs, in_specs=in_specs, out_specs=out_spe...]
    unnamed x10 -> x8, local copies, waits for them, and re-layouts: 2.26 us -> 0.02 us
    squeeze x0 -> x1, local copies, waits for them, and re-layouts: none -> 1.23 us  [on_device(): warp_coef[0, 1]]
  transfers between devices with their start and end apart: 26 -> 26, of which waited for: 12 -> 11; matrix products, arithmetic and copies ran while one was open for 0% -> 1% of each run, Pallas kernels for 41% -> 39%
where the time goes in v2:
time: 106 us; the launch traced here: 105 us
  Pallas kernels  47.7 us (45%)
  starting transfers between devices  35.5 us (33%)
  waiting for transfers between devices  20.6 us (19%)
  local copies, waits for them, and re-layouts  1.24 us (1%)
    pallas_call x18, Pallas kernels, call(): pl.pallas_call(body, out_shape=outs, in_specs=in_specs, out_specs=out_spe...  47.7 us
    ppermute x18, waiting for transfers between devices, swap(): return lax.ppermute(value, axes, route(frame_bits, slab_bits))  20.4 us
    ppermute x18, starting transfers between devices, swap(): return lax.ppermute(value, axes, route(frame_bits, slab_bits))  19 us
    ppermute x4, starting transfers between devices, halo(): lax.ppermute(side1, 'space', second)  14.7 us
  transfers between devices with their start and end apart: 26, of which 11 were waited for; matrix products, arithmetic and copies ran while one was open for 1% of the time, Pallas kernels for 39%

profile of v2, /device:TPU:8, one launch (start us, length us, event | category | flops | bytes accessed | tf_op | source)
XLA Modules:
  0.0 105.4 jit_solution(4761449904698858432)
XLA Ops:
  0.0 0.1 collective-permute-start
  0.1 1.2 %slice_bitcast_fusion.coeff_ref = f32[4,16,2048]{2,1,0:T(8,128)S(1)} fusion(f32[1,4,4,16,2048]{4,3,2,1,0:T(8,128)} %coeff_ref.3), kind=kLoop, calls=%fused_computation | loop fusion | bytes 1048576 | tf_op jit(solution)/shard_map/squeeze | solution.py:479
  1.3 0.2 shard_map.47
  1.6 1.6 %collective-permute-start.1 = (f32[4,16,640]{2,1,0:T(8,128)S(1)}, f32[4,16,640]{2,1,0:T(8,128)S(1)}, u32[]{:S(2)}, u32[]{:S(2)}) collective-permute-start(f32[4,16,640]{2,1,0:T(8,128)S(1)} %get-tuple-element.80), channel_id=1, source_target_pairs={{0,1},{1,0},{2,3},{3,2},{4,5},{5,4},{6,7},{7,6},{8,9},{9,8},{10,11... | collective-permute-start | bytes 491528 | tf_op jit(solution)/shard_map/ppermute | solution.py:456
  3.2 1.5 %collective-permute-start.2 = (f32[4,16,640]{2,1,0:T(8,128)S(1)}, f32[4,16,640]{2,1,0:T(8,128)S(1)}, u32[]{:S(2)}, u32[]{:S(2)}) collective-permute-start(f32[4,16,640]{2,1,0:T(8,128)S(1)} %get-tuple-element.81), channel_id=1, source_target_pairs={{0,16},{1,17},{2,18},{3,19},{4,20},{5,21},{6,22},{7,23},{8,24},{9,... | collective-permute-start | bytes 491528 | tf_op jit(solution)/shard_map/ppermute | solution.py:456
  4.7 0.5 collective-permute-start.3
  5.1 0.0 collective-permute-done.partner_ref
  5.2 3.6 %shard_map.46 = (f32[16,8,640]{2,1,0:T(8,128)S(1)}, f32[16,8,640]{2,1,0:T(8,128)S(1)}, f32[16,8,640]{2,1,0:T(8,128)S(1)}, f32[16,8,640]{2,1,0:T(8,128)S(1)}) custom-call(f32[16,8,2048]{2,1,0:T(8,128)S(1)} %bitcast.5, f32[16,8,2048]{2,1,0:T(8,128)S(1)} %collective-permute-done.partner_ref, f32[1,4,4,16,2048]{4,3,2,1,0:T(8,128)S(1)} %copy-done, ...), custom_call_target="tpu_custom_call" | custom-call | flops 4400000000 | bytes 5505056 | tf_op jit(solution)/shard_map/pallas_call | solution.py:139
  8.7 1.5 %collective-permute-done.2.refs_2_ = f32[4,16,640]{2,1,0:T(8,128)S(1)} collective-permute-done((f32[4,16,640]{2,1,0:T(8,128)S(1)}, f32[4,16,640]{2,1,0:T(8,128)S(1)}, u32[]{:S(2)}, u32[]{:S(2)}) %collective-permute-start.2) | collective-permute-done | bytes 163872 | tf_op jit(solution)/shard_map/ppermute | solution.py:456
  10.2 2.8 %collective-permute-done.3.refs_3_ = f32[4,16,640]{2,1,0:T(8,128)S(1)} collective-permute-done((f32[4,16,640]{2,1,0:T(8,128)S(1)}, f32[4,16,640]{2,1,0:T(8,128)S(1)}, u32[]{:S(2)}, u32[]{:S(2)}) %collective-permute-start.3) | collective-permute-done | bytes 163872 | tf_op jit(solution)/shard_map/ppermute | solution.py:456
  13.0 1.5 %collective-permute-start.4 = (f32[16,8,640]{2,1,0:T(8,128)S(1)}, f32[16,8,640]{2,1,0:T(8,128)S(1)}, u32[]{:S(2)}, u32[]{:S(2)}) collective-permute-start(f32[16,8,640]{2,1,0:T(8,128)S(1)} %get-tuple-element.84), channel_id=1, source_target_pairs={{0,1},{1,0},{2,3},{3,2},{4,5},{5,4},{6,7},{7,6},{8,9},{9,8},{10,11... | collective-permute-start | bytes 983048 | tf_op jit(solution)/shard_map/ppermute | solution.py:456
  14.5 1.5 %collective-permute-start.5 = (f32[16,8,640]{2,1,0:T(8,128)S(1)}, f32[16,8,640]{2,1,0:T(8,128)S(1)}, u32[]{:S(2)}, u32[]{:S(2)}) collective-permute-start(f32[16,8,640]{2,1,0:T(8,128)S(1)} %get-tuple-element.85), channel_id=1, source_target_pairs={{0,16},{1,17},{2,18},{3,19},{4,20},{5,21},{6,22},{7,23},{8,24},{9,... | collective-permute-start | bytes 983048 | tf_op jit(solution)/shard_map/ppermute | solution.py:456
  16.0 0.9 shard_map.50
  17.0 5.1 %collective-permute-done.4.other_ref.near_ref.refs_1_ = f32[16,8,640]{2,1,0:T(8,128)S(1)} collective-permute-done((f32[16,8,640]{2,1,0:T(8,128)S(1)}, f32[16,8,640]{2,1,0:T(8,128)S(1)}, u32[]{:S(2)}, u32[]{:S(2)}) %collective-permute-start.4) | collective-permute-done | bytes 327712 | tf_op jit(solution)/shard_map/ppermute | solution.py:456
  22.1 1.2 %collective-permute-done.5.own_ref.far_ref.refs_2_ = f32[16,8,640]{2,1,0:T(8,128)S(1)} collective-permute-done((f32[16,8,640]{2,1,0:T(8,128)S(1)}, f32[16,8,640]{2,1,0:T(8,128)S(1)}, u32[]{:S(2)}, u32[]{:S(2)}) %collective-permute-start.5) | collective-permute-done | bytes 327712 | tf_op jit(solution)/shard_map/ppermute | solution.py:456
  23.3 1.4 %collective-permute-start.6 = (f32[16,8,640]{2,1,0:T(8,128)S(1)}, f32[16,8,640]{2,1,0:T(8,128)S(1)}, u32[]{:S(2)}, u32[]{:S(2)}) collective-permute-start(f32[16,8,640]{2,1,0:T(8,128)S(1)} %get-tuple-element.87), channel_id=1, source_target_pairs={{0,17},{1,16},{2,19},{3,18},{4,21},{5,20},{6,23},{7,22},{8,25},{9,... | collective-permute-start | bytes 983048 | tf_op jit(solution)/shard_map/ppermute | solution.py:456
  24.8 3.0 %shard_map.48 = (f32[2,24,8,640]{3,2,1,0:T(8,128)S(1)}, f32[2,2,3,2,8,640]{5,4,3,2,1,0:T(8,128)S(1)}) custom-call(f32[16,8,640]{2,1,0:T(8,128)S(1)} %get-tuple-element.88.own_ref.self_ref.refs_0_, f32[16,8,640]{2,1,0:T(8,128)S(1)} %collective-permute-done.4.other_ref.near_ref.refs_1_), custom_call_target="tpu_custom_call" | custom-call | flops 3849999872 | bytes 2129920 | tf_op jit(solution)/shard_map/pallas_call | solution.py:139
  27.8 4.3 %collective-permute-done.6.other_ref.across_ref.refs_3_ = f32[16,8,640]{2,1,0:T(8,128)S(1)} collective-permute-done((f32[16,8,640]{2,1,0:T(8,128)S(1)}, f32[16,8,640]{2,1,0:T(8,128)S(1)}, u32[]{:S(2)}, u32[]{:S(2)}) %collective-permute-start.6) | collective-permute-done | bytes 327712 | tf_op jit(solution)/shard_map/ppermute | solution.py:456
  32.2 0.6 collective-permute-start.7
  32.8 1.5 %collective-permute-start.8 = (f32[2,4,16,640]{3,2,1,0:T(8,128)S(1)}, f32[2,4,16,640]{3,2,1,0:T(8,128)S(1)}, u32[]{:S(2)}, u32[]{:S(2)}) collective-permute-start(f32[2,4,16,640]{3,2,1,0:T(8,128)S(1)} %get-tuple-element.102), channel_id=1, source_target_pairs={{0,16},{1,17},{2,18},{3,19},{4,20},{5,21},{6,22},{7,23},{8,24},{9,... | collective-permute-start | bytes 983048 | tf_op jit(solution)/shard_map/ppermute | solution.py:456
  34.3 1.4 %collective-permute-start.9 = (f32[2,4,16,640]{3,2,1,0:T(8,128)S(1)}, f32[2,4,16,640]{3,2,1,0:T(8,128)S(1)}, u32[]{:S(2)}, u32[]{:S(2)}) collective-permute-start(f32[2,4,16,640]{3,2,1,0:T(8,128)S(1)} %get-tuple-element.103), channel_id=1, source_target_pairs={{0,17},{1,16},{2,19},{3,18},{4,21},{5,20},{6,23},{7,22},{8,25},{9,... | collective-permute-start | bytes 983048 | tf_op jit(solution)/shard_map/ppermute | solution.py:456
  35.7 0.4 collective-permute-start.10
  36.2 4.6 %collective-permute-start.11 = (f32[2,4,8,640]{3,2,1,0:T(8,128)S(1)}, f32[2,4,8,640]{3,2,1,0:T(8,128)S(1)}, u32[]{:S(2)}, u32[]{:S(2)}) collective-permute-start(f32[2,4,8,640]{3,2,1,0:T(8,128)S(1)} %get-tuple-element.105.side1_ref), channel_id=1, source_target_pairs={{2,4},{3,5},{4,2},{5,3},{10,12},{11,13},{12,10},{13,11},{18,20},{1... | collective-permute-start | bytes 491528 | tf_op jit(solution)/shard_map/ppermute | solution.py:468
  40.8 3.1 %shard_map.49 = (f32[2,24,8,640]{3,2,1,0:T(8,128)S(1)}, f32[2,2,3,2,8,640]{5,4,3,2,1,0:T(8,128)S(1)}) custom-call(f32[16,8,640]{2,1,0:T(8,128)S(1)} %collective-permute-done.5.own_ref.far_ref.refs_2_, f32[16,8,640]{2,1,0:T(8,128)S(1)} %collective-permute-done.6.other_ref.across_ref.refs_3_, ...), custom_call_target="tpu_custom_call", output_to_operand_aliasing={{0}: (2, {}), {1}: (3, {})} | custom-call | flops 3849999872 | bytes 3604480 | tf_op jit(solution)/shard_map/pallas_call | solution.py:139
  43.8 0.0 collective-permute-done.10.halo0_ref
  43.8 0.2 collective-permute-done.11.halo1_ref
  44.1 2.2 %shard_map.52 = (f32[2,2,4,8,640]{4,3,2,1,0:T(8,128)S(1)}, s32[1,2,2]{2,1,0:T(2,128)S(1)}) custom-call(f32[2,4,8,640]{3,2,1,0:T(8,128)S(1)} %get-tuple-element.104.side0_ref, f32[2,4,8,640]{3,2,1,0:T(8,128)S(1)} %get-tuple-element.105.side1_ref, f32[2,4,8,640]{3,2,1,0:T(8,128)S(1)} %collective-permute-done.10.halo0_ref, ...), custom_call_target="tpu_custom_call" | custom-call | flops 2640000000 | bytes 2785296 | tf_op jit(solution)/shard_map/pallas_call | solution.py:139
  46.3 1.1 shard_map.53
  47.3 0.0 collective-permute-done.8.refs_2_
  47.4 0.0 collective-permute-done.9.refs_3_
  47.4 0.4 collective-permute-start.12
  47.8 4.8 %collective-permute-start.13 = (f32[2,4,8,640]{3,2,1,0:T(8,128)S(1)}, f32[2,4,8,640]{3,2,1,0:T(8,128)S(1)}, u32[]{:S(2)}, u32[]{:S(2)}) collective-permute-start(f32[2,4,8,640]{3,2,1,0:T(8,128)S(1)} %get-tuple-element.116.side1_ref), channel_id=1, source_target_pairs={{2,4},{3,5},{4,2},{5,3},{10,12},{11,13},{12,10},{13,11},{18,20},{1... | collective-permute-start | bytes 491528 | tf_op jit(solution)/shard_map/ppermute | solution.py:468
  52.6 7.2 %shard_map.54 = (f32[2,24,8,640]{3,2,1,0:T(8,128)S(1)}, f32[2,2,3,2,8,640]{5,4,3,2,1,0:T(8,128)S(1)}) custom-call(f32[2,24,8,640]{3,2,1,0:T(8,128)S(1)} %get-tuple-element.94.own_ref.partner_ref, f32[2,24,8,640]{3,2,1,0:T(8,128)S(1)} %get-tuple-element.94.own_ref.partner_ref, f32[2,4,8,640]{3,2,1,0:T(8,128)S(1)} %get-tuple-element.115.side0_ref, ...), custom_call_target="tpu_custom_call" | custom-call | flops 8800000000 | bytes 4423712 | tf_op jit(solution)/shard_map/pallas_call | solution.py:139
  59.9 0.0 collective-permute-done.12.halo0_ref
  59.9 2.6 %shard_map.55 = (f32[2,2,4,8,640]{4,3,2,1,0:T(8,128)S(1)}, s32[2,2,2]{2,1,0:T(2,128)S(1)}) custom-call(f32[2,4,8,640]{3,2,1,0:T(8,128)S(1)} %get-tuple-element.115.side0_ref, f32[2,4,8,640]{3,2,1,0:T(8,128)S(1)} %get-tuple-element.116.side1_ref, f32[2,4,8,640]{3,2,1,0:T(8,128)S(1)} %collective-permute-done.12.halo0_ref, ...), custom_call_target="tpu_custom_call" | custom-call | flops 2640000000 | bytes 2785312 | tf_op jit(solution)/shard_map/pallas_call | solution.py:139
  62.5 0.1 collective-permute-start.14
  62.5 1.6 %collective-permute-done.14.partner_ref = f32[2,2,4,8,640]{4,3,2,1,0:T(8,128)S(1)} collective-permute-done((f32[2,2,4,8,640]{4,3,2,1,0:T(8,128)S(1)}, f32[2,2,4,8,640]{4,3,2,1,0:T(8,128)S(1)}, u32[]{:S(2)}, u32[]{:S(2)}) %collective-permute-start.14) | collective-permute-done | bytes 327712 | tf_op jit(solution)/shard_map/ppermute | solution.py:456
  64.2 0.1 collective-permute-start.15
  64.3 1.1 %shard_map.56 = (f32[2,4,8,640]{3,2,1,0:T(8,128)S(1)}, f32[2,4,8,640]{3,2,1,0:T(8,128)S(1)}) custom-call(f32[2,2,4,8,640]{4,3,2,1,0:T(8,128)S(1)} %get-tuple-element.123.own_ref, f32[2,2,4,8,640]{4,3,2,1,0:T(8,128)S(1)} %collective-permute-done.14.partner_ref, s32[2,2,2]{2,1,0:T(2,128)S(1)} %get-tuple-element.126.offset_ref, f32[4]{0:T(128)S(1)} %copy-done.3, ...), custom_call_target="tpu_custom_call" | custom-call | flops 1210000000 | bytes 2293808 | tf_op jit(solution)/shard_map/pallas_call | solution.py:139
  65.4 0.1 collective-permute-start.16
  65.4 1.9 %collective-permute-start.17 = (f32[2,4,8,640]{3,2,1,0:T(8,128)S(1)}, f32[2,4,8,640]{3,2,1,0:T(8,128)S(1)}, u32[]{:S(2)}, u32[]{:S(2)}) collective-permute-start(f32[2,4,8,640]{3,2,1,0:T(8,128)S(1)} %get-tuple-element.128.side1_ref), channel_id=1, source_target_pairs={{2,4},{3,5},{4,2},{5,3},{10,12},{11,13},{12,10},{13,11},{18,20},{1... | collective-permute-start | bytes 491528 | tf_op jit(solution)/shard_map/ppermute | solution.py:468
  67.4 0.0 collective-permute-done.15.partner_ref
  67.4 7.3 %shard_map.57 = (f32[2,24,8,640]{3,2,1,0:T(8,128)S(1)}, f32[2,2,3,2,8,640]{5,4,3,2,1,0:T(8,128)S(1)}) custom-call(f32[2,24,8,640]{3,2,1,0:T(8,128)S(1)} %get-tuple-element.124.own_ref, f32[2,24,8,640]{3,2,1,0:T(8,128)S(1)} %collective-permute-done.15.partner_ref, f32[2,4,8,640]{3,2,1,0:T(8,128)S(1)} %get-tuple-element.127.side0_ref, ...), custom_call_target="tpu_custom_call" | custom-call | flops 8800000000 | bytes 5079088 | tf_op jit(solution)/shard_map/pallas_call | solution.py:139
  74.7 0.0 collective-permute-done.16.halo0_ref
  74.7 0.0 collective-permute-done.17.halo1_ref
  74.7 2.1 %shard_map.58.own_ref.partner_ref = f32[2,2,4,8,640]{4,3,2,1,0:T(8,128)S(1)} custom-call(f32[2,4,8,640]{3,2,1,0:T(8,128)S(1)} %get-tuple-element.127.side0_ref, f32[2,4,8,640]{3,2,1,0:T(8,128)S(1)} %get-tuple-element.128.side1_ref, f32[2,4,8,640]{3,2,1,0:T(8,128)S(1)} %collective-permute-done.16.halo0_ref, ...), custom_call_target="tpu_custom_call" | custom-call | flops 2640000000 | bytes 1474560 | tf_op jit(solution)/shard_map/pallas_call | solution.py:139
  76.8 1.1 %shard_map.59 = (f32[2,4,8,640]{3,2,1,0:T(8,128)S(1)}, f32[2,4,8,640]{3,2,1,0:T(8,128)S(1)}) custom-call(f32[2,2,4,8,640]{4,3,2,1,0:T(8,128)S(1)} %shard_map.58.own_ref.partner_ref, f32[2,2,4,8,640]{4,3,2,1,0:T(8,128)S(1)} %shard_map.58.own_ref.partner_ref, s32[2,2,2]{2,1,0:T(2,128)S(1)} %get-tuple-element.126.offset_ref, f32[4]{0:T(128)S(1)} %copy-done.3, ...), custom_call_target="tpu_custom_call" | custom-call | flops 1210000000 | bytes 2293808 | tf_op jit(solution)/shard_map/pallas_call | solution.py:139
  77.9 0.8 collective-permute-start.21
  78.7 3.4 %collective-permute-start.22 = (f32[2,4,8,640]{3,2,1,0:T(8,128)S(1)}, f32[2,4,8,640]{3,2,1,0:T(8,128)S(1)}, u32[]{:S(2)}, u32[]{:S(2)}) collective-permute-start(f32[2,4,8,640]{3,2,1,0:T(8,128)S(1)} %get-tuple-element.132.side1_ref), channel_id=1, source_target_pairs={{2,4},{3,5},{4,2},{5,3},{10,12},{11,13},{12,10},{13,11},{18,20},{1... | collective-permute-start | bytes 491528 | tf_op jit(solution)/shard_map/ppermute | solution.py:468
  82.1 4.4 %shard_map.61 = (f32[12,8,512]{2,1,0:T(8,128)S(1)}, f32[12,8,512]{2,1,0:T(8,128)S(1)}, f32[2,1,3,2,8,640]{5,4,3,2,1,0:T(8,128)S(1)}) custom-call(f32[2,24,8,640]{3,2,1,0:T(8,128)S(1)} %get-tuple-element.129.own_ref.partner_ref, f32[2,24,8,640]{3,2,1,0:T(8,128)S(1)} %get-tuple-element.129.own_ref.partner_ref, ...), custom_call_target="tpu_custom_call" | custom-call | flops 4620000256 | bytes 4243504 | tf_op jit(solution)/shard_map/pallas_call | solution.py:139
  86.5 1.6 %collective-permute-start.20 = (f32[12,8,512]{2,1,0:T(8,128)S(1)}, f32[12,8,512]{2,1,0:T(8,128)S(1)}, u32[]{:S(2)}, u32[]{:S(2)}) collective-permute-start(f32[12,8,512]{2,1,0:T(8,128)S(1)} %get-tuple-element.136), channel_id=1, source_target_pairs={{0,17},{1,16},{2,19},{3,18},{4,21},{5,20},{6,23},{7,22},{8,25},{9,... | collective-permute-start | bytes 589832 | tf_op jit(solution)/shard_map/ppermute | solution.py:456
  88.1 4.4 %shard_map.60 = (f32[12,8,512]{2,1,0:T(8,128)S(1)}, f32[12,8,512]{2,1,0:T(8,128)S(1)}, f32[2,1,3,2,8,640]{5,4,3,2,1,0:T(8,128)S(1)}) custom-call(f32[2,24,8,640]{3,2,1,0:T(8,128)S(1)} %get-tuple-element.129.own_ref.partner_ref, f32[2,24,8,640]{3,2,1,0:T(8,128)S(1)} %get-tuple-element.129.own_ref.partner_ref, ...), custom_call_target="tpu_custom_call" | custom-call | flops 4620000256 | bytes 4243504 | tf_op jit(solution)/shard_map/pallas_call | solution.py:139
  92.5 1.5 %collective-permute-start.18 = (f32[12,8,512]{2,1,0:T(8,128)S(1)}, f32[12,8,512]{2,1,0:T(8,128)S(1)}, u32[]{:S(2)}, u32[]{:S(2)}) collective-permute-start(f32[12,8,512]{2,1,0:T(8,128)S(1)} %get-tuple-element.134), channel_id=1, source_target_pairs={{0,1},{1,0},{2,3},{3,2},{4,5},{5,4},{6,7},{7,6},{8,9},{9,8},{10,11... | collective-permute-start | bytes 589832 | tf_op jit(solution)/shard_map/ppermute | solution.py:456
  94.0 0.5 collective-permute-start.19
  94.6 0.0 collective-permute-done.21.halo0_ref
  94.6 2.4 %shard_map.62 = (f32[4,8,512]{2,1,0:T(8,128)S(1)}, f32[4,8,512]{2,1,0:T(8,128)S(1)}, f32[4,8,512]{2,1,0:T(8,128)S(1)}, f32[4,8,512]{2,1,0:T(8,128)S(1)}) custom-call(f32[2,4,8,640]{3,2,1,0:T(8,128)S(1)} %get-tuple-element.131.side0_ref, f32[2,4,8,640]{3,2,1,0:T(8,128)S(1)} %get-tuple-element.132.side1_ref, ...), custom_call_target="tpu_custom_call" | custom-call | flops 2750000128 | bytes 1409024 | tf_op jit(solution)/shard_map/pallas_call | solution.py:139
  97.0 0.7 collective-permute-start.23
  97.7 1.5 %collective-permute-start.24 = (f32[4,8,512]{2,1,0:T(8,128)S(1)}, f32[4,8,512]{2,1,0:T(8,128)S(1)}, u32[]{:S(2)}, u32[]{:S(2)}) collective-permute-start(f32[4,8,512]{2,1,0:T(8,128)S(1)} %get-tuple-element.143), channel_id=1, source_target_pairs={{0,16},{1,17},{2,18},{3,19},{4,20},{5,21},{6,22},{7,23},{8,24},{9,... | collective-permute-start | bytes 196616 | tf_op jit(solution)/shard_map/ppermute | solution.py:456
  99.2 1.4 %collective-permute-start.25 = (f32[4,8,512]{2,1,0:T(8,128)S(1)}, f32[4,8,512]{2,1,0:T(8,128)S(1)}, u32[]{:S(2)}, u32[]{:S(2)}) collective-permute-start(f32[4,8,512]{2,1,0:T(8,128)S(1)} %get-tuple-element.144), channel_id=1, source_target_pairs={{0,17},{1,16},{2,19},{3,18},{4,21},{5,20},{6,23},{7,22},{8,25},{9,... | collective-permute-start | bytes 196616 | tf_op jit(solution)/shard_map/ppermute | solution.py:456
  100.5 0.2 collective-permute-done.19.refs_2_
  100.8 1.3 %collective-permute-done.23.refs_5_ = f32[4,8,512]{2,1,0:T(8,128)S(1)} collective-permute-done((f32[4,8,512]{2,1,0:T(8,128)S(1)}, f32[4,8,512]{2,1,0:T(8,128)S(1)}, u32[]{:S(2)}, u32[]{:S(2)}) %collective-permute-start.23) | collective-permute-done | bytes 65568 | tf_op jit(solution)/shard_map/ppermute | solution.py:456
  102.0 0.4 collective-permute-done.24.refs_6_
  102.4 1.9 %collective-permute-done.25.refs_7_ = f32[4,8,512]{2,1,0:T(8,128)S(1)} collective-permute-done((f32[4,8,512]{2,1,0:T(8,128)S(1)}, f32[4,8,512]{2,1,0:T(8,128)S(1)}, u32[]{:S(2)}, u32[]{:S(2)}) %collective-permute-start.25) | collective-permute-done | bytes 65568 | tf_op jit(solution)/shard_map/ppermute | solution.py:456
  104.3 1.1 %shard_map.63 = f32[16,8,2048]{2,1,0:T(8,128)} custom-call(f32[12,8,512]{2,1,0:T(8,128)S(1)} %get-tuple-element.133.refs_0_, f32[12,8,512]{2,1,0:T(8,128)S(1)} %collective-permute-done.18.refs_1_, f32[12,8,512]{2,1,0:T(8,128)S(1)} %collective-permute-done.19.refs_2_, f32[12,8,512]{2,1,0:T(8,128)S(1)} %collective-permute-done.20.refs_3_, ...), custom_call_target="tpu_custom_call" | custom-call | flops 1100000000 | bytes 2097152 | tf_op jit(solution)/shard_map/pallas_call | solution.py:139
  (15 shorter events, 0.1 us)
Async XLA Ops:
  0.0 5.1 %copy-start = (f32[1,4,4,16,2048]{4,3,2,1,0:T(8,128)S(1)}, f32[1,4,4,16,2048]{4,3,2,1,0:T(8,128)}, u32[]{:S(2)}) copy-start(f32[1,4,4,16,2048]{4,3,2,1,0:T(8,128)} %coeff_ref.3) | copy-start | bytes 6291460
  0.0 5.1 %copy-start.1 = (f32[1,16,8,2048]{3,2,1,0:T(8,128)S(1)}, f32[1,16,8,2048]{3,2,1,0:T(8,128)}, u32[]{:S(2)}) copy-start(f32[1,16,8,2048]{3,2,1,0:T(8,128)} %param.4) | copy-start | bytes 3145732
  0.0 5.1 %copy-start.2 = (s32[1,1,4]{2,1,0:T(1,128)S(1)}, s32[1,1,4]{2,1,0:T(1,128)}, u32[]{:S(2)}) copy-start(s32[1,1,4]{2,1,0:T(1,128)} %offset_ref.3) | copy-start | bytes 52
  0.0 5.2 %copy-start.3 = (f32[4]{0:T(128)S(1)}, f32[4]{0:T(128)}, u32[]{:S(2)}) copy-start(f32[4]{0:T(128)} %level_ref.15) | copy-start | bytes 52
  0.0 5.1 %collective-permute-start = (f32[16,8,2048]{2,1,0:T(8,128)}, f32[16,8,2048]{2,1,0:T(8,128)S(1)}, u32[]{:S(2)}, u32[]{:S(2)}) collective-permute-start(f32[16,8,2048]{2,1,0:T(8,128)} %bitcast.4), channel_id=1, source_target_pairs={{0,8},{1,9},{2,10},{3,11},{4,12},{5,13},{6,14},{7,15},{8,0},{9,1},... | collective-permute-start | bytes 3145736 | tf_op jit(solution)/shard_map/ppermute | solution.py:456
  1.6 7.2 %collective-permute-start.1 = (f32[4,16,640]{2,1,0:T(8,128)S(1)}, f32[4,16,640]{2,1,0:T(8,128)S(1)}, u32[]{:S(2)}, u32[]{:S(2)}) collective-permute-start(f32[4,16,640]{2,1,0:T(8,128)S(1)} %get-tuple-element.80), channel_id=1, source_target_pairs={{0,1},{1,0},{2,3},{3,2},{4,5},{5,4},{6,7},{7,6},{8,9},{9,8},{10,11... | collective-permute-start | bytes 491528 | tf_op jit(solution)/shard_map/ppermute | solution.py:456
  3.2 7.0 %collective-permute-start.2 = (f32[4,16,640]{2,1,0:T(8,128)S(1)}, f32[4,16,640]{2,1,0:T(8,128)S(1)}, u32[]{:S(2)}, u32[]{:S(2)}) collective-permute-start(f32[4,16,640]{2,1,0:T(8,128)S(1)} %get-tuple-element.81), channel_id=1, source_target_pairs={{0,16},{1,17},{2,18},{3,19},{4,20},{5,21},{6,22},{7,23},{8,24},{9,... | collective-permute-start | bytes 491528 | tf_op jit(solution)/shard_map/ppermute | solution.py:456
  4.7 8.3 %collective-permute-start.3 = (f32[4,16,640]{2,1,0:T(8,128)S(1)}, f32[4,16,640]{2,1,0:T(8,128)S(1)}, u32[]{:S(2)}, u32[]{:S(2)}) collective-permute-start(f32[4,16,640]{2,1,0:T(8,128)S(1)} %get-tuple-element.82), channel_id=1, source_target_pairs={{0,17},{1,16},{2,19},{3,18},{4,21},{5,20},{6,23},{7,22},{8,25},{9,... | collective-permute-start | bytes 491528 | tf_op jit(solution)/shard_map/ppermute | solution.py:456
  13.0 9.1 %collective-permute-start.4 = (f32[16,8,640]{2,1,0:T(8,128)S(1)}, f32[16,8,640]{2,1,0:T(8,128)S(1)}, u32[]{:S(2)}, u32[]{:S(2)}) collective-permute-start(f32[16,8,640]{2,1,0:T(8,128)S(1)} %get-tuple-element.84), channel_id=1, source_target_pairs={{0,1},{1,0},{2,3},{3,2},{4,5},{5,4},{6,7},{7,6},{8,9},{9,8},{10,11... | collective-permute-start | bytes 983048 | tf_op jit(solution)/shard_map/ppermute | solution.py:456
  14.5 8.8 %collective-permute-start.5 = (f32[16,8,640]{2,1,0:T(8,128)S(1)}, f32[16,8,640]{2,1,0:T(8,128)S(1)}, u32[]{:S(2)}, u32[]{:S(2)}) collective-permute-start(f32[16,8,640]{2,1,0:T(8,128)S(1)} %get-tuple-element.85), channel_id=1, source_target_pairs={{0,16},{1,17},{2,18},{3,19},{4,20},{5,21},{6,22},{7,23},{8,24},{9,... | collective-permute-start | bytes 983048 | tf_op jit(solution)/shard_map/ppermute | solution.py:456
  23.3 8.8 %collective-permute-start.6 = (f32[16,8,640]{2,1,0:T(8,128)S(1)}, f32[16,8,640]{2,1,0:T(8,128)S(1)}, u32[]{:S(2)}, u32[]{:S(2)}) collective-permute-start(f32[16,8,640]{2,1,0:T(8,128)S(1)} %get-tuple-element.87), channel_id=1, source_target_pairs={{0,17},{1,16},{2,19},{3,18},{4,21},{5,20},{6,23},{7,22},{8,25},{9,... | collective-permute-start | bytes 983048 | tf_op jit(solution)/shard_map/ppermute | solution.py:456
  32.2 15.2 %collective-permute-start.7 = (f32[2,4,16,640]{3,2,1,0:T(8,128)S(1)}, f32[2,4,16,640]{3,2,1,0:T(8,128)S(1)}, u32[]{:S(2)}, u32[]{:S(2)}) collective-permute-start(f32[2,4,16,640]{3,2,1,0:T(8,128)S(1)} %get-tuple-element.101), channel_id=1, source_target_pairs={{0,1},{1,0},{2,3},{3,2},{4,5},{5,4},{6,7},{7,6},{8,9},{9,8},{10,11... | collective-permute-start | bytes 983048 | tf_op jit(solution)/shard_map/ppermute | solution.py:456
  32.8 14.6 %collective-permute-start.8 = (f32[2,4,16,640]{3,2,1,0:T(8,128)S(1)}, f32[2,4,16,640]{3,2,1,0:T(8,128)S(1)}, u32[]{:S(2)}, u32[]{:S(2)}) collective-permute-start(f32[2,4,16,640]{3,2,1,0:T(8,128)S(1)} %get-tuple-element.102), channel_id=1, source_target_pairs={{0,16},{1,17},{2,18},{3,19},{4,20},{5,21},{6,22},{7,23},{8,24},{9,... | collective-permute-start | bytes 983048 | tf_op jit(solution)/shard_map/ppermute | solution.py:456
  34.3 13.1 %collective-permute-start.9 = (f32[2,4,16,640]{3,2,1,0:T(8,128)S(1)}, f32[2,4,16,640]{3,2,1,0:T(8,128)S(1)}, u32[]{:S(2)}, u32[]{:S(2)}) collective-permute-start(f32[2,4,16,640]{3,2,1,0:T(8,128)S(1)} %get-tuple-element.103), channel_id=1, source_target_pairs={{0,17},{1,16},{2,19},{3,18},{4,21},{5,20},{6,23},{7,22},{8,25},{9,... | collective-permute-start | bytes 983048 | tf_op jit(solution)/shard_map/ppermute | solution.py:456
  35.7 8.1 %collective-permute-start.10 = (f32[2,4,8,640]{3,2,1,0:T(8,128)S(1)}, f32[2,4,8,640]{3,2,1,0:T(8,128)S(1)}, u32[]{:S(2)}, u32[]{:S(2)}) collective-permute-start(f32[2,4,8,640]{3,2,1,0:T(8,128)S(1)} %get-tuple-element.104.side0_ref), channel_id=1, source_target_pairs={{0,2},{1,3},{2,0},{3,1},{4,6},{5,7},{6,4},{7,5},{8,10},{9,11},{10,... | collective-permute-start | bytes 491528 | tf_op jit(solution)/shard_map/ppermute | solution.py:468
  36.2 7.9 %collective-permute-start.11 = (f32[2,4,8,640]{3,2,1,0:T(8,128)S(1)}, f32[2,4,8,640]{3,2,1,0:T(8,128)S(1)}, u32[]{:S(2)}, u32[]{:S(2)}) collective-permute-start(f32[2,4,8,640]{3,2,1,0:T(8,128)S(1)} %get-tuple-element.105.side1_ref), channel_id=1, source_target_pairs={{2,4},{3,5},{4,2},{5,3},{10,12},{11,13},{12,10},{13,11},{18,20},{1... | collective-permute-start | bytes 491528 | tf_op jit(solution)/shard_map/ppermute | solution.py:468
  47.4 12.5 %collective-permute-start.12 = (f32[2,4,8,640]{3,2,1,0:T(8,128)S(1)}, f32[2,4,8,640]{3,2,1,0:T(8,128)S(1)}, u32[]{:S(2)}, u32[]{:S(2)}) collective-permute-start(f32[2,4,8,640]{3,2,1,0:T(8,128)S(1)} %get-tuple-element.115.side0_ref), channel_id=1, source_target_pairs={{0,2},{1,3},{2,0},{3,1},{4,6},{5,7},{6,4},{7,5},{8,10},{9,11},{10,... | collective-permute-start | bytes 491528 | tf_op jit(solution)/shard_map/ppermute | solution.py:468
  47.8 12.1 %collective-permute-start.13 = (f32[2,4,8,640]{3,2,1,0:T(8,128)S(1)}, f32[2,4,8,640]{3,2,1,0:T(8,128)S(1)}, u32[]{:S(2)}, u32[]{:S(2)}) collective-permute-start(f32[2,4,8,640]{3,2,1,0:T(8,128)S(1)} %get-tuple-element.116.side1_ref), channel_id=1, source_target_pairs={{2,4},{3,5},{4,2},{5,3},{10,12},{11,13},{12,10},{13,11},{18,20},{1... | collective-permute-start | bytes 491528 | tf_op jit(solution)/shard_map/ppermute | solution.py:468
  62.5 1.7 %collective-permute-start.14 = (f32[2,2,4,8,640]{4,3,2,1,0:T(8,128)S(1)}, f32[2,2,4,8,640]{4,3,2,1,0:T(8,128)S(1)}, u32[]{:S(2)}, u32[]{:S(2)}) collective-permute-start(f32[2,2,4,8,640]{4,3,2,1,0:T(8,128)S(1)} %get-tuple-element.123.own_ref), channel_id=1, source_target_pairs={{0,8},{1,9},{2,10},{3,11},{4,12},{5,13},{6,14},{7,15},{8,0},{9,1},... | collective-permute-start | bytes 983048 | tf_op jit(solution)/shard_map/ppermute | solution.py:456
  64.2 3.2 %collective-permute-start.15 = (f32[2,24,8,640]{3,2,1,0:T(8,128)S(1)}, f32[2,24,8,640]{3,2,1,0:T(8,128)S(1)}, u32[]{:S(2)}, u32[]{:S(2)}) collective-permute-start(f32[2,24,8,640]{3,2,1,0:T(8,128)S(1)} %get-tuple-element.124.own_ref), channel_id=1, source_target_pairs={{0,8},{1,9},{2,10},{3,11},{4,12},{5,13},{6,14},{7,15},{8,0},{9,1},... | collective-permute-start | bytes 2949128 | tf_op jit(solution)/shard_map/ppermute | solution.py:456
  65.4 9.3 %collective-permute-start.16 = (f32[2,4,8,640]{3,2,1,0:T(8,128)S(1)}, f32[2,4,8,640]{3,2,1,0:T(8,128)S(1)}, u32[]{:S(2)}, u32[]{:S(2)}) collective-permute-start(f32[2,4,8,640]{3,2,1,0:T(8,128)S(1)} %get-tuple-element.127.side0_ref), channel_id=1, source_target_pairs={{0,2},{1,3},{2,0},{3,1},{4,6},{5,7},{6,4},{7,5},{8,10},{9,11},{10,... | collective-permute-start | bytes 491528 | tf_op jit(solution)/shard_map/ppermute | solution.py:468
  65.4 9.2 %collective-permute-start.17 = (f32[2,4,8,640]{3,2,1,0:T(8,128)S(1)}, f32[2,4,8,640]{3,2,1,0:T(8,128)S(1)}, u32[]{:S(2)}, u32[]{:S(2)}) collective-permute-start(f32[2,4,8,640]{3,2,1,0:T(8,128)S(1)} %get-tuple-element.128.side1_ref), channel_id=1, source_target_pairs={{2,4},{3,5},{4,2},{5,3},{10,12},{11,13},{12,10},{13,11},{18,20},{1... | collective-permute-start | bytes 491528 | tf_op jit(solution)/shard_map/ppermute | solution.py:468
  77.9 16.7 %collective-permute-start.21 = (f32[2,4,8,640]{3,2,1,0:T(8,128)S(1)}, f32[2,4,8,640]{3,2,1,0:T(8,128)S(1)}, u32[]{:S(2)}, u32[]{:S(2)}) collective-permute-start(f32[2,4,8,640]{3,2,1,0:T(8,128)S(1)} %get-tuple-element.131.side0_ref), channel_id=1, source_target_pairs={{0,2},{1,3},{2,0},{3,1},{4,6},{5,7},{6,4},{7,5},{8,10},{9,11},{10,... | collective-permute-start | bytes 491528 | tf_op jit(solution)/shard_map/ppermute | solution.py:468
  78.7 15.9 %collective-permute-start.22 = (f32[2,4,8,640]{3,2,1,0:T(8,128)S(1)}, f32[2,4,8,640]{3,2,1,0:T(8,128)S(1)}, u32[]{:S(2)}, u32[]{:S(2)}) collective-permute-start(f32[2,4,8,640]{3,2,1,0:T(8,128)S(1)} %get-tuple-element.132.side1_ref), channel_id=1, source_target_pairs={{2,4},{3,5},{4,2},{5,3},{10,12},{11,13},{12,10},{13,11},{18,20},{1... | collective-permute-start | bytes 491528 | tf_op jit(solution)/shard_map/ppermute | solution.py:468
  86.5 8.0 %collective-permute-start.20 = (f32[12,8,512]{2,1,0:T(8,128)S(1)}, f32[12,8,512]{2,1,0:T(8,128)S(1)}, u32[]{:S(2)}, u32[]{:S(2)}) collective-permute-start(f32[12,8,512]{2,1,0:T(8,128)S(1)} %get-tuple-element.136), channel_id=1, source_target_pairs={{0,17},{1,16},{2,19},{3,18},{4,21},{5,20},{6,23},{7,22},{8,25},{9,... | collective-permute-start | bytes 589832 | tf_op jit(solution)/shard_map/ppermute | solution.py:456
  92.5 8.0 %collective-permute-start.18 = (f32[12,8,512]{2,1,0:T(8,128)S(1)}, f32[12,8,512]{2,1,0:T(8,128)S(1)}, u32[]{:S(2)}, u32[]{:S(2)}) collective-permute-start(f32[12,8,512]{2,1,0:T(8,128)S(1)} %get-tuple-element.134), channel_id=1, source_target_pairs={{0,1},{1,0},{2,3},{3,2},{4,5},{5,4},{6,7},{7,6},{8,9},{9,8},{10,11... | collective-permute-start | bytes 589832 | tf_op jit(solution)/shard_map/ppermute | solution.py:456
  94.0 6.7 %collective-permute-start.19 = (f32[12,8,512]{2,1,0:T(8,128)S(1)}, f32[12,8,512]{2,1,0:T(8,128)S(1)}, u32[]{:S(2)}, u32[]{:S(2)}) collective-permute-start(f32[12,8,512]{2,1,0:T(8,128)S(1)} %get-tuple-element.135), channel_id=1, source_target_pairs={{0,16},{1,17},{2,18},{3,19},{4,20},{5,21},{6,22},{7,23},{8,24},{9,... | collective-permute-start | bytes 589832 | tf_op jit(solution)/shard_map/ppermute | solution.py:456
  97.0 5.0 %collective-permute-start.23 = (f32[4,8,512]{2,1,0:T(8,128)S(1)}, f32[4,8,512]{2,1,0:T(8,128)S(1)}, u32[]{:S(2)}, u32[]{:S(2)}) collective-permute-start(f32[4,8,512]{2,1,0:T(8,128)S(1)} %get-tuple-element.142), channel_id=1, source_target_pairs={{0,1},{1,0},{2,3},{3,2},{4,5},{5,4},{6,7},{7,6},{8,9},{9,8},{10,11... | collective-permute-start | bytes 196616 | tf_op jit(solution)/shard_map/ppermute | solution.py:456
  97.7 4.7 %collective-permute-start.24 = (f32[4,8,512]{2,1,0:T(8,128)S(1)}, f32[4,8,512]{2,1,0:T(8,128)S(1)}, u32[]{:S(2)}, u32[]{:S(2)}) collective-permute-start(f32[4,8,512]{2,1,0:T(8,128)S(1)} %get-tuple-element.143), channel_id=1, source_target_pairs={{0,16},{1,17},{2,18},{3,19},{4,20},{5,21},{6,22},{7,23},{8,24},{9,... | collective-permute-start | bytes 196616 | tf_op jit(solution)/shard_map/ppermute | solution.py:456
  99.2 5.2 %collective-permute-start.25 = (f32[4,8,512]{2,1,0:T(8,128)S(1)}, f32[4,8,512]{2,1,0:T(8,128)S(1)}, u32[]{:S(2)}, u32[]{:S(2)}) collective-permute-start(f32[4,8,512]{2,1,0:T(8,128)S(1)} %get-tuple-element.144), channel_id=1, source_target_pairs={{0,17},{1,16},{2,19},{3,18},{4,21},{5,20},{6,23},{7,22},{8,25},{9,... | collective-permute-start | bytes 196616 | tf_op jit(solution)/shard_map/ppermute | solution.py:456

commit v3 on v2

--- a/solution.py
+++ b/solution.py
@@ -526,7 +526,8 @@
         )
         used = table, thresholds, *coeff
         if section == 1:
-            late, side0, side1 = lax.optimization_barrier((late, side0, side1))
+            late, own = lax.optimization_barrier((late, own))
+            partner = own
             coeff = late
         halo0, halo1 = halo(side0, side1)
         if section == SECTIONS - 1:

time: 106 us -> 105 us (level)
  starting transfers between devices: 35.5 us -> 32.5 us
  waiting for transfers between devices: 20.6 us -> 22.9 us
    ppermute x18, waiting for transfers between devices: 20.4 us -> 22.9 us  [swap(): return lax.ppermute(value, axes, route(frame_bits, slab_bits))]
    ppermute x4, starting transfers between devices: 14.7 us -> 12.3 us  [halo(): lax.ppermute(side1, 'space', second)]
  transfers between devices with their start and end apart: 26 -> 26, of which waited for: 11 -> 10; matrix products, arithmetic and copies ran while one was open for 1% -> 1% of each run, Pallas kernels for 39% -> 39%
where the time goes in v3:
time: 105 us
  Pallas kernels  47.7 us (45%)
  starting transfers between devices  32.5 us (31%)
  waiting for transfers between devices  22.9 us (22%)
  local copies, waits for them, and re-layouts  1.24 us (1%)
    pallas_call x18, Pallas kernels, call(): pl.pallas_call(body, out_shape=outs, in_specs=in_specs, out_specs=out_spe...  47.7 us
    ppermute x18, waiting for transfers between devices, swap(): return lax.ppermute(value, axes, route(frame_bits, slab_bits))  22.9 us
    ppermute x18, starting transfers between devices, swap(): return lax.ppermute(value, axes, route(frame_bits, slab_bits))  19 us
    ppermute x4, starting transfers between devices, halo(): lax.ppermute(side1, 'space', second)  12.3 us
  transfers between devices with their start and end apart: 26, of which 10 were waited for; matrix products, arithmetic and copies ran while one was open for 1% of the time, Pallas kernels for 39%

profile of v3, /device:TPU:8, one launch (start us, length us, event | category | flops | bytes accessed | tf_op | source)
XLA Modules:
  0.0 104.7 jit_solution(3160513912968493614)
XLA Ops:
  0.0 0.1 collective-permute-start
  0.1 1.2 %slice_bitcast_fusion.coeff_ref = f32[4,16,2048]{2,1,0:T(8,128)S(1)} fusion(f32[1,4,4,16,2048]{4,3,2,1,0:T(8,128)} %coeff_ref.3), kind=kLoop, calls=%fused_computation | loop fusion | bytes 1048576 | tf_op jit(solution)/shard_map/squeeze | solution.py:479
  1.3 0.2 shard_map.48
  1.6 1.6 %collective-permute-start.1 = (f32[4,16,640]{2,1,0:T(8,128)S(1)}, f32[4,16,640]{2,1,0:T(8,128)S(1)}, u32[]{:S(2)}, u32[]{:S(2)}) collective-permute-start(f32[4,16,640]{2,1,0:T(8,128)S(1)} %get-tuple-element.83), channel_id=1, source_target_pairs={{0,1},{1,0},{2,3},{3,2},{4,5},{5,4},{6,7},{7,6},{8,9},{9,8},{10,11... | collective-permute-start | bytes 491528 | tf_op jit(solution)/shard_map/ppermute | solution.py:456
  3.2 1.5 %collective-permute-start.2 = (f32[4,16,640]{2,1,0:T(8,128)S(1)}, f32[4,16,640]{2,1,0:T(8,128)S(1)}, u32[]{:S(2)}, u32[]{:S(2)}) collective-permute-start(f32[4,16,640]{2,1,0:T(8,128)S(1)} %get-tuple-element.84), channel_id=1, source_target_pairs={{0,16},{1,17},{2,18},{3,19},{4,20},{5,21},{6,22},{7,23},{8,24},{9,... | collective-permute-start | bytes 491528 | tf_op jit(solution)/shard_map/ppermute | solution.py:456
  4.7 0.5 collective-permute-start.3
  5.1 0.0 collective-permute-done.partner_ref
  5.2 3.6 %shard_map.47 = (f32[16,8,640]{2,1,0:T(8,128)S(1)}, f32[16,8,640]{2,1,0:T(8,128)S(1)}, f32[16,8,640]{2,1,0:T(8,128)S(1)}, f32[16,8,640]{2,1,0:T(8,128)S(1)}) custom-call(f32[16,8,2048]{2,1,0:T(8,128)S(1)} %bitcast.5, f32[16,8,2048]{2,1,0:T(8,128)S(1)} %collective-permute-done.partner_ref, f32[1,4,4,16,2048]{4,3,2,1,0:T(8,128)S(1)} %copy-done, ...), custom_call_target="tpu_custom_call" | custom-call | flops 4400000000 | bytes 5505056 | tf_op jit(solution)/shard_map/pallas_call | solution.py:139
  8.7 0.0 collective-permute-done.1.refs_1_
  8.7 1.5 %collective-permute-done.2.refs_2_ = f32[4,16,640]{2,1,0:T(8,128)S(1)} collective-permute-done((f32[4,16,640]{2,1,0:T(8,128)S(1)}, f32[4,16,640]{2,1,0:T(8,128)S(1)}, u32[]{:S(2)}, u32[]{:S(2)}) %collective-permute-start.2) | collective-permute-done | bytes 163872 | tf_op jit(solution)/shard_map/ppermute | solution.py:456
  10.2 2.8 %collective-permute-done.3.refs_3_ = f32[4,16,640]{2,1,0:T(8,128)S(1)} collective-permute-done((f32[4,16,640]{2,1,0:T(8,128)S(1)}, f32[4,16,640]{2,1,0:T(8,128)S(1)}, u32[]{:S(2)}, u32[]{:S(2)}) %collective-permute-start.3) | collective-permute-done | bytes 163872 | tf_op jit(solution)/shard_map/ppermute | solution.py:456
  13.0 1.5 %collective-permute-start.4 = (f32[16,8,640]{2,1,0:T(8,128)S(1)}, f32[16,8,640]{2,1,0:T(8,128)S(1)}, u32[]{:S(2)}, u32[]{:S(2)}) collective-permute-start(f32[16,8,640]{2,1,0:T(8,128)S(1)} %get-tuple-element.88), channel_id=1, source_target_pairs={{0,1},{1,0},{2,3},{3,2},{4,5},{5,4},{6,7},{7,6},{8,9},{9,8},{10,11... | collective-permute-start | bytes 983048 | tf_op jit(solution)/shard_map/ppermute | solution.py:456
  14.5 1.5 %collective-permute-start.5 = (f32[16,8,640]{2,1,0:T(8,128)S(1)}, f32[16,8,640]{2,1,0:T(8,128)S(1)}, u32[]{:S(2)}, u32[]{:S(2)}) collective-permute-start(f32[16,8,640]{2,1,0:T(8,128)S(1)} %get-tuple-element.89), channel_id=1, source_target_pairs={{0,16},{1,17},{2,18},{3,19},{4,20},{5,21},{6,22},{7,23},{8,24},{9,... | collective-permute-start | bytes 983048 | tf_op jit(solution)/shard_map/ppermute | solution.py:456
  16.0 0.9 shard_map.46
  17.0 5.1 %collective-permute-done.4.other_ref.near_ref.refs_1_ = f32[16,8,640]{2,1,0:T(8,128)S(1)} collective-permute-done((f32[16,8,640]{2,1,0:T(8,128)S(1)}, f32[16,8,640]{2,1,0:T(8,128)S(1)}, u32[]{:S(2)}, u32[]{:S(2)}) %collective-permute-start.4) | collective-permute-done | bytes 327712 | tf_op jit(solution)/shard_map/ppermute | solution.py:456
  22.1 1.2 %collective-permute-done.5.far_ref.own_ref.refs_2_ = f32[16,8,640]{2,1,0:T(8,128)S(1)} collective-permute-done((f32[16,8,640]{2,1,0:T(8,128)S(1)}, f32[16,8,640]{2,1,0:T(8,128)S(1)}, u32[]{:S(2)}, u32[]{:S(2)}) %collective-permute-start.5) | collective-permute-done | bytes 327712 | tf_op jit(solution)/shard_map/ppermute | solution.py:456
  23.3 1.4 %collective-permute-start.6 = (f32[16,8,640]{2,1,0:T(8,128)S(1)}, f32[16,8,640]{2,1,0:T(8,128)S(1)}, u32[]{:S(2)}, u32[]{:S(2)}) collective-permute-start(f32[16,8,640]{2,1,0:T(8,128)S(1)} %get-tuple-element.92), channel_id=1, source_target_pairs={{0,17},{1,16},{2,19},{3,18},{4,21},{5,20},{6,23},{7,22},{8,25},{9,... | collective-permute-start | bytes 983048 | tf_op jit(solution)/shard_map/ppermute | solution.py:456
  24.8 3.0 %shard_map.49 = (f32[2,24,8,640]{3,2,1,0:T(8,128)S(1)}, f32[2,2,3,2,8,640]{5,4,3,2,1,0:T(8,128)S(1)}) custom-call(f32[16,8,640]{2,1,0:T(8,128)S(1)} %get-tuple-element.86.own_ref.self_ref.refs_0_, f32[16,8,640]{2,1,0:T(8,128)S(1)} %collective-permute-done.4.other_ref.near_ref.refs_1_), custom_call_target="tpu_custom_call" | custom-call | flops 3849999872 | bytes 2129920 | tf_op jit(solution)/shard_map/pallas_call | solution.py:139
  27.8 4.3 %collective-permute-done.6.across_ref.other_ref.refs_3_ = f32[16,8,640]{2,1,0:T(8,128)S(1)} collective-permute-done((f32[16,8,640]{2,1,0:T(8,128)S(1)}, f32[16,8,640]{2,1,0:T(8,128)S(1)}, u32[]{:S(2)}, u32[]{:S(2)}) %collective-permute-start.6) | collective-permute-done | bytes 327712 | tf_op jit(solution)/shard_map/ppermute | solution.py:456
  32.2 0.5 collective-permute-start.10
  32.7 4.6 %collective-permute-start.11 = (f32[2,4,8,640]{3,2,1,0:T(8,128)S(1)}, f32[2,4,8,640]{3,2,1,0:T(8,128)S(1)}, u32[]{:S(2)}, u32[]{:S(2)}) collective-permute-start(f32[2,4,8,640]{3,2,1,0:T(8,128)S(1)} %get-tuple-element.105.side1_ref), channel_id=1, source_target_pairs={{2,4},{3,5},{4,2},{5,3},{10,12},{11,13},{12,10},{13,11},{18,20},{1... | collective-permute-start | bytes 491528 | tf_op jit(solution)/shard_map/ppermute | solution.py:468
  37.3 0.6 collective-permute-start.7
  37.9 1.5 %collective-permute-start.8 = (f32[2,4,16,640]{3,2,1,0:T(8,128)S(1)}, f32[2,4,16,640]{3,2,1,0:T(8,128)S(1)}, u32[]{:S(2)}, u32[]{:S(2)}) collective-permute-start(f32[2,4,16,640]{3,2,1,0:T(8,128)S(1)} %get-tuple-element.98), channel_id=1, source_target_pairs={{0,16},{1,17},{2,18},{3,19},{4,20},{5,21},{6,22},{7,23},{8,24},{9,... | collective-permute-start | bytes 983048 | tf_op jit(solution)/shard_map/ppermute | solution.py:456
  39.4 1.4 %collective-permute-start.9 = (f32[2,4,16,640]{3,2,1,0:T(8,128)S(1)}, f32[2,4,16,640]{3,2,1,0:T(8,128)S(1)}, u32[]{:S(2)}, u32[]{:S(2)}) collective-permute-start(f32[2,4,16,640]{3,2,1,0:T(8,128)S(1)} %get-tuple-element.99), channel_id=1, source_target_pairs={{0,17},{1,16},{2,19},{3,18},{4,21},{5,20},{6,23},{7,22},{8,25},{9,... | collective-permute-start | bytes 983048 | tf_op jit(solution)/shard_map/ppermute | solution.py:456
  40.8 3.0 %shard_map.51 = (f32[2,24,8,640]{3,2,1,0:T(8,128)S(1)}, f32[2,2,3,2,8,640]{5,4,3,2,1,0:T(8,128)S(1)}) custom-call(f32[16,8,640]{2,1,0:T(8,128)S(1)} %collective-permute-done.5.far_ref.own_ref.refs_2_, f32[16,8,640]{2,1,0:T(8,128)S(1)} %collective-permute-done.6.across_ref.other_ref.refs_3_, ...), custom_call_target="tpu_custom_call", output_to_operand_aliasing={{0}: (2, {}), {1}: (3, {})} | custom-call | flops 3849999872 | bytes 3604480 | tf_op jit(solution)/shard_map/pallas_call | solution.py:139
  43.9 0.0 collective-permute-done.10.halo0_ref
  43.9 2.2 %shard_map.52 = (f32[2,2,4,8,640]{4,3,2,1,0:T(8,128)S(1)}, s32[1,2,2]{2,1,0:T(2,128)S(1)}) custom-call(f32[2,4,8,640]{3,2,1,0:T(8,128)S(1)} %get-tuple-element.104.side0_ref, f32[2,4,8,640]{3,2,1,0:T(8,128)S(1)} %get-tuple-element.105.side1_ref, f32[2,4,8,640]{3,2,1,0:T(8,128)S(1)} %collective-permute-done.10.halo0_ref, ...), custom_call_target="tpu_custom_call" | custom-call | flops 2640000000 | bytes 2785296 | tf_op jit(solution)/shard_map/pallas_call | solution.py:139
  46.1 1.1 %shard_map.53 = (f32[2,4,8,640]{3,2,1,0:T(8,128)S(1)}, f32[2,4,8,640]{3,2,1,0:T(8,128)S(1)}) custom-call(f32[2,2,4,8,640]{4,3,2,1,0:T(8,128)S(1)} %get-tuple-element.107.own_ref.partner_ref, f32[2,2,4,8,640]{4,3,2,1,0:T(8,128)S(1)} %get-tuple-element.107.own_ref.partner_ref, s32[1,2,2]{2,1,0:T(2,128)S(1)} %get-tuple-element.108.offset_ref, f32[4]{0:T(128)S(1)} %copy-done.3, ...), custom_call_target="tpu_custom_call" | custom-call | flops 1210000000 | bytes 1638432 | tf_op jit(solution)/shard_map/pallas_call | solution.py:139
  47.2 0.1 collective-permute-start.12
  47.3 2.1 %collective-permute-start.13 = (f32[2,4,8,640]{3,2,1,0:T(8,128)S(1)}, f32[2,4,8,640]{3,2,1,0:T(8,128)S(1)}, u32[]{:S(2)}, u32[]{:S(2)}) collective-permute-start(f32[2,4,8,640]{3,2,1,0:T(8,128)S(1)} %get-tuple-element.114.side1_ref), channel_id=1, source_target_pairs={{2,4},{3,5},{4,2},{5,3},{10,12},{11,13},{12,10},{13,11},{18,20},{1... | collective-permute-start | bytes 491528 | tf_op jit(solution)/shard_map/ppermute | solution.py:468
  49.4 0.0 collective-permute-done.7.refs_1_
  49.4 0.0 collective-permute-done.8.refs_2_
  49.4 2.6 %collective-permute-done.9.refs_3_ = f32[2,4,16,640]{3,2,1,0:T(8,128)S(1)} collective-permute-done((f32[2,4,16,640]{3,2,1,0:T(8,128)S(1)}, f32[2,4,16,640]{3,2,1,0:T(8,128)S(1)}, u32[]{:S(2)}, u32[]{:S(2)}) %collective-permute-start.9) | collective-permute-done | bytes 327712 | tf_op jit(solution)/shard_map/ppermute | solution.py:456
  52.0 7.2 %shard_map.54 = (f32[2,24,8,640]{3,2,1,0:T(8,128)S(1)}, f32[2,2,3,2,8,640]{5,4,3,2,1,0:T(8,128)S(1)}) custom-call(f32[2,24,8,640]{3,2,1,0:T(8,128)S(1)} %get-tuple-element.103.own_ref.partner_ref, f32[2,24,8,640]{3,2,1,0:T(8,128)S(1)} %get-tuple-element.103.own_ref.partner_ref, f32[2,4,8,640]{3,2,1,0:T(8,128)S(1)} %get-tuple-element.113.side0_ref, ...), custom_call_target="tpu_custom_call" | custom-call | flops 8800000000 | bytes 4423712 | tf_op jit(solution)/shard_map/pallas_call | solution.py:139
  59.2 0.0 collective-permute-done.12.halo0_ref
  59.3 0.0 collective-permute-done.13.halo1_ref
  59.3 2.6 %shard_map.55 = (f32[2,2,4,8,640]{4,3,2,1,0:T(8,128)S(1)}, s32[2,2,2]{2,1,0:T(2,128)S(1)}) custom-call(f32[2,4,8,640]{3,2,1,0:T(8,128)S(1)} %get-tuple-element.113.side0_ref, f32[2,4,8,640]{3,2,1,0:T(8,128)S(1)} %get-tuple-element.114.side1_ref, f32[2,4,8,640]{3,2,1,0:T(8,128)S(1)} %collective-permute-done.12.halo0_ref, ...), custom_call_target="tpu_custom_call" | custom-call | flops 2640000000 | bytes 2785312 | tf_op jit(solution)/shard_map/pallas_call | solution.py:139
  61.8 0.1 collective-permute-start.14
  61.9 1.6 %collective-permute-done.14.partner_ref = f32[2,2,4,8,640]{4,3,2,1,0:T(8,128)S(1)} collective-permute-done((f32[2,2,4,8,640]{4,3,2,1,0:T(8,128)S(1)}, f32[2,2,4,8,640]{4,3,2,1,0:T(8,128)S(1)}, u32[]{:S(2)}, u32[]{:S(2)}) %collective-permute-start.14) | collective-permute-done | bytes 327712 | tf_op jit(solution)/shard_map/ppermute | solution.py:456
  63.5 0.1 collective-permute-start.15
  63.7 1.1 %shard_map.56 = (f32[2,4,8,640]{3,2,1,0:T(8,128)S(1)}, f32[2,4,8,640]{3,2,1,0:T(8,128)S(1)}) custom-call(f32[2,2,4,8,640]{4,3,2,1,0:T(8,128)S(1)} %get-tuple-element.121.own_ref, f32[2,2,4,8,640]{4,3,2,1,0:T(8,128)S(1)} %collective-permute-done.14.partner_ref, s32[2,2,2]{2,1,0:T(2,128)S(1)} %get-tuple-element.124.offset_ref, f32[4]{0:T(128)S(1)} %copy-done.3, ...), custom_call_target="tpu_custom_call" | custom-call | flops 1210000000 | bytes 2293808 | tf_op jit(solution)/shard_map/pallas_call | solution.py:139
  64.7 0.1 collective-permute-start.16
  64.8 2.2 %collective-permute-start.17 = (f32[2,4,8,640]{3,2,1,0:T(8,128)S(1)}, f32[2,4,8,640]{3,2,1,0:T(8,128)S(1)}, u32[]{:S(2)}, u32[]{:S(2)}) collective-permute-start(f32[2,4,8,640]{3,2,1,0:T(8,128)S(1)} %get-tuple-element.126.side1_ref), channel_id=1, source_target_pairs={{2,4},{3,5},{4,2},{5,3},{10,12},{11,13},{12,10},{13,11},{18,20},{1... | collective-permute-start | bytes 491528 | tf_op jit(solution)/shard_map/ppermute | solution.py:468
  67.0 0.0 collective-permute-done.15.partner_ref
  67.0 7.3 %shard_map.57 = (f32[2,24,8,640]{3,2,1,0:T(8,128)S(1)}, f32[2,2,3,2,8,640]{5,4,3,2,1,0:T(8,128)S(1)}) custom-call(f32[2,24,8,640]{3,2,1,0:T(8,128)S(1)} %get-tuple-element.122.own_ref, f32[2,24,8,640]{3,2,1,0:T(8,128)S(1)} %collective-permute-done.15.partner_ref, f32[2,4,8,640]{3,2,1,0:T(8,128)S(1)} %get-tuple-element.125.side0_ref, ...), custom_call_target="tpu_custom_call" | custom-call | flops 8800000000 | bytes 5079088 | tf_op jit(solution)/shard_map/pallas_call | solution.py:139
  74.3 0.0 collective-permute-done.16.halo0_ref
  74.3 0.0 collective-permute-done.17.halo1_ref
  74.3 2.1 %shard_map.58.own_ref.partner_ref = f32[2,2,4,8,640]{4,3,2,1,0:T(8,128)S(1)} custom-call(f32[2,4,8,640]{3,2,1,0:T(8,128)S(1)} %get-tuple-element.125.side0_ref, f32[2,4,8,640]{3,2,1,0:T(8,128)S(1)} %get-tuple-element.126.side1_ref, f32[2,4,8,640]{3,2,1,0:T(8,128)S(1)} %collective-permute-done.16.halo0_ref, ...), custom_call_target="tpu_custom_call" | custom-call | flops 2640000000 | bytes 1474560 | tf_op jit(solution)/shard_map/pallas_call | solution.py:139
  76.4 1.1 %shard_map.59 = (f32[2,4,8,640]{3,2,1,0:T(8,128)S(1)}, f32[2,4,8,640]{3,2,1,0:T(8,128)S(1)}) custom-call(f32[2,2,4,8,640]{4,3,2,1,0:T(8,128)S(1)} %shard_map.58.own_ref.partner_ref, f32[2,2,4,8,640]{4,3,2,1,0:T(8,128)S(1)} %shard_map.58.own_ref.partner_ref, s32[2,2,2]{2,1,0:T(2,128)S(1)} %get-tuple-element.124.offset_ref, f32[4]{0:T(128)S(1)} %copy-done.3, ...), custom_call_target="tpu_custom_call" | custom-call | flops 1210000000 | bytes 2293808 | tf_op jit(solution)/shard_map/pallas_call | solution.py:139
  77.5 0.6 collective-permute-start.21
  78.1 3.4 %collective-permute-start.22 = (f32[2,4,8,640]{3,2,1,0:T(8,128)S(1)}, f32[2,4,8,640]{3,2,1,0:T(8,128)S(1)}, u32[]{:S(2)}, u32[]{:S(2)}) collective-permute-start(f32[2,4,8,640]{3,2,1,0:T(8,128)S(1)} %get-tuple-element.130.side1_ref), channel_id=1, source_target_pairs={{2,4},{3,5},{4,2},{5,3},{10,12},{11,13},{12,10},{13,11},{18,20},{1... | collective-permute-start | bytes 491528 | tf_op jit(solution)/shard_map/ppermute | solution.py:468
  81.5 4.4 %shard_map.61 = (f32[12,8,512]{2,1,0:T(8,128)S(1)}, f32[12,8,512]{2,1,0:T(8,128)S(1)}, f32[2,1,3,2,8,640]{5,4,3,2,1,0:T(8,128)S(1)}) custom-call(f32[2,24,8,640]{3,2,1,0:T(8,128)S(1)} %get-tuple-element.127.own_ref.partner_ref, f32[2,24,8,640]{3,2,1,0:T(8,128)S(1)} %get-tuple-element.127.own_ref.partner_ref, ...), custom_call_target="tpu_custom_call" | custom-call | flops 4620000256 | bytes 4243504 | tf_op jit(solution)/shard_map/pallas_call | solution.py:139
  85.9 1.6 %collective-permute-start.20 = (f32[12,8,512]{2,1,0:T(8,128)S(1)}, f32[12,8,512]{2,1,0:T(8,128)S(1)}, u32[]{:S(2)}, u32[]{:S(2)}) collective-permute-start(f32[12,8,512]{2,1,0:T(8,128)S(1)} %get-tuple-element.134), channel_id=1, source_target_pairs={{0,17},{1,16},{2,19},{3,18},{4,21},{5,20},{6,23},{7,22},{8,25},{9,... | collective-permute-start | bytes 589832 | tf_op jit(solution)/shard_map/ppermute | solution.py:456
  87.5 4.4 %shard_map.60 = (f32[12,8,512]{2,1,0:T(8,128)S(1)}, f32[12,8,512]{2,1,0:T(8,128)S(1)}, f32[2,1,3,2,8,640]{5,4,3,2,1,0:T(8,128)S(1)}) custom-call(f32[2,24,8,640]{3,2,1,0:T(8,128)S(1)} %get-tuple-element.127.own_ref.partner_ref, f32[2,24,8,640]{3,2,1,0:T(8,128)S(1)} %get-tuple-element.127.own_ref.partner_ref, ...), custom_call_target="tpu_custom_call" | custom-call | flops 4620000256 | bytes 4243504 | tf_op jit(solution)/shard_map/pallas_call | solution.py:139
  91.9 0.6 collective-permute-start.19
  92.5 1.4 %collective-permute-start.18 = (f32[12,8,512]{2,1,0:T(8,128)S(1)}, f32[12,8,512]{2,1,0:T(8,128)S(1)}, u32[]{:S(2)}, u32[]{:S(2)}) collective-permute-start(f32[12,8,512]{2,1,0:T(8,128)S(1)} %get-tuple-element.132), channel_id=1, source_target_pairs={{0,1},{1,0},{2,3},{3,2},{4,5},{5,4},{6,7},{7,6},{8,9},{9,8},{10,11... | collective-permute-start | bytes 589832 | tf_op jit(solution)/shard_map/ppermute | solution.py:456
  93.9 2.4 %shard_map.62 = (f32[4,8,512]{2,1,0:T(8,128)S(1)}, f32[4,8,512]{2,1,0:T(8,128)S(1)}, f32[4,8,512]{2,1,0:T(8,128)S(1)}, f32[4,8,512]{2,1,0:T(8,128)S(1)}) custom-call(f32[2,4,8,640]{3,2,1,0:T(8,128)S(1)} %get-tuple-element.129.side0_ref, f32[2,4,8,640]{3,2,1,0:T(8,128)S(1)} %get-tuple-element.130.side1_ref, ...), custom_call_target="tpu_custom_call" | custom-call | flops 2750000128 | bytes 1409024 | tf_op jit(solution)/shard_map/pallas_call | solution.py:139
  96.4 0.7 collective-permute-start.23
  97.0 1.5 %collective-permute-start.24 = (f32[4,8,512]{2,1,0:T(8,128)S(1)}, f32[4,8,512]{2,1,0:T(8,128)S(1)}, u32[]{:S(2)}, u32[]{:S(2)}) collective-permute-start(f32[4,8,512]{2,1,0:T(8,128)S(1)} %get-tuple-element.141), channel_id=1, source_target_pairs={{0,16},{1,17},{2,18},{3,19},{4,20},{5,21},{6,22},{7,23},{8,24},{9,... | collective-permute-start | bytes 196616 | tf_op jit(solution)/shard_map/ppermute | solution.py:456
  98.5 1.4 %collective-permute-start.25 = (f32[4,8,512]{2,1,0:T(8,128)S(1)}, f32[4,8,512]{2,1,0:T(8,128)S(1)}, u32[]{:S(2)}, u32[]{:S(2)}) collective-permute-start(f32[4,8,512]{2,1,0:T(8,128)S(1)} %get-tuple-element.142), channel_id=1, source_target_pairs={{0,17},{1,16},{2,19},{3,18},{4,21},{5,20},{6,23},{7,22},{8,25},{9,... | collective-permute-start | bytes 196616 | tf_op jit(solution)/shard_map/ppermute | solution.py:456
  99.9 1.5 %collective-permute-done.23.refs_5_ = f32[4,8,512]{2,1,0:T(8,128)S(1)} collective-permute-done((f32[4,8,512]{2,1,0:T(8,128)S(1)}, f32[4,8,512]{2,1,0:T(8,128)S(1)}, u32[]{:S(2)}, u32[]{:S(2)}) %collective-permute-start.23) | collective-permute-done | bytes 65568 | tf_op jit(solution)/shard_map/ppermute | solution.py:456
  101.4 0.4 collective-permute-done.24.refs_6_
  101.8 1.9 %collective-permute-done.25.refs_7_ = f32[4,8,512]{2,1,0:T(8,128)S(1)} collective-permute-done((f32[4,8,512]{2,1,0:T(8,128)S(1)}, f32[4,8,512]{2,1,0:T(8,128)S(1)}, u32[]{:S(2)}, u32[]{:S(2)}) %collective-permute-start.25) | collective-permute-done | bytes 65568 | tf_op jit(solution)/shard_map/ppermute | solution.py:456
  103.7 1.1 %shard_map.63 = f32[16,8,2048]{2,1,0:T(8,128)} custom-call(f32[12,8,512]{2,1,0:T(8,128)S(1)} %get-tuple-element.131.refs_0_, f32[12,8,512]{2,1,0:T(8,128)S(1)} %collective-permute-done.18.refs_1_, f32[12,8,512]{2,1,0:T(8,128)S(1)} %collective-permute-done.19.refs_2_, f32[12,8,512]{2,1,0:T(8,128)S(1)} %collective-permute-done.20.refs_3_, ...), custom_call_target="tpu_custom_call" | custom-call | flops 1100000000 | bytes 2097152 | tf_op jit(solution)/shard_map/pallas_call | solution.py:139
  (15 shorter events, 0.1 us)
Async XLA Ops:
  0.0 5.1 %copy-start = (f32[1,4,4,16,2048]{4,3,2,1,0:T(8,128)S(1)}, f32[1,4,4,16,2048]{4,3,2,1,0:T(8,128)}, u32[]{:S(2)}) copy-start(f32[1,4,4,16,2048]{4,3,2,1,0:T(8,128)} %coeff_ref.3) | copy-start | bytes 6291460
  0.0 5.1 %copy-start.1 = (f32[1,16,8,2048]{3,2,1,0:T(8,128)S(1)}, f32[1,16,8,2048]{3,2,1,0:T(8,128)}, u32[]{:S(2)}) copy-start(f32[1,16,8,2048]{3,2,1,0:T(8,128)} %param.4) | copy-start | bytes 3145732
  0.0 5.1 %copy-start.2 = (s32[1,1,4]{2,1,0:T(1,128)S(1)}, s32[1,1,4]{2,1,0:T(1,128)}, u32[]{:S(2)}) copy-start(s32[1,1,4]{2,1,0:T(1,128)} %offset_ref.3) | copy-start | bytes 52
  0.0 5.2 %copy-start.3 = (f32[4]{0:T(128)S(1)}, f32[4]{0:T(128)}, u32[]{:S(2)}) copy-start(f32[4]{0:T(128)} %level_ref.15) | copy-start | bytes 52
  0.0 5.1 %collective-permute-start = (f32[16,8,2048]{2,1,0:T(8,128)}, f32[16,8,2048]{2,1,0:T(8,128)S(1)}, u32[]{:S(2)}, u32[]{:S(2)}) collective-permute-start(f32[16,8,2048]{2,1,0:T(8,128)} %bitcast.4), channel_id=1, source_target_pairs={{0,8},{1,9},{2,10},{3,11},{4,12},{5,13},{6,14},{7,15},{8,0},{9,1},... | collective-permute-start | bytes 3145736 | tf_op jit(solution)/shard_map/ppermute | solution.py:456
  1.6 7.2 %collective-permute-start.1 = (f32[4,16,640]{2,1,0:T(8,128)S(1)}, f32[4,16,640]{2,1,0:T(8,128)S(1)}, u32[]{:S(2)}, u32[]{:S(2)}) collective-permute-start(f32[4,16,640]{2,1,0:T(8,128)S(1)} %get-tuple-element.83), channel_id=1, source_target_pairs={{0,1},{1,0},{2,3},{3,2},{4,5},{5,4},{6,7},{7,6},{8,9},{9,8},{10,11... | collective-permute-start | bytes 491528 | tf_op jit(solution)/shard_map/ppermute | solution.py:456
  3.2 7.0 %collective-permute-start.2 = (f32[4,16,640]{2,1,0:T(8,128)S(1)}, f32[4,16,640]{2,1,0:T(8,128)S(1)}, u32[]{:S(2)}, u32[]{:S(2)}) collective-permute-start(f32[4,16,640]{2,1,0:T(8,128)S(1)} %get-tuple-element.84), channel_id=1, source_target_pairs={{0,16},{1,17},{2,18},{3,19},{4,20},{5,21},{6,22},{7,23},{8,24},{9,... | collective-permute-start | bytes 491528 | tf_op jit(solution)/shard_map/ppermute | solution.py:456
  4.7 8.3 %collective-permute-start.3 = (f32[4,16,640]{2,1,0:T(8,128)S(1)}, f32[4,16,640]{2,1,0:T(8,128)S(1)}, u32[]{:S(2)}, u32[]{:S(2)}) collective-permute-start(f32[4,16,640]{2,1,0:T(8,128)S(1)} %get-tuple-element.85), channel_id=1, source_target_pairs={{0,17},{1,16},{2,19},{3,18},{4,21},{5,20},{6,23},{7,22},{8,25},{9,... | collective-permute-start | bytes 491528 | tf_op jit(solution)/shard_map/ppermute | solution.py:456
  13.0 9.1 %collective-permute-start.4 = (f32[16,8,640]{2,1,0:T(8,128)S(1)}, f32[16,8,640]{2,1,0:T(8,128)S(1)}, u32[]{:S(2)}, u32[]{:S(2)}) collective-permute-start(f32[16,8,640]{2,1,0:T(8,128)S(1)} %get-tuple-element.88), channel_id=1, source_target_pairs={{0,1},{1,0},{2,3},{3,2},{4,5},{5,4},{6,7},{7,6},{8,9},{9,8},{10,11... | collective-permute-start | bytes 983048 | tf_op jit(solution)/shard_map/ppermute | solution.py:456
  14.5 8.8 %collective-permute-start.5 = (f32[16,8,640]{2,1,0:T(8,128)S(1)}, f32[16,8,640]{2,1,0:T(8,128)S(1)}, u32[]{:S(2)}, u32[]{:S(2)}) collective-permute-start(f32[16,8,640]{2,1,0:T(8,128)S(1)} %get-tuple-element.89), channel_id=1, source_target_pairs={{0,16},{1,17},{2,18},{3,19},{4,20},{5,21},{6,22},{7,23},{8,24},{9,... | collective-permute-start | bytes 983048 | tf_op jit(solution)/shard_map/ppermute | solution.py:456
  23.3 8.8 %collective-permute-start.6 = (f32[16,8,640]{2,1,0:T(8,128)S(1)}, f32[16,8,640]{2,1,0:T(8,128)S(1)}, u32[]{:S(2)}, u32[]{:S(2)}) collective-permute-start(f32[16,8,640]{2,1,0:T(8,128)S(1)} %get-tuple-element.92), channel_id=1, source_target_pairs={{0,17},{1,16},{2,19},{3,18},{4,21},{5,20},{6,23},{7,22},{8,25},{9,... | collective-permute-start | bytes 983048 | tf_op jit(solution)/shard_map/ppermute | solution.py:456
  32.2 11.7 %collective-permute-start.10 = (f32[2,4,8,640]{3,2,1,0:T(8,128)S(1)}, f32[2,4,8,640]{3,2,1,0:T(8,128)S(1)}, u32[]{:S(2)}, u32[]{:S(2)}) collective-permute-start(f32[2,4,8,640]{3,2,1,0:T(8,128)S(1)} %get-tuple-element.104.side0_ref), channel_id=1, source_target_pairs={{0,2},{1,3},{2,0},{3,1},{4,6},{5,7},{6,4},{7,5},{8,10},{9,11},{10,... | collective-permute-start | bytes 491528 | tf_op jit(solution)/shard_map/ppermute | solution.py:468
  32.7 11.2 %collective-permute-start.11 = (f32[2,4,8,640]{3,2,1,0:T(8,128)S(1)}, f32[2,4,8,640]{3,2,1,0:T(8,128)S(1)}, u32[]{:S(2)}, u32[]{:S(2)}) collective-permute-start(f32[2,4,8,640]{3,2,1,0:T(8,128)S(1)} %get-tuple-element.105.side1_ref), channel_id=1, source_target_pairs={{2,4},{3,5},{4,2},{5,3},{10,12},{11,13},{12,10},{13,11},{18,20},{1... | collective-permute-start | bytes 491528 | tf_op jit(solution)/shard_map/ppermute | solution.py:468
  37.3 12.1 %collective-permute-start.7 = (f32[2,4,16,640]{3,2,1,0:T(8,128)S(1)}, f32[2,4,16,640]{3,2,1,0:T(8,128)S(1)}, u32[]{:S(2)}, u32[]{:S(2)}) collective-permute-start(f32[2,4,16,640]{3,2,1,0:T(8,128)S(1)} %get-tuple-element.97), channel_id=1, source_target_pairs={{0,1},{1,0},{2,3},{3,2},{4,5},{5,4},{6,7},{7,6},{8,9},{9,8},{10,11... | collective-permute-start | bytes 983048 | tf_op jit(solution)/shard_map/ppermute | solution.py:456
  37.9 11.5 %collective-permute-start.8 = (f32[2,4,16,640]{3,2,1,0:T(8,128)S(1)}, f32[2,4,16,640]{3,2,1,0:T(8,128)S(1)}, u32[]{:S(2)}, u32[]{:S(2)}) collective-permute-start(f32[2,4,16,640]{3,2,1,0:T(8,128)S(1)} %get-tuple-element.98), channel_id=1, source_target_pairs={{0,16},{1,17},{2,18},{3,19},{4,20},{5,21},{6,22},{7,23},{8,24},{9,... | collective-permute-start | bytes 983048 | tf_op jit(solution)/shard_map/ppermute | solution.py:456
  39.4 12.6 %collective-permute-start.9 = (f32[2,4,16,640]{3,2,1,0:T(8,128)S(1)}, f32[2,4,16,640]{3,2,1,0:T(8,128)S(1)}, u32[]{:S(2)}, u32[]{:S(2)}) collective-permute-start(f32[2,4,16,640]{3,2,1,0:T(8,128)S(1)} %get-tuple-element.99), channel_id=1, source_target_pairs={{0,17},{1,16},{2,19},{3,18},{4,21},{5,20},{6,23},{7,22},{8,25},{9,... | collective-permute-start | bytes 983048 | tf_op jit(solution)/shard_map/ppermute | solution.py:456
  47.2 12.0 %collective-permute-start.12 = (f32[2,4,8,640]{3,2,1,0:T(8,128)S(1)}, f32[2,4,8,640]{3,2,1,0:T(8,128)S(1)}, u32[]{:S(2)}, u32[]{:S(2)}) collective-permute-start(f32[2,4,8,640]{3,2,1,0:T(8,128)S(1)} %get-tuple-element.113.side0_ref), channel_id=1, source_target_pairs={{0,2},{1,3},{2,0},{3,1},{4,6},{5,7},{6,4},{7,5},{8,10},{9,11},{10,... | collective-permute-start | bytes 491528 | tf_op jit(solution)/shard_map/ppermute | solution.py:468
  47.3 12.0 %collective-permute-start.13 = (f32[2,4,8,640]{3,2,1,0:T(8,128)S(1)}, f32[2,4,8,640]{3,2,1,0:T(8,128)S(1)}, u32[]{:S(2)}, u32[]{:S(2)}) collective-permute-start(f32[2,4,8,640]{3,2,1,0:T(8,128)S(1)} %get-tuple-element.114.side1_ref), channel_id=1, source_target_pairs={{2,4},{3,5},{4,2},{5,3},{10,12},{11,13},{12,10},{13,11},{18,20},{1... | collective-permute-start | bytes 491528 | tf_op jit(solution)/shard_map/ppermute | solution.py:468
  61.8 1.7 %collective-permute-start.14 = (f32[2,2,4,8,640]{4,3,2,1,0:T(8,128)S(1)}, f32[2,2,4,8,640]{4,3,2,1,0:T(8,128)S(1)}, u32[]{:S(2)}, u32[]{:S(2)}) collective-permute-start(f32[2,2,4,8,640]{4,3,2,1,0:T(8,128)S(1)} %get-tuple-element.121.own_ref), channel_id=1, source_target_pairs={{0,8},{1,9},{2,10},{3,11},{4,12},{5,13},{6,14},{7,15},{8,0},{9,1},... | collective-permute-start | bytes 983048 | tf_op jit(solution)/shard_map/ppermute | solution.py:456
  63.5 3.5 %collective-permute-start.15 = (f32[2,24,8,640]{3,2,1,0:T(8,128)S(1)}, f32[2,24,8,640]{3,2,1,0:T(8,128)S(1)}, u32[]{:S(2)}, u32[]{:S(2)}) collective-permute-start(f32[2,24,8,640]{3,2,1,0:T(8,128)S(1)} %get-tuple-element.122.own_ref), channel_id=1, source_target_pairs={{0,8},{1,9},{2,10},{3,11},{4,12},{5,13},{6,14},{7,15},{8,0},{9,1},... | collective-permute-start | bytes 2949128 | tf_op jit(solution)/shard_map/ppermute | solution.py:456
  64.7 9.5 %collective-permute-start.16 = (f32[2,4,8,640]{3,2,1,0:T(8,128)S(1)}, f32[2,4,8,640]{3,2,1,0:T(8,128)S(1)}, u32[]{:S(2)}, u32[]{:S(2)}) collective-permute-start(f32[2,4,8,640]{3,2,1,0:T(8,128)S(1)} %get-tuple-element.125.side0_ref), channel_id=1, source_target_pairs={{0,2},{1,3},{2,0},{3,1},{4,6},{5,7},{6,4},{7,5},{8,10},{9,11},{10,... | collective-permute-start | bytes 491528 | tf_op jit(solution)/shard_map/ppermute | solution.py:468
  64.8 9.5 %collective-permute-start.17 = (f32[2,4,8,640]{3,2,1,0:T(8,128)S(1)}, f32[2,4,8,640]{3,2,1,0:T(8,128)S(1)}, u32[]{:S(2)}, u32[]{:S(2)}) collective-permute-start(f32[2,4,8,640]{3,2,1,0:T(8,128)S(1)} %get-tuple-element.126.side1_ref), channel_id=1, source_target_pairs={{2,4},{3,5},{4,2},{5,3},{10,12},{11,13},{12,10},{13,11},{18,20},{1... | collective-permute-start | bytes 491528 | tf_op jit(solution)/shard_map/ppermute | solution.py:468
  77.5 16.4 %collective-permute-start.21 = (f32[2,4,8,640]{3,2,1,0:T(8,128)S(1)}, f32[2,4,8,640]{3,2,1,0:T(8,128)S(1)}, u32[]{:S(2)}, u32[]{:S(2)}) collective-permute-start(f32[2,4,8,640]{3,2,1,0:T(8,128)S(1)} %get-tuple-element.129.side0_ref), channel_id=1, source_target_pairs={{0,2},{1,3},{2,0},{3,1},{4,6},{5,7},{6,4},{7,5},{8,10},{9,11},{10,... | collective-permute-start | bytes 491528 | tf_op jit(solution)/shard_map/ppermute | solution.py:468
  78.1 15.9 %collective-permute-start.22 = (f32[2,4,8,640]{3,2,1,0:T(8,128)S(1)}, f32[2,4,8,640]{3,2,1,0:T(8,128)S(1)}, u32[]{:S(2)}, u32[]{:S(2)}) collective-permute-start(f32[2,4,8,640]{3,2,1,0:T(8,128)S(1)} %get-tuple-element.130.side1_ref), channel_id=1, source_target_pairs={{2,4},{3,5},{4,2},{5,3},{10,12},{11,13},{12,10},{13,11},{18,20},{1... | collective-permute-start | bytes 491528 | tf_op jit(solution)/shard_map/ppermute | solution.py:468
  85.9 8.0 %collective-permute-start.20 = (f32[12,8,512]{2,1,0:T(8,128)S(1)}, f32[12,8,512]{2,1,0:T(8,128)S(1)}, u32[]{:S(2)}, u32[]{:S(2)}) collective-permute-start(f32[12,8,512]{2,1,0:T(8,128)S(1)} %get-tuple-element.134), channel_id=1, source_target_pairs={{0,17},{1,16},{2,19},{3,18},{4,21},{5,20},{6,23},{7,22},{8,25},{9,... | collective-permute-start | bytes 589832 | tf_op jit(solution)/shard_map/ppermute | solution.py:456
  91.9 8.0 %collective-permute-start.19 = (f32[12,8,512]{2,1,0:T(8,128)S(1)}, f32[12,8,512]{2,1,0:T(8,128)S(1)}, u32[]{:S(2)}, u32[]{:S(2)}) collective-permute-start(f32[12,8,512]{2,1,0:T(8,128)S(1)} %get-tuple-element.133), channel_id=1, source_target_pairs={{0,16},{1,17},{2,18},{3,19},{4,20},{5,21},{6,22},{7,23},{8,24},{9,... | collective-permute-start | bytes 589832 | tf_op jit(solution)/shard_map/ppermute | solution.py:456
  92.5 7.4 %collective-permute-start.18 = (f32[12,8,512]{2,1,0:T(8,128)S(1)}, f32[12,8,512]{2,1,0:T(8,128)S(1)}, u32[]{:S(2)}, u32[]{:S(2)}) collective-permute-start(f32[12,8,512]{2,1,0:T(8,128)S(1)} %get-tuple-element.132), channel_id=1, source_target_pairs={{0,1},{1,0},{2,3},{3,2},{4,5},{5,4},{6,7},{7,6},{8,9},{9,8},{10,11... | collective-permute-start | bytes 589832 | tf_op jit(solution)/shard_map/ppermute | solution.py:456
  96.4 5.0 %collective-permute-start.23 = (f32[4,8,512]{2,1,0:T(8,128)S(1)}, f32[4,8,512]{2,1,0:T(8,128)S(1)}, u32[]{:S(2)}, u32[]{:S(2)}) collective-permute-start(f32[4,8,512]{2,1,0:T(8,128)S(1)} %get-tuple-element.140), channel_id=1, source_target_pairs={{0,1},{1,0},{2,3},{3,2},{4,5},{5,4},{6,7},{7,6},{8,9},{9,8},{10,11... | collective-permute-start | bytes 196616 | tf_op jit(solution)/shard_map/ppermute | solution.py:456
  97.0 4.7 %collective-permute-start.24 = (f32[4,8,512]{2,1,0:T(8,128)S(1)}, f32[4,8,512]{2,1,0:T(8,128)S(1)}, u32[]{:S(2)}, u32[]{:S(2)}) collective-permute-start(f32[4,8,512]{2,1,0:T(8,128)S(1)} %get-tuple-element.141), channel_id=1, source_target_pairs={{0,16},{1,17},{2,18},{3,19},{4,20},{5,21},{6,22},{7,23},{8,24},{9,... | collective-permute-start | bytes 196616 | tf_op jit(solution)/shard_map/ppermute | solution.py:456
  98.5 5.2 %collective-permute-start.25 = (f32[4,8,512]{2,1,0:T(8,128)S(1)}, f32[4,8,512]{2,1,0:T(8,128)S(1)}, u32[]{:S(2)}, u32[]{:S(2)}) collective-permute-start(f32[4,8,512]{2,1,0:T(8,128)S(1)} %get-tuple-element.142), channel_id=1, source_target_pairs={{0,17},{1,16},{2,19},{3,18},{4,21},{5,20},{6,23},{7,22},{8,25},{9,... | collective-permute-start | bytes 196616 | tf_op jit(solution)/shard_map/ppermute | solution.py:456

commit v4 on v3

--- a/solution.py
+++ b/solution.py
@@ -315,7 +315,7 @@
         other = 1 - slot if bit == 1 else slot
         for away in range(2):
             slab = place.slab ^ away
-            offset = offset_ref[0 if section == 1 else section - 2, slot, away]
+            offset = offset_ref[0, slot, away]
             start = jnp.where(slab == 0, EDGE, 0)
             for i in range(half - EDGE):
                 z = start + i
@@ -397,7 +397,7 @@
         for away in range(2):
             is_top = place.slab ^ away == 1
             side = jnp.where(is_top, place.odd, 1 - place.odd)
-            offset = offset_ref[0 if section == 1 else section - 2, slot, away]
+            offset = offset_ref[0, slot, away]
             for e in range(EDGE):
                 z = jnp.where(is_top, half - 1 - e, e)
                 rows = [rows_of[2 * slot + away](k, z) for k in range(BAND)]
@@ -507,11 +507,11 @@
     table = None
     for section in range(1, SECTIONS):
         bit = section % levels
-        corners = {1: [(0,)], 2: [(i, 0) for i in range(SECTIONS - 2)]}.get(section, [])
+        corners = [(0,)] if section == 1 else [(section - 2, 0)]
         edges, *shift = call(
             functools.partial(wedge_kernel, corners),
             [edges_shape] + [jax.ShapeDtypeStruct((len(corners), 2, 2), jnp.int32)] * bool(corners),
-            side0, side1, halo0, halo1, saved, *({1: (mine, near, far, across), 2: coeff}.get(section, ())),
+            side0, side1, halo0, halo1, saved, *((mine, near, far, across) if section == 1 else coeff),
             smem_outs=(1,), micros=2.4,
         )
         table = shift[0] if shift else table

time: 105 us -> 105 us (level)
  no operation moved by 1% of the time
where the time goes in v4:
time: 105 us; the launch traced here: 104 us
  Pallas kernels  47.5 us (45%)
  starting transfers between devices  32.5 us (31%)
  waiting for transfers between devices  22.9 us (22%)
  local copies, waits for them, and re-layouts  1.24 us (1%)
    pallas_call x18, Pallas kernels, call(): pl.pallas_call(body, out_shape=outs, in_specs=in_specs, out_specs=out_spe...  47.5 us
    ppermute x18, waiting for transfers between devices, swap(): return lax.ppermute(value, axes, route(frame_bits, slab_bits))  22.9 us
    ppermute x18, starting transfers between devices, swap(): return lax.ppermute(value, axes, route(frame_bits, slab_bits))  19 us
    ppermute x4, starting transfers between devices, halo(): lax.ppermute(side1, 'space', second)  12.3 us
  transfers between devices with their start and end apart: 26, of which 10 were waited for; matrix products, arithmetic and copies ran while one was open for 1% of the time, Pallas kernels for 39%

profile of v4, /device:TPU:8, one launch (start us, length us, event | category | flops | bytes accessed | tf_op | source)
XLA Modules:
  0.0 104.5 jit_solution(367627004852826581)
XLA Ops:
  0.0 0.1 collective-permute-start
  0.1 1.2 %slice_bitcast_fusion.coeff_ref = f32[4,16,2048]{2,1,0:T(8,128)S(1)} fusion(f32[1,4,4,16,2048]{4,3,2,1,0:T(8,128)} %coeff_ref.3), kind=kLoop, calls=%fused_computation | loop fusion | bytes 1048576 | tf_op jit(solution)/shard_map/squeeze | solution.py:479
  1.3 0.2 shard_map.48
  1.6 1.6 %collective-permute-start.1 = (f32[4,16,640]{2,1,0:T(8,128)S(1)}, f32[4,16,640]{2,1,0:T(8,128)S(1)}, u32[]{:S(2)}, u32[]{:S(2)}) collective-permute-start(f32[4,16,640]{2,1,0:T(8,128)S(1)} %get-tuple-element.85), channel_id=1, source_target_pairs={{0,1},{1,0},{2,3},{3,2},{4,5},{5,4},{6,7},{7,6},{8,9},{9,8},{10,11... | collective-permute-start | bytes 491528 | tf_op jit(solution)/shard_map/ppermute | solution.py:456
  3.2 1.5 %collective-permute-start.2 = (f32[4,16,640]{2,1,0:T(8,128)S(1)}, f32[4,16,640]{2,1,0:T(8,128)S(1)}, u32[]{:S(2)}, u32[]{:S(2)}) collective-permute-start(f32[4,16,640]{2,1,0:T(8,128)S(1)} %get-tuple-element.86), channel_id=1, source_target_pairs={{0,16},{1,17},{2,18},{3,19},{4,20},{5,21},{6,22},{7,23},{8,24},{9,... | collective-permute-start | bytes 491528 | tf_op jit(solution)/shard_map/ppermute | solution.py:456
  4.7 0.5 collective-permute-start.3
  5.1 0.0 collective-permute-done.partner_ref
  5.2 3.6 %shard_map.47 = (f32[16,8,640]{2,1,0:T(8,128)S(1)}, f32[16,8,640]{2,1,0:T(8,128)S(1)}, f32[16,8,640]{2,1,0:T(8,128)S(1)}, f32[16,8,640]{2,1,0:T(8,128)S(1)}) custom-call(f32[16,8,2048]{2,1,0:T(8,128)S(1)} %bitcast.5, f32[16,8,2048]{2,1,0:T(8,128)S(1)} %collective-permute-done.partner_ref, f32[1,4,4,16,2048]{4,3,2,1,0:T(8,128)S(1)} %copy-done, ...), custom_call_target="tpu_custom_call" | custom-call | flops 4400000000 | bytes 5505056 | tf_op jit(solution)/shard_map/pallas_call | solution.py:139
  8.7 0.0 collective-permute-done.1.refs_1_
  8.7 1.5 %collective-permute-done.2.refs_2_ = f32[4,16,640]{2,1,0:T(8,128)S(1)} collective-permute-done((f32[4,16,640]{2,1,0:T(8,128)S(1)}, f32[4,16,640]{2,1,0:T(8,128)S(1)}, u32[]{:S(2)}, u32[]{:S(2)}) %collective-permute-start.2) | collective-permute-done | bytes 163872 | tf_op jit(solution)/shard_map/ppermute | solution.py:456
  10.2 2.8 %collective-permute-done.3.refs_3_ = f32[4,16,640]{2,1,0:T(8,128)S(1)} collective-permute-done((f32[4,16,640]{2,1,0:T(8,128)S(1)}, f32[4,16,640]{2,1,0:T(8,128)S(1)}, u32[]{:S(2)}, u32[]{:S(2)}) %collective-permute-start.3) | collective-permute-done | bytes 163872 | tf_op jit(solution)/shard_map/ppermute | solution.py:456
  13.0 1.5 %collective-permute-start.4 = (f32[16,8,640]{2,1,0:T(8,128)S(1)}, f32[16,8,640]{2,1,0:T(8,128)S(1)}, u32[]{:S(2)}, u32[]{:S(2)}) collective-permute-start(f32[16,8,640]{2,1,0:T(8,128)S(1)} %get-tuple-element.90), channel_id=1, source_target_pairs={{0,1},{1,0},{2,3},{3,2},{4,5},{5,4},{6,7},{7,6},{8,9},{9,8},{10,11... | collective-permute-start | bytes 983048 | tf_op jit(solution)/shard_map/ppermute | solution.py:456
  14.5 1.5 %collective-permute-start.5 = (f32[16,8,640]{2,1,0:T(8,128)S(1)}, f32[16,8,640]{2,1,0:T(8,128)S(1)}, u32[]{:S(2)}, u32[]{:S(2)}) collective-permute-start(f32[16,8,640]{2,1,0:T(8,128)S(1)} %get-tuple-element.91), channel_id=1, source_target_pairs={{0,16},{1,17},{2,18},{3,19},{4,20},{5,21},{6,22},{7,23},{8,24},{9,... | collective-permute-start | bytes 983048 | tf_op jit(solution)/shard_map/ppermute | solution.py:456
  16.0 0.9 shard_map.46
  17.0 5.1 %collective-permute-done.4.other_ref.near_ref.refs_1_ = f32[16,8,640]{2,1,0:T(8,128)S(1)} collective-permute-done((f32[16,8,640]{2,1,0:T(8,128)S(1)}, f32[16,8,640]{2,1,0:T(8,128)S(1)}, u32[]{:S(2)}, u32[]{:S(2)}) %collective-permute-start.4) | collective-permute-done | bytes 327712 | tf_op jit(solution)/shard_map/ppermute | solution.py:456
  22.1 1.2 %collective-permute-done.5.far_ref.own_ref.refs_2_ = f32[16,8,640]{2,1,0:T(8,128)S(1)} collective-permute-done((f32[16,8,640]{2,1,0:T(8,128)S(1)}, f32[16,8,640]{2,1,0:T(8,128)S(1)}, u32[]{:S(2)}, u32[]{:S(2)}) %collective-permute-start.5) | collective-permute-done | bytes 327712 | tf_op jit(solution)/shard_map/ppermute | solution.py:456
  23.3 1.4 %collective-permute-start.6 = (f32[16,8,640]{2,1,0:T(8,128)S(1)}, f32[16,8,640]{2,1,0:T(8,128)S(1)}, u32[]{:S(2)}, u32[]{:S(2)}) collective-permute-start(f32[16,8,640]{2,1,0:T(8,128)S(1)} %get-tuple-element.94), channel_id=1, source_target_pairs={{0,17},{1,16},{2,19},{3,18},{4,21},{5,20},{6,23},{7,22},{8,25},{9,... | collective-permute-start | bytes 983048 | tf_op jit(solution)/shard_map/ppermute | solution.py:456
  24.8 3.0 %shard_map.49 = (f32[2,24,8,640]{3,2,1,0:T(8,128)S(1)}, f32[2,2,3,2,8,640]{5,4,3,2,1,0:T(8,128)S(1)}) custom-call(f32[16,8,640]{2,1,0:T(8,128)S(1)} %get-tuple-element.88.own_ref.self_ref.refs_0_, f32[16,8,640]{2,1,0:T(8,128)S(1)} %collective-permute-done.4.other_ref.near_ref.refs_1_), custom_call_target="tpu_custom_call" | custom-call | flops 3849999872 | bytes 2129920 | tf_op jit(solution)/shard_map/pallas_call | solution.py:139
  27.8 4.3 %collective-permute-done.6.across_ref.other_ref.refs_3_ = f32[16,8,640]{2,1,0:T(8,128)S(1)} collective-permute-done((f32[16,8,640]{2,1,0:T(8,128)S(1)}, f32[16,8,640]{2,1,0:T(8,128)S(1)}, u32[]{:S(2)}, u32[]{:S(2)}) %collective-permute-start.6) | collective-permute-done | bytes 327712 | tf_op jit(solution)/shard_map/ppermute | solution.py:456
  32.2 0.5 collective-permute-start.10
  32.7 4.6 %collective-permute-start.11 = (f32[2,4,8,640]{3,2,1,0:T(8,128)S(1)}, f32[2,4,8,640]{3,2,1,0:T(8,128)S(1)}, u32[]{:S(2)}, u32[]{:S(2)}) collective-permute-start(f32[2,4,8,640]{3,2,1,0:T(8,128)S(1)} %get-tuple-element.107.side1_ref), channel_id=1, source_target_pairs={{2,4},{3,5},{4,2},{5,3},{10,12},{11,13},{12,10},{13,11},{18,20},{1... | collective-permute-start | bytes 491528 | tf_op jit(solution)/shard_map/ppermute | solution.py:468
  37.3 0.6 collective-permute-start.7
  37.9 1.5 %collective-permute-start.8 = (f32[2,4,16,640]{3,2,1,0:T(8,128)S(1)}, f32[2,4,16,640]{3,2,1,0:T(8,128)S(1)}, u32[]{:S(2)}, u32[]{:S(2)}) collective-permute-start(f32[2,4,16,640]{3,2,1,0:T(8,128)S(1)} %get-tuple-element.100), channel_id=1, source_target_pairs={{0,16},{1,17},{2,18},{3,19},{4,20},{5,21},{6,22},{7,23},{8,24},{9,... | collective-permute-start | bytes 983048 | tf_op jit(solution)/shard_map/ppermute | solution.py:456
  39.4 1.4 %collective-permute-start.9 = (f32[2,4,16,640]{3,2,1,0:T(8,128)S(1)}, f32[2,4,16,640]{3,2,1,0:T(8,128)S(1)}, u32[]{:S(2)}, u32[]{:S(2)}) collective-permute-start(f32[2,4,16,640]{3,2,1,0:T(8,128)S(1)} %get-tuple-element.101), channel_id=1, source_target_pairs={{0,17},{1,16},{2,19},{3,18},{4,21},{5,20},{6,23},{7,22},{8,25},{9,... | collective-permute-start | bytes 983048 | tf_op jit(solution)/shard_map/ppermute | solution.py:456
  40.8 3.0 %shard_map.51 = (f32[2,24,8,640]{3,2,1,0:T(8,128)S(1)}, f32[2,2,3,2,8,640]{5,4,3,2,1,0:T(8,128)S(1)}) custom-call(f32[16,8,640]{2,1,0:T(8,128)S(1)} %collective-permute-done.5.far_ref.own_ref.refs_2_, f32[16,8,640]{2,1,0:T(8,128)S(1)} %collective-permute-done.6.across_ref.other_ref.refs_3_, ...), custom_call_target="tpu_custom_call", output_to_operand_aliasing={{0}: (2, {}), {1}: (3, {})} | custom-call | flops 3849999872 | bytes 3604480 | tf_op jit(solution)/shard_map/pallas_call | solution.py:139
  43.9 0.0 collective-permute-done.10.halo0_ref
  43.9 0.0 collective-permute-done.11.halo1_ref
  43.9 2.2 %shard_map.52 = (f32[2,2,4,8,640]{4,3,2,1,0:T(8,128)S(1)}, s32[1,2,2]{2,1,0:T(2,128)S(1)}) custom-call(f32[2,4,8,640]{3,2,1,0:T(8,128)S(1)} %get-tuple-element.106.side0_ref, f32[2,4,8,640]{3,2,1,0:T(8,128)S(1)} %get-tuple-element.107.side1_ref, f32[2,4,8,640]{3,2,1,0:T(8,128)S(1)} %collective-permute-done.10.halo0_ref, ...), custom_call_target="tpu_custom_call" | custom-call | flops 2640000000 | bytes 2785296 | tf_op jit(solution)/shard_map/pallas_call | solution.py:139
  46.1 1.1 %shard_map.53 = (f32[2,4,8,640]{3,2,1,0:T(8,128)S(1)}, f32[2,4,8,640]{3,2,1,0:T(8,128)S(1)}) custom-call(f32[2,2,4,8,640]{4,3,2,1,0:T(8,128)S(1)} %get-tuple-element.109.own_ref.partner_ref, f32[2,2,4,8,640]{4,3,2,1,0:T(8,128)S(1)} %get-tuple-element.109.own_ref.partner_ref, s32[1,2,2]{2,1,0:T(2,128)S(1)} %get-tuple-element.110.offset_ref, f32[4]{0:T(128)S(1)} %copy-done.3, ...), custom_call_target="tpu_custom_call" | custom-call | flops 1210000000 | bytes 1638432 | tf_op jit(solution)/shard_map/pallas_call | solution.py:139
  47.2 0.1 collective-permute-start.12
  47.3 2.1 %collective-permute-start.13 = (f32[2,4,8,640]{3,2,1,0:T(8,128)S(1)}, f32[2,4,8,640]{3,2,1,0:T(8,128)S(1)}, u32[]{:S(2)}, u32[]{:S(2)}) collective-permute-start(f32[2,4,8,640]{3,2,1,0:T(8,128)S(1)} %get-tuple-element.116.side1_ref), channel_id=1, source_target_pairs={{2,4},{3,5},{4,2},{5,3},{10,12},{11,13},{12,10},{13,11},{18,20},{1... | collective-permute-start | bytes 491528 | tf_op jit(solution)/shard_map/ppermute | solution.py:468
  49.4 0.0 collective-permute-done.7.refs_1_
  49.4 0.0 collective-permute-done.8.refs_2_
  49.4 2.6 %collective-permute-done.9.refs_3_ = f32[2,4,16,640]{3,2,1,0:T(8,128)S(1)} collective-permute-done((f32[2,4,16,640]{3,2,1,0:T(8,128)S(1)}, f32[2,4,16,640]{3,2,1,0:T(8,128)S(1)}, u32[]{:S(2)}, u32[]{:S(2)}) %collective-permute-start.9) | collective-permute-done | bytes 327712 | tf_op jit(solution)/shard_map/ppermute | solution.py:456
  52.0 7.2 %shard_map.54 = (f32[2,24,8,640]{3,2,1,0:T(8,128)S(1)}, f32[2,2,3,2,8,640]{5,4,3,2,1,0:T(8,128)S(1)}) custom-call(f32[2,24,8,640]{3,2,1,0:T(8,128)S(1)} %get-tuple-element.105.own_ref.partner_ref, f32[2,24,8,640]{3,2,1,0:T(8,128)S(1)} %get-tuple-element.105.own_ref.partner_ref, f32[2,4,8,640]{3,2,1,0:T(8,128)S(1)} %get-tuple-element.115.side0_ref, ...), custom_call_target="tpu_custom_call" | custom-call | flops 8800000000 | bytes 4423712 | tf_op jit(solution)/shard_map/pallas_call | solution.py:139
  59.2 0.0 collective-permute-done.12.halo0_ref
  59.3 0.0 collective-permute-done.13.halo1_ref
  59.3 2.2 %shard_map.55 = (f32[2,2,4,8,640]{4,3,2,1,0:T(8,128)S(1)}, s32[1,2,2]{2,1,0:T(2,128)S(1)}) custom-call(f32[2,4,8,640]{3,2,1,0:T(8,128)S(1)} %get-tuple-element.115.side0_ref, f32[2,4,8,640]{3,2,1,0:T(8,128)S(1)} %get-tuple-element.116.side1_ref, f32[2,4,8,640]{3,2,1,0:T(8,128)S(1)} %collective-permute-done.12.halo0_ref, ...), custom_call_target="tpu_custom_call" | custom-call | flops 2640000000 | bytes 2785296 | tf_op jit(solution)/shard_map/pallas_call | solution.py:139
  61.5 0.1 collective-permute-start.14
  61.6 1.6 %collective-permute-done.14.partner_ref = f32[2,2,4,8,640]{4,3,2,1,0:T(8,128)S(1)} collective-permute-done((f32[2,2,4,8,640]{4,3,2,1,0:T(8,128)S(1)}, f32[2,2,4,8,640]{4,3,2,1,0:T(8,128)S(1)}, u32[]{:S(2)}, u32[]{:S(2)}) %collective-permute-start.14) | collective-permute-done | bytes 327712 | tf_op jit(solution)/shard_map/ppermute | solution.py:456
  63.2 0.1 collective-permute-start.15
  63.4 1.0 shard_map.56
  64.4 0.1 collective-permute-start.16
  64.5 2.2 %collective-permute-start.17 = (f32[2,4,8,640]{3,2,1,0:T(8,128)S(1)}, f32[2,4,8,640]{3,2,1,0:T(8,128)S(1)}, u32[]{:S(2)}, u32[]{:S(2)}) collective-permute-start(f32[2,4,8,640]{3,2,1,0:T(8,128)S(1)} %get-tuple-element.128.side1_ref), channel_id=1, source_target_pairs={{2,4},{3,5},{4,2},{5,3},{10,12},{11,13},{12,10},{13,11},{18,20},{1... | collective-permute-start | bytes 491528 | tf_op jit(solution)/shard_map/ppermute | solution.py:468
  66.7 7.2 %shard_map.57 = (f32[2,24,8,640]{3,2,1,0:T(8,128)S(1)}, f32[2,2,3,2,8,640]{5,4,3,2,1,0:T(8,128)S(1)}) custom-call(f32[2,24,8,640]{3,2,1,0:T(8,128)S(1)} %get-tuple-element.124.own_ref, f32[2,24,8,640]{3,2,1,0:T(8,128)S(1)} %collective-permute-done.15.partner_ref, f32[2,4,8,640]{3,2,1,0:T(8,128)S(1)} %get-tuple-element.127.side0_ref, ...), custom_call_target="tpu_custom_call" | custom-call | flops 8800000000 | bytes 5079072 | tf_op jit(solution)/shard_map/pallas_call | solution.py:139
  73.9 0.0 collective-permute-done.16.halo0_ref
  73.9 2.2 %shard_map.58 = (f32[2,2,4,8,640]{4,3,2,1,0:T(8,128)S(1)}, s32[1,2,2]{2,1,0:T(2,128)S(1)}) custom-call(f32[2,4,8,640]{3,2,1,0:T(8,128)S(1)} %get-tuple-element.127.side0_ref, f32[2,4,8,640]{3,2,1,0:T(8,128)S(1)} %get-tuple-element.128.side1_ref, f32[2,4,8,640]{3,2,1,0:T(8,128)S(1)} %collective-permute-done.16.halo0_ref, ...), custom_call_target="tpu_custom_call" | custom-call | flops 2640000000 | bytes 2785296 | tf_op jit(solution)/shard_map/pallas_call | solution.py:139
  76.2 1.1 %shard_map.59 = (f32[2,4,8,640]{3,2,1,0:T(8,128)S(1)}, f32[2,4,8,640]{3,2,1,0:T(8,128)S(1)}) custom-call(f32[2,2,4,8,640]{4,3,2,1,0:T(8,128)S(1)} %get-tuple-element.131.own_ref.partner_ref, f32[2,2,4,8,640]{4,3,2,1,0:T(8,128)S(1)} %get-tuple-element.131.own_ref.partner_ref, s32[1,2,2]{2,1,0:T(2,128)S(1)} %get-tuple-element.132.offset_ref, f32[4]{0:T(128)S(1)} %copy-done.3, ...), custom_call_target="tpu_custom_call" | custom-call | flops 1210000000 | bytes 2293792 | tf_op jit(solution)/shard_map/pallas_call | solution.py:139
  77.3 0.6 collective-permute-start.21
  77.8 3.4 %collective-permute-start.22 = (f32[2,4,8,640]{3,2,1,0:T(8,128)S(1)}, f32[2,4,8,640]{3,2,1,0:T(8,128)S(1)}, u32[]{:S(2)}, u32[]{:S(2)}) collective-permute-start(f32[2,4,8,640]{3,2,1,0:T(8,128)S(1)} %get-tuple-element.134.side1_ref), channel_id=1, source_target_pairs={{2,4},{3,5},{4,2},{5,3},{10,12},{11,13},{12,10},{13,11},{18,20},{1... | collective-permute-start | bytes 491528 | tf_op jit(solution)/shard_map/ppermute | solution.py:468
  81.2 4.4 %shard_map.61 = (f32[12,8,512]{2,1,0:T(8,128)S(1)}, f32[12,8,512]{2,1,0:T(8,128)S(1)}, f32[2,1,3,2,8,640]{5,4,3,2,1,0:T(8,128)S(1)}) custom-call(f32[2,24,8,640]{3,2,1,0:T(8,128)S(1)} %get-tuple-element.129.own_ref.partner_ref, f32[2,24,8,640]{3,2,1,0:T(8,128)S(1)} %get-tuple-element.129.own_ref.partner_ref, ...), custom_call_target="tpu_custom_call" | custom-call | flops 4620000256 | bytes 4243488 | tf_op jit(solution)/shard_map/pallas_call | solution.py:139
  85.6 1.6 %collective-permute-start.20 = (f32[12,8,512]{2,1,0:T(8,128)S(1)}, f32[12,8,512]{2,1,0:T(8,128)S(1)}, u32[]{:S(2)}, u32[]{:S(2)}) collective-permute-start(f32[12,8,512]{2,1,0:T(8,128)S(1)} %get-tuple-element.138), channel_id=1, source_target_pairs={{0,17},{1,16},{2,19},{3,18},{4,21},{5,20},{6,23},{7,22},{8,25},{9,... | collective-permute-start | bytes 589832 | tf_op jit(solution)/shard_map/ppermute | solution.py:456
  87.2 4.4 %shard_map.60 = (f32[12,8,512]{2,1,0:T(8,128)S(1)}, f32[12,8,512]{2,1,0:T(8,128)S(1)}, f32[2,1,3,2,8,640]{5,4,3,2,1,0:T(8,128)S(1)}) custom-call(f32[2,24,8,640]{3,2,1,0:T(8,128)S(1)} %get-tuple-element.129.own_ref.partner_ref, f32[2,24,8,640]{3,2,1,0:T(8,128)S(1)} %get-tuple-element.129.own_ref.partner_ref, ...), custom_call_target="tpu_custom_call" | custom-call | flops 4620000256 | bytes 4243488 | tf_op jit(solution)/shard_map/pallas_call | solution.py:139
  91.6 0.6 collective-permute-start.19
  92.2 1.4 %collective-permute-start.18 = (f32[12,8,512]{2,1,0:T(8,128)S(1)}, f32[12,8,512]{2,1,0:T(8,128)S(1)}, u32[]{:S(2)}, u32[]{:S(2)}) collective-permute-start(f32[12,8,512]{2,1,0:T(8,128)S(1)} %get-tuple-element.136), channel_id=1, source_target_pairs={{0,1},{1,0},{2,3},{3,2},{4,5},{5,4},{6,7},{7,6},{8,9},{9,8},{10,11... | collective-permute-start | bytes 589832 | tf_op jit(solution)/shard_map/ppermute | solution.py:456
  93.7 0.0 collective-permute-done.22.halo1_ref
  93.7 2.4 %shard_map.62 = (f32[4,8,512]{2,1,0:T(8,128)S(1)}, f32[4,8,512]{2,1,0:T(8,128)S(1)}, f32[4,8,512]{2,1,0:T(8,128)S(1)}, f32[4,8,512]{2,1,0:T(8,128)S(1)}) custom-call(f32[2,4,8,640]{3,2,1,0:T(8,128)S(1)} %get-tuple-element.133.side0_ref, f32[2,4,8,640]{3,2,1,0:T(8,128)S(1)} %get-tuple-element.134.side1_ref, ...), custom_call_target="tpu_custom_call" | custom-call | flops 2750000128 | bytes 1409024 | tf_op jit(solution)/shard_map/pallas_call | solution.py:139
  96.1 0.7 collective-permute-start.23
  96.8 1.5 %collective-permute-start.24 = (f32[4,8,512]{2,1,0:T(8,128)S(1)}, f32[4,8,512]{2,1,0:T(8,128)S(1)}, u32[]{:S(2)}, u32[]{:S(2)}) collective-permute-start(f32[4,8,512]{2,1,0:T(8,128)S(1)} %get-tuple-element.145), channel_id=1, source_target_pairs={{0,16},{1,17},{2,18},{3,19},{4,20},{5,21},{6,22},{7,23},{8,24},{9,... | collective-permute-start | bytes 196616 | tf_op jit(solution)/shard_map/ppermute | solution.py:456
  98.3 1.4 %collective-permute-start.25 = (f32[4,8,512]{2,1,0:T(8,128)S(1)}, f32[4,8,512]{2,1,0:T(8,128)S(1)}, u32[]{:S(2)}, u32[]{:S(2)}) collective-permute-start(f32[4,8,512]{2,1,0:T(8,128)S(1)} %get-tuple-element.146), channel_id=1, source_target_pairs={{0,17},{1,16},{2,19},{3,18},{4,21},{5,20},{6,23},{7,22},{8,25},{9,... | collective-permute-start | bytes 196616 | tf_op jit(solution)/shard_map/ppermute | solution.py:456
  99.7 1.5 %collective-permute-done.23.refs_5_ = f32[4,8,512]{2,1,0:T(8,128)S(1)} collective-permute-done((f32[4,8,512]{2,1,0:T(8,128)S(1)}, f32[4,8,512]{2,1,0:T(8,128)S(1)}, u32[]{:S(2)}, u32[]{:S(2)}) %collective-permute-start.23) | collective-permute-done | bytes 65568 | tf_op jit(solution)/shard_map/ppermute | solution.py:456
  101.1 0.4 collective-permute-done.24.refs_6_
  101.5 1.9 %collective-permute-done.25.refs_7_ = f32[4,8,512]{2,1,0:T(8,128)S(1)} collective-permute-done((f32[4,8,512]{2,1,0:T(8,128)S(1)}, f32[4,8,512]{2,1,0:T(8,128)S(1)}, u32[]{:S(2)}, u32[]{:S(2)}) %collective-permute-start.25) | collective-permute-done | bytes 65568 | tf_op jit(solution)/shard_map/ppermute | solution.py:456
  103.4 1.1 %shard_map.63 = f32[16,8,2048]{2,1,0:T(8,128)} custom-call(f32[12,8,512]{2,1,0:T(8,128)S(1)} %get-tuple-element.135.refs_0_, f32[12,8,512]{2,1,0:T(8,128)S(1)} %collective-permute-done.18.refs_1_, f32[12,8,512]{2,1,0:T(8,128)S(1)} %collective-permute-done.19.refs_2_, f32[12,8,512]{2,1,0:T(8,128)S(1)} %collective-permute-done.20.refs_3_, ...), custom_call_target="tpu_custom_call" | custom-call | flops 1100000000 | bytes 2097152 | tf_op jit(solution)/shard_map/pallas_call | solution.py:139
  (15 shorter events, 0.1 us)
Async XLA Ops:
  0.0 5.1 %copy-start = (f32[1,4,4,16,2048]{4,3,2,1,0:T(8,128)S(1)}, f32[1,4,4,16,2048]{4,3,2,1,0:T(8,128)}, u32[]{:S(2)}) copy-start(f32[1,4,4,16,2048]{4,3,2,1,0:T(8,128)} %coeff_ref.3) | copy-start | bytes 6291460
  0.0 5.1 %copy-start.1 = (f32[1,16,8,2048]{3,2,1,0:T(8,128)S(1)}, f32[1,16,8,2048]{3,2,1,0:T(8,128)}, u32[]{:S(2)}) copy-start(f32[1,16,8,2048]{3,2,1,0:T(8,128)} %param.4) | copy-start | bytes 3145732
  0.0 5.1 %copy-start.2 = (s32[1,1,4]{2,1,0:T(1,128)S(1)}, s32[1,1,4]{2,1,0:T(1,128)}, u32[]{:S(2)}) copy-start(s32[1,1,4]{2,1,0:T(1,128)} %offset_ref.3) | copy-start | bytes 52
  0.0 5.2 %copy-start.3 = (f32[4]{0:T(128)S(1)}, f32[4]{0:T(128)}, u32[]{:S(2)}) copy-start(f32[4]{0:T(128)} %level_ref.15) | copy-start | bytes 52
  0.0 5.1 %collective-permute-start = (f32[16,8,2048]{2,1,0:T(8,128)}, f32[16,8,2048]{2,1,0:T(8,128)S(1)}, u32[]{:S(2)}, u32[]{:S(2)}) collective-permute-start(f32[16,8,2048]{2,1,0:T(8,128)} %bitcast.4), channel_id=1, source_target_pairs={{0,8},{1,9},{2,10},{3,11},{4,12},{5,13},{6,14},{7,15},{8,0},{9,1},... | collective-permute-start | bytes 3145736 | tf_op jit(solution)/shard_map/ppermute | solution.py:456
  1.6 7.2 %collective-permute-start.1 = (f32[4,16,640]{2,1,0:T(8,128)S(1)}, f32[4,16,640]{2,1,0:T(8,128)S(1)}, u32[]{:S(2)}, u32[]{:S(2)}) collective-permute-start(f32[4,16,640]{2,1,0:T(8,128)S(1)} %get-tuple-element.85), channel_id=1, source_target_pairs={{0,1},{1,0},{2,3},{3,2},{4,5},{5,4},{6,7},{7,6},{8,9},{9,8},{10,11... | collective-permute-start | bytes 491528 | tf_op jit(solution)/shard_map/ppermute | solution.py:456
  3.2 7.0 %collective-permute-start.2 = (f32[4,16,640]{2,1,0:T(8,128)S(1)}, f32[4,16,640]{2,1,0:T(8,128)S(1)}, u32[]{:S(2)}, u32[]{:S(2)}) collective-permute-start(f32[4,16,640]{2,1,0:T(8,128)S(1)} %get-tuple-element.86), channel_id=1, source_target_pairs={{0,16},{1,17},{2,18},{3,19},{4,20},{5,21},{6,22},{7,23},{8,24},{9,... | collective-permute-start | bytes 491528 | tf_op jit(solution)/shard_map/ppermute | solution.py:456
  4.7 8.3 %collective-permute-start.3 = (f32[4,16,640]{2,1,0:T(8,128)S(1)}, f32[4,16,640]{2,1,0:T(8,128)S(1)}, u32[]{:S(2)}, u32[]{:S(2)}) collective-permute-start(f32[4,16,640]{2,1,0:T(8,128)S(1)} %get-tuple-element.87), channel_id=1, source_target_pairs={{0,17},{1,16},{2,19},{3,18},{4,21},{5,20},{6,23},{7,22},{8,25},{9,... | collective-permute-start | bytes 491528 | tf_op jit(solution)/shard_map/ppermute | solution.py:456
  13.0 9.1 %collective-permute-start.4 = (f32[16,8,640]{2,1,0:T(8,128)S(1)}, f32[16,8,640]{2,1,0:T(8,128)S(1)}, u32[]{:S(2)}, u32[]{:S(2)}) collective-permute-start(f32[16,8,640]{2,1,0:T(8,128)S(1)} %get-tuple-element.90), channel_id=1, source_target_pairs={{0,1},{1,0},{2,3},{3,2},{4,5},{5,4},{6,7},{7,6},{8,9},{9,8},{10,11... | collective-permute-start | bytes 983048 | tf_op jit(solution)/shard_map/ppermute | solution.py:456
  14.5 8.8 %collective-permute-start.5 = (f32[16,8,640]{2,1,0:T(8,128)S(1)}, f32[16,8,640]{2,1,0:T(8,128)S(1)}, u32[]{:S(2)}, u32[]{:S(2)}) collective-permute-start(f32[16,8,640]{2,1,0:T(8,128)S(1)} %get-tuple-element.91), channel_id=1, source_target_pairs={{0,16},{1,17},{2,18},{3,19},{4,20},{5,21},{6,22},{7,23},{8,24},{9,... | collective-permute-start | bytes 983048 | tf_op jit(solution)/shard_map/ppermute | solution.py:456
  23.3 8.8 %collective-permute-start.6 = (f32[16,8,640]{2,1,0:T(8,128)S(1)}, f32[16,8,640]{2,1,0:T(8,128)S(1)}, u32[]{:S(2)}, u32[]{:S(2)}) collective-permute-start(f32[16,8,640]{2,1,0:T(8,128)S(1)} %get-tuple-element.94), channel_id=1, source_target_pairs={{0,17},{1,16},{2,19},{3,18},{4,21},{5,20},{6,23},{7,22},{8,25},{9,... | collective-permute-start | bytes 983048 | tf_op jit(solution)/shard_map/ppermute | solution.py:456
  32.2 11.7 %collective-permute-start.10 = (f32[2,4,8,640]{3,2,1,0:T(8,128)S(1)}, f32[2,4,8,640]{3,2,1,0:T(8,128)S(1)}, u32[]{:S(2)}, u32[]{:S(2)}) collective-permute-start(f32[2,4,8,640]{3,2,1,0:T(8,128)S(1)} %get-tuple-element.106.side0_ref), channel_id=1, source_target_pairs={{0,2},{1,3},{2,0},{3,1},{4,6},{5,7},{6,4},{7,5},{8,10},{9,11},{10,... | collective-permute-start | bytes 491528 | tf_op jit(solution)/shard_map/ppermute | solution.py:468
  32.7 11.2 %collective-permute-start.11 = (f32[2,4,8,640]{3,2,1,0:T(8,128)S(1)}, f32[2,4,8,640]{3,2,1,0:T(8,128)S(1)}, u32[]{:S(2)}, u32[]{:S(2)}) collective-permute-start(f32[2,4,8,640]{3,2,1,0:T(8,128)S(1)} %get-tuple-element.107.side1_ref), channel_id=1, source_target_pairs={{2,4},{3,5},{4,2},{5,3},{10,12},{11,13},{12,10},{13,11},{18,20},{1... | collective-permute-start | bytes 491528 | tf_op jit(solution)/shard_map/ppermute | solution.py:468
  37.3 12.1 %collective-permute-start.7 = (f32[2,4,16,640]{3,2,1,0:T(8,128)S(1)}, f32[2,4,16,640]{3,2,1,0:T(8,128)S(1)}, u32[]{:S(2)}, u32[]{:S(2)}) collective-permute-start(f32[2,4,16,640]{3,2,1,0:T(8,128)S(1)} %get-tuple-element.99), channel_id=1, source_target_pairs={{0,1},{1,0},{2,3},{3,2},{4,5},{5,4},{6,7},{7,6},{8,9},{9,8},{10,11... | collective-permute-start | bytes 983048 | tf_op jit(solution)/shard_map/ppermute | solution.py:456
  37.9 11.5 %collective-permute-start.8 = (f32[2,4,16,640]{3,2,1,0:T(8,128)S(1)}, f32[2,4,16,640]{3,2,1,0:T(8,128)S(1)}, u32[]{:S(2)}, u32[]{:S(2)}) collective-permute-start(f32[2,4,16,640]{3,2,1,0:T(8,128)S(1)} %get-tuple-element.100), channel_id=1, source_target_pairs={{0,16},{1,17},{2,18},{3,19},{4,20},{5,21},{6,22},{7,23},{8,24},{9,... | collective-permute-start | bytes 983048 | tf_op jit(solution)/shard_map/ppermute | solution.py:456
  39.4 12.6 %collective-permute-start.9 = (f32[2,4,16,640]{3,2,1,0:T(8,128)S(1)}, f32[2,4,16,640]{3,2,1,0:T(8,128)S(1)}, u32[]{:S(2)}, u32[]{:S(2)}) collective-permute-start(f32[2,4,16,640]{3,2,1,0:T(8,128)S(1)} %get-tuple-element.101), channel_id=1, source_target_pairs={{0,17},{1,16},{2,19},{3,18},{4,21},{5,20},{6,23},{7,22},{8,25},{9,... | collective-permute-start | bytes 983048 | tf_op jit(solution)/shard_map/ppermute | solution.py:456
  47.2 12.0 %collective-permute-start.12 = (f32[2,4,8,640]{3,2,1,0:T(8,128)S(1)}, f32[2,4,8,640]{3,2,1,0:T(8,128)S(1)}, u32[]{:S(2)}, u32[]{:S(2)}) collective-permute-start(f32[2,4,8,640]{3,2,1,0:T(8,128)S(1)} %get-tuple-element.115.side0_ref), channel_id=1, source_target_pairs={{0,2},{1,3},{2,0},{3,1},{4,6},{5,7},{6,4},{7,5},{8,10},{9,11},{10,... | collective-permute-start | bytes 491528 | tf_op jit(solution)/shard_map/ppermute | solution.py:468
  47.3 12.0 %collective-permute-start.13 = (f32[2,4,8,640]{3,2,1,0:T(8,128)S(1)}, f32[2,4,8,640]{3,2,1,0:T(8,128)S(1)}, u32[]{:S(2)}, u32[]{:S(2)}) collective-permute-start(f32[2,4,8,640]{3,2,1,0:T(8,128)S(1)} %get-tuple-element.116.side1_ref), channel_id=1, source_target_pairs={{2,4},{3,5},{4,2},{5,3},{10,12},{11,13},{12,10},{13,11},{18,20},{1... | collective-permute-start | bytes 491528 | tf_op jit(solution)/shard_map/ppermute | solution.py:468
  61.5 1.7 %collective-permute-start.14 = (f32[2,2,4,8,640]{4,3,2,1,0:T(8,128)S(1)}, f32[2,2,4,8,640]{4,3,2,1,0:T(8,128)S(1)}, u32[]{:S(2)}, u32[]{:S(2)}) collective-permute-start(f32[2,2,4,8,640]{4,3,2,1,0:T(8,128)S(1)} %get-tuple-element.123.own_ref), channel_id=1, source_target_pairs={{0,8},{1,9},{2,10},{3,11},{4,12},{5,13},{6,14},{7,15},{8,0},{9,1},... | collective-permute-start | bytes 983048 | tf_op jit(solution)/shard_map/ppermute | solution.py:456
  63.2 3.5 %collective-permute-start.15 = (f32[2,24,8,640]{3,2,1,0:T(8,128)S(1)}, f32[2,24,8,640]{3,2,1,0:T(8,128)S(1)}, u32[]{:S(2)}, u32[]{:S(2)}) collective-permute-start(f32[2,24,8,640]{3,2,1,0:T(8,128)S(1)} %get-tuple-element.124.own_ref), channel_id=1, source_target_pairs={{0,8},{1,9},{2,10},{3,11},{4,12},{5,13},{6,14},{7,15},{8,0},{9,1},... | collective-permute-start | bytes 2949128 | tf_op jit(solution)/shard_map/ppermute | solution.py:456
  64.4 9.5 %collective-permute-start.16 = (f32[2,4,8,640]{3,2,1,0:T(8,128)S(1)}, f32[2,4,8,640]{3,2,1,0:T(8,128)S(1)}, u32[]{:S(2)}, u32[]{:S(2)}) collective-permute-start(f32[2,4,8,640]{3,2,1,0:T(8,128)S(1)} %get-tuple-element.127.side0_ref), channel_id=1, source_target_pairs={{0,2},{1,3},{2,0},{3,1},{4,6},{5,7},{6,4},{7,5},{8,10},{9,11},{10,... | collective-permute-start | bytes 491528 | tf_op jit(solution)/shard_map/ppermute | solution.py:468
  64.5 9.5 %collective-permute-start.17 = (f32[2,4,8,640]{3,2,1,0:T(8,128)S(1)}, f32[2,4,8,640]{3,2,1,0:T(8,128)S(1)}, u32[]{:S(2)}, u32[]{:S(2)}) collective-permute-start(f32[2,4,8,640]{3,2,1,0:T(8,128)S(1)} %get-tuple-element.128.side1_ref), channel_id=1, source_target_pairs={{2,4},{3,5},{4,2},{5,3},{10,12},{11,13},{12,10},{13,11},{18,20},{1... | collective-permute-start | bytes 491528 | tf_op jit(solution)/shard_map/ppermute | solution.py:468
  77.3 16.4 %collective-permute-start.21 = (f32[2,4,8,640]{3,2,1,0:T(8,128)S(1)}, f32[2,4,8,640]{3,2,1,0:T(8,128)S(1)}, u32[]{:S(2)}, u32[]{:S(2)}) collective-permute-start(f32[2,4,8,640]{3,2,1,0:T(8,128)S(1)} %get-tuple-element.133.side0_ref), channel_id=1, source_target_pairs={{0,2},{1,3},{2,0},{3,1},{4,6},{5,7},{6,4},{7,5},{8,10},{9,11},{10,... | collective-permute-start | bytes 491528 | tf_op jit(solution)/shard_map/ppermute | solution.py:468
  77.8 15.8 %collective-permute-start.22 = (f32[2,4,8,640]{3,2,1,0:T(8,128)S(1)}, f32[2,4,8,640]{3,2,1,0:T(8,128)S(1)}, u32[]{:S(2)}, u32[]{:S(2)}) collective-permute-start(f32[2,4,8,640]{3,2,1,0:T(8,128)S(1)} %get-tuple-element.134.side1_ref), channel_id=1, source_target_pairs={{2,4},{3,5},{4,2},{5,3},{10,12},{11,13},{12,10},{13,11},{18,20},{1... | collective-permute-start | bytes 491528 | tf_op jit(solution)/shard_map/ppermute | solution.py:468
  85.6 8.0 %collective-permute-start.20 = (f32[12,8,512]{2,1,0:T(8,128)S(1)}, f32[12,8,512]{2,1,0:T(8,128)S(1)}, u32[]{:S(2)}, u32[]{:S(2)}) collective-permute-start(f32[12,8,512]{2,1,0:T(8,128)S(1)} %get-tuple-element.138), channel_id=1, source_target_pairs={{0,17},{1,16},{2,19},{3,18},{4,21},{5,20},{6,23},{7,22},{8,25},{9,... | collective-permute-start | bytes 589832 | tf_op jit(solution)/shard_map/ppermute | solution.py:456
  91.6 8.0 %collective-permute-start.19 = (f32[12,8,512]{2,1,0:T(8,128)S(1)}, f32[12,8,512]{2,1,0:T(8,128)S(1)}, u32[]{:S(2)}, u32[]{:S(2)}) collective-permute-start(f32[12,8,512]{2,1,0:T(8,128)S(1)} %get-tuple-element.137), channel_id=1, source_target_pairs={{0,16},{1,17},{2,18},{3,19},{4,20},{5,21},{6,22},{7,23},{8,24},{9,... | collective-permute-start | bytes 589832 | tf_op jit(solution)/shard_map/ppermute | solution.py:456
  92.2 7.4 %collective-permute-start.18 = (f32[12,8,512]{2,1,0:T(8,128)S(1)}, f32[12,8,512]{2,1,0:T(8,128)S(1)}, u32[]{:S(2)}, u32[]{:S(2)}) collective-permute-start(f32[12,8,512]{2,1,0:T(8,128)S(1)} %get-tuple-element.136), channel_id=1, source_target_pairs={{0,1},{1,0},{2,3},{3,2},{4,5},{5,4},{6,7},{7,6},{8,9},{9,8},{10,11... | collective-permute-start | bytes 589832 | tf_op jit(solution)/shard_map/ppermute | solution.py:456
  96.1 5.0 %collective-permute-start.23 = (f32[4,8,512]{2,1,0:T(8,128)S(1)}, f32[4,8,512]{2,1,0:T(8,128)S(1)}, u32[]{:S(2)}, u32[]{:S(2)}) collective-permute-start(f32[4,8,512]{2,1,0:T(8,128)S(1)} %get-tuple-element.144), channel_id=1, source_target_pairs={{0,1},{1,0},{2,3},{3,2},{4,5},{5,4},{6,7},{7,6},{8,9},{9,8},{10,11... | collective-permute-start | bytes 196616 | tf_op jit(solution)/shard_map/ppermute | solution.py:456
  96.8 4.7 %collective-permute-start.24 = (f32[4,8,512]{2,1,0:T(8,128)S(1)}, f32[4,8,512]{2,1,0:T(8,128)S(1)}, u32[]{:S(2)}, u32[]{:S(2)}) collective-permute-start(f32[4,8,512]{2,1,0:T(8,128)S(1)} %get-tuple-element.145), channel_id=1, source_target_pairs={{0,16},{1,17},{2,18},{3,19},{4,20},{5,21},{6,22},{7,23},{8,24},{9,... | collective-permute-start | bytes 196616 | tf_op jit(solution)/shard_map/ppermute | solution.py:456
  98.3 5.2 %collective-permute-start.25 = (f32[4,8,512]{2,1,0:T(8,128)S(1)}, f32[4,8,512]{2,1,0:T(8,128)S(1)}, u32[]{:S(2)}, u32[]{:S(2)}) collective-permute-start(f32[4,8,512]{2,1,0:T(8,128)S(1)} %get-tuple-element.146), channel_id=1, source_target_pairs={{0,17},{1,16},{2,19},{3,18},{4,21},{5,20},{6,23},{7,22},{8,25},{9,... | collective-permute-start | bytes 196616 | tf_op jit(solution)/shard_map/ppermute | solution.py:456
